TPU v7x, 32 devices: a whole 2x2x4 slice. The times are simulated.
32 devices in a mesh: seq: 32 (over z, y, x, core).
Axes of the slice: x: 2, y: 2, z: 4, core: 2. Of those that a mesh axis runs over, the one named last changes fastest.
Arguments:
- rhs: float32 [4096, 2048], P('seq'), may hold values from -17 to 17
- rate: float32 [16, 2048], replicated, may hold values from 9.765625e-05 to 0.0333333333, as said below
- delta: float32 [4096, 2048], P('seq'), may hold values from 0.25 to 2048, as said below
- b_proj: float32 [4096, 16], P('seq'), may hold values from -1 to 3
- c_proj: float32 [4096, 16], P('seq'), may hold values from -0.21 to 0.33
- skip: float32 [2048], replicated, may hold values from 0.5 to 1.5
- curvature: float32 [4096, 2048], P('seq'), may hold values from 0.3 to 3
- damping: float32 [2048], replicated, may hold values from 0.1 to 1
Outputs:
- solution: float32 [4096, 2048], P('seq')
- residual: float32 [4096, 2048], P('seq')
Inputs may be any that keep to these rules, and one draw needn't show every extreme that they name: `rate`: all entries positive. `delta`: all entries positive.
All inputs are finite; a program needn't handle non-finite values.
Results may differ from a plain program's by a relative error of at most 0.0003.
Values sent between devices are 32-bit elements; how exact they have to be, the bound alone decides.
No kernel may reach another device: no remote copies, remote signals or barrier semaphores. Data moves between devices by JAX's collectives and lax.ppermute only.
A program may use at most 192 MiB of HBM per device.

v0:
```python
import jax
import jax.numpy as jnp
from jax import lax
from jax.sharding import PartitionSpec as P

CG_ITERS = 2


def entering_2(value, axis, join, neutral, backward):
    count, mine = (lax.axis_size(axis), lax.axis_index(axis))
    pieces = jax.tree.map(lambda part: lax.all_gather(part, axis), value)
    if backward:
        pieces = jax.tree.map(lambda part: part[::-1], pieces)
        mine = count - 1 - mine
    total = jax.tree.map(
        lambda part, zero: jnp.full_like(part, 0) + jnp.asarray(zero, part.dtype), value, neutral
    )

    def lap(position, total):
        longer = join(total, jax.tree.map(lambda part: part[position], pieces))
        return jax.tree.map(lambda new, old: jnp.where(position < mine, new, old), longer, total)

    return lax.fori_loop(0, count - 1, lap, total)


def link_combine(earlier, later):
    return (earlier[0] * later[0], later[0] * earlier[1] + later[1])


def prepare(rate, delta, b_proj, c_proj):
    tokens_here, columns = delta.shape
    entries = rate.shape[0]
    length = 8
    groups = tokens_here // length
    delta_blocks = delta.reshape(groups, length, columns)
    b_blocks = b_proj.reshape(groups, length, entries)
    c_blocks = c_proj.reshape(groups, length, entries)
    within = jnp.cumsum(delta_blocks, axis=1)
    group_total = within[:, -1]
    group_decay = jnp.exp(-group_total[:, None, :] * rate[None])
    running_total = jnp.cumsum(group_total, axis=0)
    device_total = running_total[-1]
    before_total = running_total - group_total
    after_total = device_total[None, :] - running_total
    span_decay = jnp.exp(-device_total[None, :] * rate)
    return (
        rate,
        delta_blocks,
        b_blocks,
        c_blocks,
        within,
        group_total,
        group_decay,
        before_total,
        after_total,
        device_total,
        span_decay,
    )


def forward_local(vector, prepared, skip, linker):
    (
        rate,
        delta_blocks,
        b_blocks,
        c_blocks,
        within,
        group_total,
        group_decay,
        before_total,
        after_total,
        device_total,
        span_decay,
    ) = prepared
    groups, length, columns = delta_blocks.shape
    tangent = vector.reshape(groups, length, columns)
    state = jnp.zeros(group_decay.shape, jnp.float32)
    pieces = []
    for position in range(length):
        exponent = delta_blocks[:, position][:, None, :] * rate[None]
        drive = b_blocks[:, position][:, :, None] * tangent[:, position][:, None, :]
        state = jnp.exp(-exponent) * state - jnp.expm1(-exponent) * drive
        pieces.append(jnp.sum(c_blocks[:, position][:, :, None] * state, axis=1))

    def forward_link_groups(entering, inputs):
        decay_here, state_here = inputs
        return (decay_here * entering + state_here, entering)

    start_state = jnp.zeros(rate.shape, jnp.float32)
    span_state, entering = lax.scan(forward_link_groups, start_state, (group_decay, state))
    arrival = linker(span_decay, span_state, device_total)
    carried = entering + jnp.exp(-before_total[:, None, :] * rate[None]) * arrival[None]
    for position in range(length):
        running = jnp.exp(-within[:, position][:, None, :] * rate[None])
        pieces[position] = pieces[position] + jnp.sum(
            c_blocks[:, position][:, :, None] * (running * carried), axis=1
        )
    output = jnp.stack(pieces, axis=1).reshape(groups * length, columns)
    return output + skip[None, :] * vector


def reverse_local(weights, prepared, skip, linker):
    (
        rate,
        delta_blocks,
        b_blocks,
        c_blocks,
        within,
        group_total,
        group_decay,
        before_total,
        after_total,
        device_total,
        span_decay,
    ) = prepared
    groups, length, columns = delta_blocks.shape
    weight_blocks = weights.reshape(groups, length, columns)
    passed = jnp.zeros(group_decay.shape, jnp.float32)
    pieces = [None] * length
    for position in reversed(range(length)):
        exponent = delta_blocks[:, position][:, None, :] * rate[None]
        costate = (
            c_blocks[:, position][:, :, None] * weight_blocks[:, position][:, None, :] + passed
        )
        gained = -jnp.expm1(-exponent) * costate
        pieces[position] = jnp.sum(b_blocks[:, position][:, :, None] * gained, axis=1)
        passed = jnp.exp(-exponent) * costate

    def reverse_link_groups(incoming, inputs):
        decay_here, passed_here = inputs
        return (decay_here * incoming + passed_here, incoming)

    start_state = jnp.zeros(rate.shape, jnp.float32)
    span_state, incoming = lax.scan(
        reverse_link_groups, start_state, (group_decay, passed), reverse=True
    )
    arrival = linker(span_decay, span_state, device_total)
    carried = incoming + jnp.exp(-after_total[:, None, :] * rate[None]) * arrival[None]
    for position in range(length):
        exponent = delta_blocks[:, position][:, None, :] * rate[None]
        running = jnp.exp(-(group_total - within[:, position])[:, None, :] * rate[None])
        gained = -jnp.expm1(-exponent) * (running * carried)
        pieces[position] = pieces[position] + jnp.sum(
            b_blocks[:, position][:, :, None] * gained, axis=1
        )
    output = jnp.stack(pieces, axis=1).reshape(groups * length, columns)
    return output + skip[None, :] * weights


def paired(residual, curved):
    return lax.psum((jnp.sum(residual * residual), jnp.sum(residual * curved)), "seq")


def solver_run(rhs, damped_product):
    solution = jnp.zeros_like(rhs)
    residual = rhs
    curved = damped_product(residual)
    norm_now, inner = paired(residual, curved)
    step_size = norm_now / inner
    direction, along = (residual, curved)
    for iteration in range(CG_ITERS):
        solution = solution + step_size * direction
        residual = residual - step_size * along
        if iteration + 1 < CG_ITERS:
            curved = damped_product(residual)
            norm_next, inner = paired(residual, curved)
            ratio = norm_next / norm_now
            step_size = norm_next / (inner - ratio * norm_next / step_size)
            direction = residual + ratio * direction
            along = curved + ratio * along
            norm_now = norm_next
    return (solution, residual)


def per_device(rhs, rate, delta, b_proj, c_proj, skip, curvature, damping):
    prepared = prepare(rate, delta, b_proj, c_proj)

    def summarize(span_decay, span_state):
        summary = (span_decay, span_state)
        neutral = (jnp.ones_like(span_decay), jnp.zeros_like(span_state))
        return (summary, neutral, link_combine)

    def carry_forward(span_decay, span_state, span_total):
        summary, neutral, combine = summarize(span_decay, span_state)
        return entering_2(summary, "seq", combine, neutral, False)[1]

    def carry_backward(span_decay, span_state, span_total):
        summary, neutral, combine = summarize(span_decay, span_state)
        return entering_2(summary, "seq", combine, neutral, True)[1]

    def damped_product(vector):
        forward = forward_local(vector, prepared, skip, carry_forward)
        return (
            reverse_local(curvature * forward, prepared, skip, carry_backward)
            + damping[None, :] * vector
        )

    return solver_run(rhs, damped_product)


def solution(mesh):
    placed = (
        P("seq", None),
        P(),
        P("seq", None),
        P("seq", None),
        P("seq", None),
        P(),
        P("seq", None),
        P(),
    )
    return jax.shard_map(
        per_device,
        mesh=mesh,
        in_specs=placed,
        out_specs=(P("seq", None), P("seq", None)),
        check_vma=False,
    )
```

profile of v0, /device:TPU:0, one launch (start us, length us, event | category | flops | bytes accessed | tf_op | source)
XLA Modules:
  0.0 849.8 jit_solution(9692354284152529560)
XLA Ops:
  7.2 6.6 fusion.51
  24.0 9.3 %multiply_subtract_fusion.8 = f32[16,16,2048]{2,1,0:T(8,128)} fusion(f32[16,2048]{1,0:T(8,128)S(1)} %get-tuple-element.1022, f32[16,16]{1,0:T(8,128)S(1)} %bitcast.486, f32[16,2048]{1,0:T(8,128)S(1)} %get-tuple-element.1036, f32[16,2048]{1,0:T(8,128)S(1)} %copy-done.14, f32[16,2048]{1,0:T(8,128)S(1)} %get-tuple-element.1023, f32[16,16]{1,0:T(8,128)S(1)} %bitcast.494, ...), kind=kLoop, calls=%fused_computation.135 | loop fusion | flops 25165824 | bytes 4333568 | tf_op jit(solution)/shard_map/sub | solution.py:82
  34.9 26.6 %while.116 = (s32[]{:T(128)}, f32[16,2048]{1,0:T(8,128)S(1)}, f32[16,16,2048]{2,1,0:T(8,128)}, f32[16,16,2048]{2,1,0:T(8,128)S(1)}, f32[16,16,2048]{2,1,0:T(8,128)}, /*index=5*/s32[]{:T(128)}, s32[]{:T(128)}) while((s32[]{:T(128)}, f32[16,2048]{1,0:T(8,128)S(1)}, f32[16,16,2048]{2,1,0:T(8,128)}, f32[16,16,2048]{2,1,0:T(8,128)S(1)}, ...), condition=%wide.region_5.6_spmd.clone, body=%wide.region_4.5_spmd.clone.sunk | while | flops 131075 | bytes 787036 | solution.py:90
  66.1 8.0 multiply_reduce_fusion.53
  74.3 6.5 multiply_reduce_fusion.51
  80.9 7.4 multiply_reduce_fusion.49
  88.3 38.5 %all-gather.13.cloned.1.call-done = f32[512,2048]{1,0:T(8,128)} async-done(((f32[16,2048]{1,0:T(8,128)}), f32[512,2048]{1,0:T(8,128)}) %all-gather.13.cloned.1.call-update) | async-done | bytes 4194320 | tf_op jit(solution)/shard_map/all_gather | solution.py:11
  126.8 64.0 %all-gather.11.cloned.1.call-done = f32[512,2048]{1,0:T(8,128)} async-done(((f32[16,2048]{1,0:T(8,128)}), f32[512,2048]{1,0:T(8,128)}) %all-gather.11.cloned.1.call-update) | async-done | bytes 4194320 | tf_op jit(solution)/shard_map/all_gather | solution.py:11
  190.8 33.8 %while.117 = (s32[]{:T(128)}, f32[16,2048]{1,0:T(8,128)S(1)}, s32[]{:T(128)}, f32[32,16,2048]{2,1,0:T(8,128)}, f32[32,16,2048]{2,1,0:T(8,128)}, /*index=5*/s32[]{:T(128)}, s32[]{:T(128)}) while((s32[]{:T(128)}, f32[16,2048]{1,0:T(8,128)S(1)}, s32[]{:T(128)}, f32[32,16,2048]{2,1,0:T(8,128)}, f32[32,16,2048]{2,1,0:T(8,128)}, ...), condition=%wide.region_8.9_spmd.clone, body=%wide.region_7.8_spmd.clone.sunk | while | flops 131076 | bytes 524389 | solution.py:23
  224.7 16.9 %multiply_reduce_fusion.46 = (f32[16,2048]{1,0:T(8,128)S(1)}, f32[16,2048]{1,0:T(8,128)S(1)}, f32[16,2048]{1,0:T(8,128)S(1)}, f32[16,2048]{1,0:T(8,128)S(1)}, f3...) fusion(f32[16,16]{1,0:T(8,128)} %bitcast.554, ...), kind=kLoop, calls=%fused_computation.112 | loop fusion | flops 42205184 | bytes 6568960 | tf_op jit(solution)/shard_map/reduce_sum | solution.py:95
  246.3 3.9 multiply_reduce_fusion.59
  257.2 5.6 fusion.35
  264.3 27.6 %while.118 = (s32[]{:T(128)}, f32[16,2048]{1,0:T(8,128)S(1)}, f32[16,16,2048]{2,1,0:T(8,128)}, f32[16,16,2048]{2,1,0:T(8,128)}, f32[16,16,2048]{2,1,0:T(8,128)}, /*index=5*/s32[]{:T(128)}, s32[]{:T(128)}, s32[]{:T(128)}) while((s32[]{:T(128)}, f32[16,2048]{1,0:T(8,128)S(1)}, f32[16,16,2048]{2,1,0:T(8,128)}, ...), condition=%wide.region_26.27_spmd.clone, body=%wide.region_25.26_spmd.clone.sunk | while | flops 131076 | bytes 786548 | solution.py:134
  293.3 4.8 rev.10
  298.2 5.4 multiply_reduce_fusion.41
  303.8 6.0 multiply_reduce_fusion.37
  309.9 5.4 multiply_reduce_fusion.43
  315.3 5.6 multiply_reduce_fusion.45
  320.9 32.4 %all-gather.15.cloned.1.call-done = f32[512,2048]{1,0:T(8,128)} async-done(((f32[16,2048]{1,0:T(8,128)}), f32[512,2048]{1,0:T(8,128)}) %all-gather.15.cloned.1.call-update) | async-done | bytes 4194320 | tf_op jit(solution)/shard_map/all_gather | solution.py:11
  353.2 4.7 rev.11
  357.9 33.9 %while.119 = (s32[]{:T(128)}, f32[16,2048]{1,0:T(8,128)S(1)}, s32[]{:T(128)}, f32[32,16,2048]{2,1,0:T(8,128)}, f32[32,16,2048]{2,1,0:T(8,128)}, /*index=5*/s32[]{:T(128)}, s32[]{:T(128)}) while((s32[]{:T(128)}, f32[16,2048]{1,0:T(8,128)S(1)}, s32[]{:T(128)}, f32[32,16,2048]{2,1,0:T(8,128)}, f32[32,16,2048]{2,1,0:T(8,128)}, ...), condition=%wide.region_28.29_spmd.clone, body=%wide.region_27.28_spmd.clone.sunk | while | flops 131076 | bytes 524389 | solution.py:23
  392.0 8.6 %fusion.6 = (f32[16,2048]{1,0:T(8,128)S(1)}, f32[16,2048]{1,0:T(8,128)S(1)}, f32[16,2048]{1,0:T(8,128)S(1)}, f32[16,2048]{1,0:T(8,128)S(1)}, f32[16,2048]{1,0:T(8,128)S(1)}) fusion(f32[16,2048]{1,0:T(8,128)} %bitcast.328, f32[16,16]{1,0:T(8,128)} %bitcast.556, f32[16,16]{1,0:T(8,128)} %bitcast.482, f32[16,2048]{1,0:T(8,128)} %copy-done.172, ...), kind=kLoop, calls=%fused_computation.30 | loop fusion | flops 20807680 | bytes 4331520 | tf_op jit(solution)/shard_map/reduce_sum | solution.py:126
  400.7 8.5 multiply_reduce_fusion.31
  415.3 3.9 stack.9
  422.5 39.4 %all-reduce.1 = (f32[]{:T(128)}, f32[]{:T(128)}) all-reduce(f32[]{:T(128)} %get-tuple-element.839, f32[]{:T(128)} %get-tuple-element.838), channel_id=1, replica_groups=mesh['seq'=32] {'seq'}, use_global_device_ids=true, to_apply=%region_1.2 | all-reduce | flops 2 | bytes 16 | tf_op jit(solution)/shard_map/psum | solution.py:151
  466.1 9.3 %multiply_subtract_fusion = f32[16,16,2048]{2,1,0:T(8,128)} fusion(f32[16,2048]{1,0:T(8,128)S(1)} %bitcast.335, f32[16,16]{1,0:T(8,128)S(1)} %bitcast.488, f32[16,2048]{1,0:T(8,128)S(1)} %copy-done.176, f32[16,2048]{1,0:T(8,128)S(1)} %copy-done.17, f32[16,2048]{1,0:T(8,128)S(1)} %bitcast.343, f32[16,16]{1,0:T(8,128)S(1)} %bitcast.496, ...), kind=kLoop, calls=%fused_computation.72 | loop fusion | flops 25165824 | bytes 4333568 | tf_op jit(solution)/shard_map/sub | solution.py:82
  477.0 27.6 %while.120 = (s32[]{:T(128)}, f32[16,2048]{1,0:T(8,128)S(1)}, f32[16,16,2048]{2,1,0:T(8,128)}, f32[16,16,2048]{2,1,0:T(8,128)}, f32[16,16,2048]{2,1,0:T(8,128)}, /*index=5*/s32[]{:T(128)}, s32[]{:T(128)}) while((s32[]{:T(128)}, f32[16,2048]{1,0:T(8,128)S(1)}, f32[16,16,2048]{2,1,0:T(8,128)}, f32[16,16,2048]{2,1,0:T(8,128)}, ...), condition=%wide.region_50.51_spmd.clone, body=%wide.region_49.50_spmd.clone.sunk | while | flops 131075 | bytes 787036 | solution.py:90
  505.6 9.0 %multiply_reduce_fusion.22 = (f32[16,2048]{1,0:T(8,128)}, f32[16,2048]{1,0:T(8,128)}, f32[16,2048]{1,0:T(8,128)}) fusion(f32[16,16]{1,0:T(8,128)} %bitcast.585, f32[16,2048]{1,0:T(8,128)} %bitcast.357, f32[16,16]{1,0:T(8,128)} %bitcast.513, f32[16,2048]{1,0:T(8,128)} %bitcast.362, f32[16,16]{1,0:T(8,128)} %bitcast.526, f32[16,2048]{1,0:T(8,128)} %bitcast.367, ...), kind=kLoop, calls=%fused_computation.63 | loop fusion | flops 18776064 | bytes 1843200 | tf_op jit(solution)/shard_map/reduce_sum | solution.py:83
  514.8 7.1 multiply_reduce_fusion.20
  521.9 8.1 multiply_reduce_fusion.18
  530.0 37.4 %all-gather.17.cloned.1.call-done = f32[512,2048]{1,0:T(8,128)} async-done(((f32[16,2048]{1,0:T(8,128)}), f32[512,2048]{1,0:T(8,128)}) %all-gather.17.cloned.1.call-update) | async-done | bytes 4194320 | tf_op jit(solution)/shard_map/all_gather | solution.py:11
  567.5 33.8 %while.121 = (s32[]{:T(128)}, f32[16,2048]{1,0:T(8,128)S(1)}, s32[]{:T(128)}, f32[32,16,2048]{2,1,0:T(8,128)}, f32[32,16,2048]{2,1,0:T(8,128)}, /*index=5*/s32[]{:T(128)}, s32[]{:T(128)}) while((s32[]{:T(128)}, f32[16,2048]{1,0:T(8,128)S(1)}, s32[]{:T(128)}, f32[32,16,2048]{2,1,0:T(8,128)}, f32[32,16,2048]{2,1,0:T(8,128)}, ...), condition=%wide.region_52.53_spmd.clone, body=%wide.region_51.52_spmd.clone.sunk | while | flops 131076 | bytes 524389 | solution.py:23
  601.4 17.0 %multiply_reduce_fusion.15 = (f32[16,2048]{1,0:T(8,128)S(1)}, f32[16,2048]{1,0:T(8,128)S(1)}, f32[16,2048]{1,0:T(8,128)S(1)}, f32[16,2048]{1,0:T(8,128)S(1)}, f3...) fusion(f32[16,16]{1,0:T(8,128)} %bitcast.557, ...), kind=kLoop, calls=%fused_computation.56 | loop fusion | flops 42205184 | bytes 6568960 | tf_op jit(solution)/shard_map/reduce_sum | solution.py:95
  618.6 4.0 multiply_reduce_fusion.28
  634.3 5.7 fusion.34
  641.6 27.6 %while.122 = (s32[]{:T(128)}, f32[16,2048]{1,0:T(8,128)S(1)}, f32[16,16,2048]{2,1,0:T(8,128)}, f32[16,16,2048]{2,1,0:T(8,128)}, f32[16,16,2048]{2,1,0:T(8,128)}, /*index=5*/s32[]{:T(128)}, s32[]{:T(128)}, s32[]{:T(128)}) while((s32[]{:T(128)}, f32[16,2048]{1,0:T(8,128)S(1)}, f32[16,16,2048]{2,1,0:T(8,128)}, ...), condition=%wide.region_70.71_spmd.clone, body=%wide.region_69.70_spmd.clone.sunk | while | flops 131076 | bytes 786548 | solution.py:134
  670.0 4.7 fusion.9
  674.9 4.3 multiply_reduce_fusion.10
  679.3 6.4 multiply_reduce_fusion.6
  685.7 5.4 multiply_reduce_fusion.12
  691.2 5.7 multiply_reduce_fusion.14
  696.9 33.6 %all-gather.19.cloned.1.call-done = f32[512,2048]{1,0:T(8,128)} async-done(((f32[16,2048]{1,0:T(8,128)}), f32[512,2048]{1,0:T(8,128)}) %all-gather.19.cloned.1.call-update) | async-done | bytes 4194320 | tf_op jit(solution)/shard_map/all_gather | solution.py:11
  730.5 4.8 rev.12
  735.3 33.8 %while.123 = (s32[]{:T(128)}, f32[16,2048]{1,0:T(8,128)S(1)}, s32[]{:T(128)}, f32[32,16,2048]{2,1,0:T(8,128)}, f32[32,16,2048]{2,1,0:T(8,128)}, /*index=5*/s32[]{:T(128)}, s32[]{:T(128)}) while((s32[]{:T(128)}, f32[16,2048]{1,0:T(8,128)S(1)}, s32[]{:T(128)}, f32[32,16,2048]{2,1,0:T(8,128)}, f32[32,16,2048]{2,1,0:T(8,128)}, ...), condition=%wide.region_72.73_spmd.clone, body=%wide.region_71.72_spmd.clone.sunk | while | flops 131076 | bytes 524389 | solution.py:23
  769.2 9.9 %multiply_reduce_fusion = (f32[16,2048]{1,0:T(8,128)S(1)}, f32[16,2048]{1,0:T(8,128)S(1)}, f32[16,2048]{1,0:T(8,128)S(1)}, f32[16,2048]{1,0:T(8,128)S(1)}, f32[16,2048]{1,0:T(8,128)S(1)}) fusion(f32[16,2048]{1,0:T(8,128)} %get-tuple-element.964, f32[16,16]{1,0:T(8,128)} %bitcast.485, f32[16,2048]{1,0:T(8,128)} %copy-done.172, f32[16,2048]{1,0:T(8,128)S(1)} %copy-done.20, ...), kind=kLoop, calls=%fused_computation.34 | loop fusion | flops 22380544 | bytes 4461568 | tf_op jit(solution)/shard_map/reduce_sum | solution.py:143
  779.3 4.9 multiply_reduce_fusion.9
  794.9 39.3 %all-reduce = (f32[]{:T(128)}, f32[]{:T(128)}) all-reduce(f32[]{:T(128)} %get-tuple-element.837, f32[]{:T(128)} %get-tuple-element.836), channel_id=1, replica_groups=mesh['seq'=32] {'seq'}, use_global_device_ids=true, to_apply=%region_47.48 | all-reduce | flops 2 | bytes 16 | tf_op jit(solution)/shard_map/psum | solution.py:151
  838.8 4.0 multiply_subtract_fusion.16
  (982 shorter events, 309.3 us)
Async XLA Ops:
  7.2 119.6 %all-gather.13.cloned.1.call-start = ((), (), s32[]{:S(2)}) async-start(), calls=%async_computation.1 | async-start | bytes 4325376 | tf_op jit(solution)/shard_map/all_gather | solution.py:11
  23.0 10.3 %copy-start.179 = (f32[16,2048]{1,0:T(8,128)}, f32[16,2048]{1,0:T(8,128)S(1)}, u32[]{:S(2)}) copy-start(f32[16,2048]{1,0:T(8,128)S(1)} %get-tuple-element.1028) | copy-start | bytes 393220
  23.0 10.3 %copy-start.182 = (f32[16,2048]{1,0:T(8,128)}, f32[16,2048]{1,0:T(8,128)S(1)}, u32[]{:S(2)}) copy-start(f32[16,2048]{1,0:T(8,128)S(1)} %get-tuple-element.1029) | copy-start | bytes 393220
  23.2 10.1 %copy-start.185 = (f32[16,2048]{1,0:T(8,128)}, f32[16,2048]{1,0:T(8,128)S(1)}, u32[]{:S(2)}) copy-start(f32[16,2048]{1,0:T(8,128)S(1)} %get-tuple-element.1024) | copy-start | bytes 393220
  23.2 10.1 %copy-start.187 = (f32[16,2048]{1,0:T(8,128)}, f32[16,2048]{1,0:T(8,128)S(1)}, u32[]{:S(2)}) copy-start(f32[16,2048]{1,0:T(8,128)S(1)} %get-tuple-element.1025) | copy-start | bytes 393220
  23.3 10.0 %copy-start.189 = (f32[16,2048]{1,0:T(8,128)}, f32[16,2048]{1,0:T(8,128)S(1)}, u32[]{:S(2)}) copy-start(f32[16,2048]{1,0:T(8,128)S(1)} %get-tuple-element.1026) | copy-start | bytes 393220
  23.3 10.0 %copy-start.191 = (f32[16,2048]{1,0:T(8,128)}, f32[16,2048]{1,0:T(8,128)S(1)}, u32[]{:S(2)}) copy-start(f32[16,2048]{1,0:T(8,128)S(1)} %get-tuple-element.1027) | copy-start | bytes 393220
  62.2 128.6 %all-gather.11.cloned.1.call-start = ((), (), s32[]{:S(2)}) async-start(), calls=%async_computation | async-start | bytes 4325376 | tf_op jit(solution)/shard_map/all_gather | solution.py:11
  63.9 289.4 %all-gather.15.cloned.1.call-start = ((), (), s32[]{:S(2)}) async-start(), calls=%async_computation.2 | async-start | bytes 4325376 | tf_op jit(solution)/shard_map/all_gather | solution.py:11
  65.9 14.9 %copy-start.251 = (f32[16,1,16]{2,1,0:T(1,128)}, f32[16,1,16]{2,1,0:T(1,128)S(1)}, u32[]{:S(2)}) copy-start(f32[16,1,16]{2,1,0:T(1,128)S(1)} %get-tuple-element.1006) | copy-start | bytes 3076
  80.8 143.8 %copy-start.46 = (f32[16,2048]{1,0:T(8,128)S(1)}, f32[16,2048]{1,0:T(8,128)}, u32[]{:S(2)}) copy-start(f32[16,2048]{1,0:T(8,128)} %get-tuple-element.982) | copy-start | bytes 393220
  80.9 143.8 %copy-start.47 = (f32[16,2048]{1,0:T(8,128)S(1)}, f32[16,2048]{1,0:T(8,128)}, u32[]{:S(2)}) copy-start(f32[16,2048]{1,0:T(8,128)} %get-tuple-element.984) | copy-start | bytes 393220
  80.9 143.8 %copy-start.48 = (f32[16,2048]{1,0:T(8,128)S(1)}, f32[16,2048]{1,0:T(8,128)}, u32[]{:S(2)}) copy-start(f32[16,2048]{1,0:T(8,128)} %get-tuple-element.985) | copy-start | bytes 393220
  88.3 136.4 %copy-start.39 = (f32[16,2048]{1,0:T(8,128)S(1)}, f32[16,2048]{1,0:T(8,128)}, u32[]{:S(2)}) copy-start(f32[16,2048]{1,0:T(8,128)} %get-tuple-element.971) | copy-start | bytes 393220
  88.3 136.4 %copy-start.40 = (f32[16,2048]{1,0:T(8,128)S(1)}, f32[16,2048]{1,0:T(8,128)}, u32[]{:S(2)}) copy-start(f32[16,2048]{1,0:T(8,128)} %get-tuple-element.972) | copy-start | bytes 393220
  88.3 136.4 %copy-start.41 = (f32[16,2048]{1,0:T(8,128)S(1)}, f32[16,2048]{1,0:T(8,128)}, u32[]{:S(2)}) copy-start(f32[16,2048]{1,0:T(8,128)} %get-tuple-element.973) | copy-start | bytes 393220
  88.3 136.4 %copy-start.42 = (f32[16,2048]{1,0:T(8,128)S(1)}, f32[16,2048]{1,0:T(8,128)}, u32[]{:S(2)}) copy-start(f32[16,2048]{1,0:T(8,128)} %get-tuple-element.983) | copy-start | bytes 393220
  256.6 58.6 %copy-start.70 = (f32[16,1,2048]{2,0,1:T(8,128)}, f32[16,1,2048]{2,0,1:T(8,128)S(1)}, u32[]{:S(2)}) copy-start(f32[16,1,2048]{2,0,1:T(8,128)S(1)} %copy.143) | copy-start | bytes 393220
  256.7 58.6 %copy-start.71 = (f32[16,1,2048]{2,0,1:T(8,128)}, f32[16,1,2048]{2,0,1:T(8,128)S(1)}, u32[]{:S(2)}) copy-start(f32[16,1,2048]{2,0,1:T(8,128)S(1)} %copy.144) | copy-start | bytes 393220
  292.6 274.9 %all-gather.17.cloned.1.call-start = ((), (), s32[]{:S(2)}) async-start(), calls=%async_computation.3 | async-start | bytes 4325376 | tf_op jit(solution)/shard_map/all_gather | solution.py:11
  357.9 33.9 %copy-start.35 = (f32[16,2048]{1,0:T(8,128)S(1)}, f32[16,2048]{1,0:T(8,128)}, u32[]{:S(2)}) copy-start(f32[16,2048]{1,0:T(8,128)} %get-tuple-element.962) | copy-start | bytes 393220
  357.9 33.9 %copy-start.38 = (f32[16,2048]{1,0:T(8,128)S(1)}, f32[16,2048]{1,0:T(8,128)}, u32[]{:S(2)}) copy-start(f32[16,2048]{1,0:T(8,128)} %get-tuple-element.969) | copy-start | bytes 393220
  400.7 10.1 %copy-start.66 = (f32[16,2048]{1,0:T(8,128)S(1)}, f32[16,2048]{1,0:T(8,128)}, u32[]{:S(2)}) copy-start(f32[16,2048]{1,0:T(8,128)} %get-tuple-element.842) | copy-start | bytes 393220
  400.7 10.8 %copy-start.64 = (f32[16,2048]{1,0:T(8,128)S(1)}, f32[16,2048]{1,0:T(8,128)}, u32[]{:S(2)}) copy-start(f32[16,2048]{1,0:T(8,128)} %get-tuple-element.832) | copy-start | bytes 393220
  505.3 225.2 %all-gather.19.cloned.1.call-start = ((), (), s32[]{:S(2)}) async-start(), calls=%async_computation.4 | async-start | bytes 4325376 | tf_op jit(solution)/shard_map/all_gather | solution.py:11
  601.3 17.1 %copy-start.13 = (f32[16,16,2048]{2,1,0:T(8,128)S(1)}, f32[16,16,2048]{2,1,0:T(8,128)}, u32[]{:S(2)}) copy-start(f32[16,16,2048]{2,1,0:T(8,128)} %get-tuple-element.648) | copy-start | bytes 6291460
  601.3 17.1 %copy-start.19 = (f32[16,2048]{1,0:T(8,128)S(1)}, f32[16,2048]{1,0:T(8,128)}, u32[]{:S(2)}) copy-start(f32[16,2048]{1,0:T(8,128)} %param.25) | copy-start | bytes 393220
  601.3 17.1 %copy-start.43 = (f32[16,2048]{1,0:T(8,128)S(1)}, f32[16,2048]{1,0:T(8,128)}, u32[]{:S(2)}) copy-start(f32[16,2048]{1,0:T(8,128)} %get-tuple-element.983) | copy-start | bytes 393220
  601.3 17.1 %copy-start.45 = (f32[16,2048]{1,0:T(8,128)S(1)}, f32[16,2048]{1,0:T(8,128)}, u32[]{:S(2)}) copy-start(f32[16,2048]{1,0:T(8,128)} %get-tuple-element.987) | copy-start | bytes 393220
  601.3 17.1 %copy-start.75 = (f32[16,1,2048]{2,0,1:T(8,128)S(1)}, f32[16,1,2048]{2,0,1:T(8,128)}, u32[]{:S(2)}) copy-start(f32[16,1,2048]{2,0,1:T(8,128)} %copy-done.73) | copy-start | bytes 393220
  601.3 17.1 %copy-start.82 = (f32[16,1,2048]{2,0,1:T(8,128)S(1)}, f32[16,1,2048]{2,0,1:T(8,128)}, u32[]{:S(2)}) copy-start(f32[16,1,2048]{2,0,1:T(8,128)} %copy-done.80) | copy-start | bytes 393220
  601.4 17.1 %copy-start.113 = (f32[16,2048]{1,0:T(8,128)S(1)}, f32[16,2048]{1,0:T(8,128)}, u32[]{:S(2)}) copy-start(f32[16,2048]{1,0:T(8,128)} %copy-done.105) | copy-start | bytes 393220
  601.4 17.1 %copy-start.152 = (f32[16,2048]{1,0:T(8,128)S(1)}, f32[16,2048]{1,0:T(8,128)}, u32[]{:S(2)}) copy-start(f32[16,2048]{1,0:T(8,128)} %copy-done.144) | copy-start | bytes 393220
  601.4 17.1 %copy-start.212 = (f32[16,1,16]{2,1,0:T(1,128)S(1)}, f32[16,1,16]{2,1,0:T(1,128)}, u32[]{:S(2)}) copy-start(f32[16,1,16]{2,1,0:T(1,128)} %copy-done.205) | copy-start | bytes 3076
  601.4 17.1 %copy-start.222 = (f32[16,1,16]{2,1,0:T(1,128)S(1)}, f32[16,1,16]{2,1,0:T(1,128)}, u32[]{:S(2)}) copy-start(f32[16,1,16]{2,1,0:T(1,128)} %get-tuple-element.1021) | copy-start | bytes 3076
  601.4 17.1 %copy-start.285 = (f32[16,1,16]{2,1,0:T(1,128)S(1)}, f32[16,1,16]{2,1,0:T(1,128)}, u32[]{:S(2)}) copy-start(f32[16,1,16]{2,1,0:T(1,128)} %get-tuple-element.1012) | copy-start | bytes 3076
  601.4 17.1 %copy-start.291 = (f32[16,1,16]{2,1,0:T(1,128)S(1)}, f32[16,1,16]{2,1,0:T(1,128)}, u32[]{:S(2)}) copy-start(f32[16,1,16]{2,1,0:T(1,128)} %get-tuple-element.1013) | copy-start | bytes 3076
  769.1 10.1 %copy-start.10 = (f32[16,16,2048]{2,1,0:T(8,128)S(1)}, f32[16,16,2048]{2,1,0:T(8,128)}, u32[]{:S(2)}) copy-start(f32[16,16,2048]{2,1,0:T(8,128)} %get-tuple-element.651) | copy-start | bytes 6291460
  769.1 10.1 %copy-start.30 = (f32[16,2048]{1,0:T(8,128)S(1)}, f32[16,2048]{1,0:T(8,128)}, u32[]{:S(2)}) copy-start(f32[16,2048]{1,0:T(8,128)} %get-tuple-element.965) | copy-start | bytes 393220
  769.1 10.1 %copy-start.32 = (f32[16,2048]{1,0:T(8,128)S(1)}, f32[16,2048]{1,0:T(8,128)}, u32[]{:S(2)}) copy-start(f32[16,2048]{1,0:T(8,128)} %get-tuple-element.966) | copy-start | bytes 393220
  769.1 10.1 %copy-start.34 = (f32[16,2048]{1,0:T(8,128)S(1)}, f32[16,2048]{1,0:T(8,128)}, u32[]{:S(2)}) copy-start(f32[16,2048]{1,0:T(8,128)} %get-tuple-element.967) | copy-start | bytes 393220
  769.2 10.1 %copy-start.69 = (f32[16,2048]{1,0:T(8,128)S(1)}, f32[16,2048]{1,0:T(8,128)}, u32[]{:S(2)}) copy-start(f32[16,2048]{1,0:T(8,128)} %subtract_negate_fusion) | copy-start | bytes 393220
  769.2 10.1 %copy-start.116 = (f32[16,2048]{1,0:T(8,128)S(1)}, f32[16,2048]{1,0:T(8,128)}, u32[]{:S(2)}) copy-start(f32[16,2048]{1,0:T(8,128)} %copy-done.105) | copy-start | bytes 393220
  769.2 10.1 %copy-start.126 = (f32[16,2048]{1,0:T(8,128)S(1)}, f32[16,2048]{1,0:T(8,128)}, u32[]{:S(2)}) copy-start(f32[16,2048]{1,0:T(8,128)} %copy-done.117) | copy-start | bytes 393220
  769.2 10.1 %copy-start.155 = (f32[16,2048]{1,0:T(8,128)S(1)}, f32[16,2048]{1,0:T(8,128)}, u32[]{:S(2)}) copy-start(f32[16,2048]{1,0:T(8,128)} %copy-done.144) | copy-start | bytes 393220
  769.2 10.1 %copy-start.204 = (f32[16,1,16]{2,1,0:T(1,128)S(1)}, f32[16,1,16]{2,1,0:T(1,128)}, u32[]{:S(2)}) copy-start(f32[16,1,16]{2,1,0:T(1,128)} %copy-done.198) | copy-start | bytes 3076
  769.2 10.1 %copy-start.214 = (f32[16,1,16]{2,1,0:T(1,128)S(1)}, f32[16,1,16]{2,1,0:T(1,128)}, u32[]{:S(2)}) copy-start(f32[16,1,16]{2,1,0:T(1,128)} %copy-done.205) | copy-start | bytes 3076
  769.2 10.1 %copy-start.224 = (f32[16,1,16]{2,1,0:T(1,128)S(1)}, f32[16,1,16]{2,1,0:T(1,128)}, u32[]{:S(2)}) copy-start(f32[16,1,16]{2,1,0:T(1,128)} %get-tuple-element.1021) | copy-start | bytes 3076
  (251 other events, 1290.6 us)
Sparse Core Ops, SparseCore 0:
  62.3 64.4 all-gather.12
  130.2 60.4 all-gather.10
  292.7 60.4 all-gather.14
  505.4 62.0 all-gather.16
  670.0 60.5 all-gather.18
where the time goes:
time: 860 us; the launch traced here: 850 us
  other arithmetic  459 us (53%)
  waiting for transfers between devices  206 us (24%)
  blocking collectives  78.7 us (9%)
  local copies, waits for them, and re-layouts  77.1 us (9%)
  between operations  24.8 us (3%)
    all_gather x5, waiting for transfers between devices, entering_2(): pieces = jax.tree.map(lambda part: lax.all_gather(part, axis), value)  206 us
    select_n x124, other arithmetic, lap(): jnp.where(position < mine, new, old)  133 us
    reduce_sum x13, other arithmetic, reverse_local(): jnp.sum(b_blocks[:, position][:, :, None] * gained, axis=1)  80.8 us
    psum x2, blocking collectives, paired(): lax.psum((jnp.sum(residual * residual), jnp.sum(residual * curved)), 'seq')  78.7 us
    reduce_sum x8, other arithmetic, forward_local(): pieces.append(jnp.sum(c_blocks[:, position][:, :, None] * state, axis=1))  54 us
    dynamic_update_slice x64, other arithmetic, forward_local(): lax.scan(forward_link_groups, start_state, (group_decay, state))  42.4 us
    reduce_sum x2, other arithmetic, forward_local(): jnp.sum(c_blocks[:, position][:, :, None] * (running * carried), axis=1)  33.9 us
    add x32, other arithmetic, reverse_link_groups(): return (decay_here * incoming + passed_here, incoming)  33.4 us
  transfers between devices with their start and end apart: 5, of which 5 were waited for; matrix products, arithmetic and copies ran while one was open for 12% of the time, Pallas kernels for 0%

commit v1 on v0

v1 whole, which is shorter than its diff:
```python
import functools

import jax
import jax.numpy as jnp
from jax import lax
from jax.experimental import pallas as pl
from jax.experimental.pallas import tpu as pltpu
from jax.sharding import PartitionSpec as P

SUB, LANE = 8, 128
LOG2E = 1.4426950408889634
LN2 = 0.6931471805599453
SMALL = 0.03
G1, G2, G3 = LN2, LN2 * LN2 / 2.0, LN2 * LN2 * LN2 / 6.0
F32 = jnp.float32


def gain_of(z):
    near = -z * (G1 + z * (G2 + z * G3))
    return jnp.where(z > -SMALL, near, 1.0 - jnp.exp2(z))


def sub_index():
    return lax.broadcasted_iota(jnp.int32, (SUB, LANE), 0)


def spread(row):
    return jnp.broadcast_to(row, (SUB, LANE))


def rolled(x, shift):
    return pltpu.roll(x, shift % SUB, 0)


def scan_chunks(value, decay, backward):
    at = sub_index()
    edge = at == (SUB - 1 if backward else 0)
    keep = jnp.where(edge, 0.0, decay)
    for step in (1, 2, 4):
        shift = -step if backward else step
        value = value + keep * rolled(value, shift)
        if step < 4:
            keep = keep * rolled(keep, shift)
    entering = jnp.where(edge, 0.0, rolled(value, -1 if backward else 1))
    last = value[0:1] if backward else value[SUB - 1 : SUB]
    return entering, last


def totals_around(total):
    at = sub_index()
    before = jnp.zeros_like(total)
    after = jnp.zeros_like(total)
    for step in range(1, SUB):
        before = before + jnp.where(at >= step, rolled(total, step), 0.0)
        after = after + jnp.where(at < SUB - step, rolled(total, -step), 0.0)
    return before, after


def summed(parts):
    while len(parts) > 1:
        parts = [sum(parts[i : i + 2]) for i in range(0, len(parts), 2)]
    return parts[0]


class Sizes:
    def __init__(self, tokens, columns, entries, devices):
        self.tokens, self.columns = tokens, columns
        self.entries, self.devices = entries, devices
        self.steps = tokens // SUB
        self.blocks = columns // LANE
        self.rows = entries * self.blocks // devices


def cols(block):
    return pl.ds(pl.multiple_of(block * LANE, LANE), LANE)


def write_state(s, ref, block, rows_of):
    per = s.entries // s.rows
    for piece in range(per):
        where = block * per + piece
        for row in range(s.rows):
            ref[where, row : row + 1, :] = rows_of[piece * s.rows + row]


def read_state(s, ref, block):
    per = s.entries // s.rows
    out = []
    for piece in range(per):
        where = block * per + piece
        for row in range(s.rows):
            out.append(spread(ref[where, row : row + 1, :]))
    return out


def load_rates(s, rate_ref, block):
    return [
        spread(rate_ref[n : n + 1, cols(block)]) * (-LOG2E) for n in range(s.entries)
    ]


def forward_summary(s, block, get_v, gain_ref, bx_ref, rates, total, e_ref, put):
    state = [jnp.zeros((SUB, LANE), F32)] * s.entries
    for j in range(s.steps):
        v = get_v(j)
        for n in range(s.entries):
            state[n] = state[n] + gain_ref[block, j, n] * (bx_ref[j, n] * v - state[n])
    finish_summary(s, block, state, rates, total, e_ref, put, False)


def backward_summary(s, block, get_w, gain_ref, cx_ref, rates, total, e_ref, put):
    passed = [jnp.zeros((SUB, LANE), F32)] * s.entries
    for j in reversed(range(s.steps)):
        w = get_w(j)
        for n in range(s.entries):
            costate = cx_ref[j, n] * w + passed[n]
            passed[n] = costate - gain_ref[block, j, n] * costate
    finish_summary(s, block, passed, rates, total, e_ref, put, True)


def finish_summary(s, block, state, rates, total, e_ref, put, backward):
    lasts = []
    for n in range(s.entries):
        entering, last = scan_chunks(
            state[n], jnp.exp2(total * rates[n]), backward
        )
        e_ref[block, n] = entering
        lasts.append(last)
    write_state(s, put, block, lasts)


def first_kernel(
    s, rhs_ref, delta_ref, rate_ref, b_ref, c_ref,
    gain_ref, bx_ref, cx_ref, total_ref, e_ref, out_ref, tile_v, tile_d,
):
    for j in range(s.steps):
        rows = pl.ds(j, SUB, stride=s.steps)
        b, c = b_ref[rows, :], c_ref[rows, :]
        for n in range(s.entries):
            bx_ref[j, n] = jnp.broadcast_to(b[:, n : n + 1], (SUB, LANE))
            cx_ref[j, n] = jnp.broadcast_to(c[:, n : n + 1], (SUB, LANE))

    def body(block, carry):
        tile_v[...] = rhs_ref[:, cols(block)]
        tile_d[...] = delta_ref[:, cols(block)]
        rates = load_rates(s, rate_ref, block)
        total = jnp.zeros((SUB, LANE), F32)
        for j in range(s.steps):
            d = tile_d[pl.ds(j, SUB, stride=s.steps), :]
            total = total + d
            for n in range(s.entries):
                gain_ref[block, j, n] = gain_of(d * rates[n])
        total_ref[block] = total

        def get_v(j):
            return tile_v[pl.ds(j, SUB, stride=s.steps), :]

        forward_summary(
            s, block, get_v, gain_ref, bx_ref, rates, total, e_ref, out_ref
        )
        whole = jnp.sum(total, axis=0, keepdims=True)
        per = s.entries // s.rows
        for n in range(s.entries):
            out_ref[
                block * per + n // s.rows,
                s.rows + n % s.rows : s.rows + n % s.rows + 1,
                :,
            ] = jnp.exp2(whole * rates[n][0:1])
        return carry

    lax.fori_loop(0, s.blocks, body, 0)


def put_sums(s, out_ref, first, second):
    first = jnp.sum(first, axis=0, keepdims=True)
    second = jnp.sum(second, axis=0, keepdims=True)

    def body(device, carry):
        out_ref[device, s.rows : s.rows + 1, :] = first
        out_ref[device, s.rows + 1 : s.rows + 2, :] = second
        return carry

    lax.fori_loop(0, s.devices, body, 0)


def link_kernel(s, backward, has_sums, got_ref, decay_ref, arrive_ref, sums_ref):
    carried = jnp.zeros((s.rows, LANE), F32)
    first = jnp.zeros((1, LANE), F32)
    second = jnp.zeros((1, LANE), F32)
    order = range(s.devices)
    for device in reversed(order) if backward else order:
        arrive_ref[device] = carried
        carried = (
            decay_ref[device, s.rows : 2 * s.rows, :] * carried
            + got_ref[device, 0 : s.rows, :]
        )
        if has_sums:
            first = first + got_ref[device, s.rows : s.rows + 1, :]
            second = second + got_ref[device, s.rows + 1 : s.rows + 2, :]
    sums_ref[0] = spread(jnp.sum(first, axis=1, keepdims=True))
    sums_ref[1] = spread(jnp.sum(second, axis=1, keepdims=True))


def enter(s, arrive_ref, e_ref, block, rates, around):
    arrive = read_state(s, arrive_ref, block)
    return [
        e_ref[block, n] + jnp.exp2(around * rates[n]) * arrive[n]
        for n in range(s.entries)
    ]


def forward_kernel(s, first, *refs):
    refs = list(refs)
    v_ref, curv_ref, rate_ref, skip_ref, damp_ref = refs[:5]
    gain_ref, bx_ref, cx_ref, total_ref, e_in, arrive_ref = refs[5:11]
    refs = refs[11:]
    if not first:
        rhs_ref, y0_ref, sums_b, sums_c = refs[:4]
        refs = refs[4:]
        ratio = sums_c[0] / sums_b[0]
    e_out, out_ref, w_ref = refs[:3]
    refs = refs[3:]
    y_ref, tile_v, tile_c = refs if first else (refs[0], refs[1], refs[2])

    def body(block, carry):
        squares, inner = carry
        tile_c[...] = curv_ref[:, cols(block)]
        if first:
            tile_v[...] = v_ref[:, cols(block)]
        else:
            tile_v[...] = rhs_ref[:, cols(block)]
        rates = load_rates(s, rate_ref, block)
        total = total_ref[block]
        before, after = totals_around(total)
        skip = spread(skip_ref[0:1, cols(block)])
        damp = spread(damp_ref[0:1, cols(block)])
        state = enter(s, arrive_ref, e_in, block, rates, before)
        for j in range(s.steps):
            rows = pl.ds(j, SUB, stride=s.steps)
            v = tile_v[rows, :] if first else v_ref[block, j]
            parts = [skip * v]
            for n in range(s.entries):
                state[n] = state[n] + gain_ref[block, j, n] * (
                    bx_ref[j, n] * v - state[n]
                )
                parts.append(cx_ref[j, n] * state[n])
            y = summed(parts)
            if first:
                y_ref[block, j] = y
                squares = squares + v * v
                along = v
            else:
                y = y + ratio * y0_ref[block, j]
                along = v + ratio * tile_v[rows, :]
                y_ref[block, j] = along
            w = tile_c[rows, :] * y
            w_ref[block, j] = w
            inner = inner + (w * y + damp * (along * along))

        def get_w(j):
            return w_ref[block, j]

        backward_summary(
            s, block, get_w, gain_ref, cx_ref, rates, total, e_out, out_ref
        )
        return squares, inner

    zero = jnp.zeros((SUB, LANE), F32)
    squares, inner = lax.fori_loop(0, s.blocks, body, (zero, zero))
    put_sums(s, out_ref, squares, inner)


def backward_block(s, block, w_ref, skip, gain_ref, bx_ref, cx_ref, passed, use):
    for j in reversed(range(s.steps)):
        w = w_ref[block, j]
        parts = [skip * w]
        for n in range(s.entries):
            costate = cx_ref[j, n] * w + passed[n]
            gained = gain_ref[block, j, n] * costate
            passed[n] = costate - gained
            parts.append(bx_ref[j, n] * gained)
        use(j, summed(parts))


def backward_kernel(
    s, w_ref, rhs_ref, rate_ref, skip_ref, damp_ref,
    gain_ref, bx_ref, cx_ref, total_ref, e_in, arrive_ref, sums_ref,
    e_out, out_ref, r_ref, tile_v,
):
    step = sums_ref[0] / sums_ref[1]

    def body(block, squares):
        tile_v[...] = rhs_ref[:, cols(block)]
        rates = load_rates(s, rate_ref, block)
        total = total_ref[block]
        before, after = totals_around(total)
        skip = spread(skip_ref[0:1, cols(block)])
        damp = spread(damp_ref[0:1, cols(block)])
        passed = enter(s, arrive_ref, e_in, block, rates, after)
        acc = [squares]

        def use(j, product):
            v = tile_v[pl.ds(j, SUB, stride=s.steps), :]
            r = v - step * (product + damp * v)
            r_ref[block, j] = r
            acc[0] = acc[0] + r * r

        backward_block(s, block, w_ref, skip, gain_ref, bx_ref, cx_ref, passed, use)

        def get_v(j):
            return r_ref[block, j]

        forward_summary(
            s, block, get_v, gain_ref, bx_ref, rates, total, e_out, out_ref
        )
        return acc[0]

    zero = jnp.zeros((SUB, LANE), F32)
    squares = lax.fori_loop(0, s.blocks, body, zero)
    put_sums(s, out_ref, squares, zero)


def last_kernel(
    s, w_ref, rhs_ref, r_ref, d_ref, rate_ref, skip_ref, damp_ref,
    gain_ref, bx_ref, cx_ref, total_ref, e_in, arrive_ref, sums_b, sums_c, sums_d,
    solution_ref, residual_ref, tile_v, tile_s, tile_r,
):
    before_step = sums_b[0] / sums_b[1]
    step = sums_c[0] / sums_d[1]

    def body(block, carry):
        tile_v[...] = rhs_ref[:, cols(block)]
        rates = load_rates(s, rate_ref, block)
        total = total_ref[block]
        before, after = totals_around(total)
        skip = spread(skip_ref[0:1, cols(block)])
        damp = spread(damp_ref[0:1, cols(block)])
        passed = enter(s, arrive_ref, e_in, block, rates, after)

        def use(j, product):
            rows = pl.ds(j, SUB, stride=s.steps)
            along = d_ref[block, j]
            tile_s[rows, :] = before_step * tile_v[rows, :] + step * along
            tile_r[rows, :] = r_ref[block, j] - step * (product + damp * along)

        backward_block(s, block, w_ref, skip, gain_ref, bx_ref, cx_ref, passed, use)
        solution_ref[:, cols(block)] = tile_s[...]
        residual_ref[:, cols(block)] = tile_r[...]
        return carry

    lax.fori_loop(0, s.blocks, body, 0)


VM = pl.BlockSpec(memory_space=pltpu.VMEM)
LIMIT = 4 * 1024 * 1024


def call(body, name, outs, scratch, args, limit=LIMIT):
    return pl.pallas_call(
        body,
        name=name,
        out_shape=outs,
        in_specs=[VM] * len(args),
        out_specs=[VM] * len(outs),
        scratch_shapes=scratch,
        compiler_params=pltpu.CompilerParams(vmem_limit_bytes=limit),
    )(*args)


def per_device(devices, rhs, rate, delta, b_proj, c_proj, skip, curvature, damping):
    tokens, columns = rhs.shape
    s = Sizes(tokens, columns, rate.shape[0], devices)
    skip, damping = skip[None], damping[None]
    held = pltpu.VMEM
    per_token = (s.blocks, s.steps, SUB, LANE)
    expanded = (s.steps, s.entries, SUB, LANE)
    edge = (s.blocks, s.entries, SUB, LANE)
    tile = pltpu.VMEM((tokens, LANE), F32)
    packet = jax.ShapeDtypeStruct((devices, 2 * s.rows, LANE), F32)

    def exchange(send):
        return lax.all_to_all(send, "seq", 0, 0)

    def link(got, decays, backward, has_sums, name):
        arrive, sums = call(
            functools.partial(link_kernel, s, backward, has_sums),
            name,
            [
                jax.ShapeDtypeStruct((devices, s.rows, LANE), F32),
                held((2, SUB, LANE), F32),
            ],
            [],
            (got, decays),
        )
        return exchange(arrive), sums

    gain, bx, cx, total, e, send = call(
        functools.partial(first_kernel, s),
        "first",
        [
            held((s.blocks, s.steps, s.entries, SUB, LANE), F32),
            held(expanded, F32),
            held(expanded, F32),
            held((s.blocks, SUB, LANE), F32),
            held(edge, F32),
            packet,
        ],
        [tile, tile],
        (rhs, delta, rate, b_proj, c_proj),
    )
    got_a = exchange(send)
    arrive, _ = link(got_a, got_a, False, False, "link_a")
    e, send, w, y0 = call(
        functools.partial(forward_kernel, s, True),
        "forward_a",
        [held(edge, F32), packet, held(per_token, F32), held(per_token, F32)],
        [tile, tile],
        (rhs, curvature, rate, skip, damping, gain, bx, cx, total, e, arrive),
    )
    arrive, sums_b = link(exchange(send), got_a, True, True, "link_b")
    e, send, r = call(
        functools.partial(backward_kernel, s),
        "backward_a",
        [held(edge, F32), packet, held(per_token, F32)],
        [tile],
        (w, rhs, rate, skip, damping, gain, bx, cx, total, e, arrive, sums_b),
    )
    arrive, sums_c = link(exchange(send), got_a, False, True, "link_c")
    e, send, w, d = call(
        functools.partial(forward_kernel, s, False),
        "forward_b",
        [held(edge, F32), packet, held(per_token, F32), held(per_token, F32)],
        [tile, tile],
        (
            r, curvature, rate, skip, damping, gain, bx, cx, total, e, arrive,
            rhs, y0, sums_b, sums_c,
        ),
    )
    arrive, sums_d = link(exchange(send), got_a, True, True, "link_d")
    whole = jax.ShapeDtypeStruct((tokens, columns), F32)
    return call(
        functools.partial(last_kernel, s),
        "backward_b",
        [whole, whole],
        [tile, tile, tile],
        (
            w, rhs, r, d, rate, skip, damping, gain, bx, cx, total, e, arrive,
            sums_b, sums_c, sums_d,
        ),
    )


def solution(mesh):
    placed = (
        P("seq", None),
        P(),
        P("seq", None),
        P("seq", None),
        P("seq", None),
        P(),
        P("seq", None),
        P(),
    )
    return jax.shard_map(
        functools.partial(per_device, mesh.shape["seq"]),
        mesh=mesh,
        in_specs=placed,
        out_specs=(P("seq", None), P("seq", None)),
        check_vma=False,
    )
```

time: 860 us -> 146 us (0.17); the launches traced: 850 us -> 146 us
  other arithmetic: 459 us -> 0 us
  waiting for transfers between devices: 206 us -> 0 us
  local copies, waits for them, and re-layouts: 77.1 us -> 8.8 us
  Pallas kernels: 0 us -> 39.9 us
  between operations: 24.8 us -> 0.7 us
  blocking collectives: 78.7 us -> 96.3 us
    all_gather x5 -> x0, waiting for transfers between devices: 206 us -> none  [entering_2(): pieces = jax.tree.map(lambda part: lax.all_gather(part, axis), value)]
    reduce_sum x25 -> x0, other arithmetic: 175 us -> none  [the longest x13 80.8 us: reverse_local(): jnp.sum(b_blocks[:, position][:, :, None] * gained, axis=1)]
    select_n x124 -> x0, other arithmetic: 133 us -> none  [lap(): jnp.where(position < mine, new, old)]
    all_to_all x0 -> x8, blocking collectives: none -> 96.3 us  [exchange(): return lax.all_to_all(send, 'seq', 0, 0)]
    psum x2 -> x0, blocking collectives: 78.7 us -> none  [paired(): lax.psum((jnp.sum(residual * residual), jnp.sum(residual * curved)), 'seq')]
    add x96 -> x0, other arithmetic: 66.3 us -> none  [the longest x32 33.4 us: reverse_link_groups(): return (decay_here * incoming + passed_here, incoming)]
    dynamic_update_slice x64 -> x0, other arithmetic: 42.4 us -> none  [forward_local(): lax.scan(forward_link_groups, start_state, (group_decay, state))]
    pallas_call x0 -> x9, Pallas kernels: none -> 39.9 us  [call(): pl.pallas_call(body, name=name, out_shape=outs, in_specs=[VM] * len(args)...]
  transfers between devices with their start and end apart: 5 -> 0, of which waited for: 5 -> 0; matrix products, arithmetic and copies ran while one was open for 12% -> 0% of each run, Pallas kernels for 0% -> 0%
where the time goes in v1:
time: 146 us
  blocking collectives  96.3 us (66%)
  Pallas kernels  39.9 us (27%)
  local copies, waits for them, and re-layouts  8.8 us (6%)
    all_to_all x8, blocking collectives, exchange(): return lax.all_to_all(send, 'seq', 0, 0)  96.3 us
    pallas_call x9, Pallas kernels, call(): pl.pallas_call(body, name=name, out_shape=outs, in_specs=[VM] * len(args)...  39.9 us
    unnamed x22, local copies, waits for them, and re-layouts  8.8 us

profile of v1, /device:TPU:0, one launch (start us, length us, event | category | flops | bytes accessed | tf_op | source)
XLA Modules:
  0.0 145.7 jit_solution(14977233754343116924)
XLA Ops:
  0.6 0.0 copy-start.9
  0.6 0.8 copy.10.b_ref
  1.4 0.8 copy.11.c_ref
  2.2 0.0 copy-start
  2.2 1.2 copy-done
  3.5 0.0 copy-start.5
  3.5 0.9 copy-done.5
  4.4 0.0 copy-start.6
  4.4 1.2 copy-done.6
  5.6 0.0 copy-start.2
  5.6 10.6 %first.1 = (f32[16,16,16,8,128]{4,3,2,1,0:T(8,128)S(1)}, f32[16,16,8,128]{3,2,1,0:T(8,128)S(1)}, f32[16,16,8,128]{3,2,1,0:T(8,128)S(1)}, f32[16,8,128]{2,1,0:T(8...) custom-call(f32[128,2048]{1,0:T(8,128)S(1)} %copy-done, f32[128,2048]{1,0:T(8,128)S(1)} %copy-done.6, ...), custom_call_target="tpu_custom_call" | custom-call | tf_op jit(solution)/shard_map/first/pallas_call | solution.py:359
  16.2 17.7 %all_to_all.40.got_ref.decay_ref = f32[32,16,128]{2,1,0:T(8,128)S(1)} all-to-all(f32[32,16,128]{2,1,0:T(8,128)S(1)} %get-tuple-element.31), channel_id=1, replica_groups=mesh['seq'=32] {'seq'}, dimensions={0} | all-to-all | bytes 524288 | tf_op jit(solution)/shard_map/all_to_all | solution.py:382
  33.9 0.7 link_a.1
  34.6 10.4 %all_to_all.41.refs_10_ = f32[32,8,128]{2,1,0:T(8,128)S(1)} all-to-all(f32[32,8,128]{2,1,0:T(8,128)S(1)} %get-tuple-element.32), channel_id=1, replica_groups=mesh['seq'=32] {'seq'}, dimensions={0} | all-to-all | bytes 262144 | tf_op jit(solution)/shard_map/all_to_all | solution.py:382
  45.0 0.0 copy-start.1
  45.0 1.2 copy-done.1
  46.2 0.0 copy-start.3
  46.2 1.2 copy-done.3
  47.5 0.0 copy-start.7
  47.5 0.7 copy-done.7
  48.2 0.0 copy-start.8
  48.2 0.7 copy-done.8
  48.9 7.5 %forward_a.1 = (f32[16,16,8,128]{3,2,1,0:T(8,128)S(1)}, f32[32,16,128]{2,1,0:T(8,128)S(1)}, f32[16,16,8,128]{3,2,1,0:T(8,128)S(1)}, f32[16,16,8,128]{3,2,1,0:T(8,128)S(1)}) custom-call(f32[128,2048]{1,0:T(8,128)S(1)} %copy-done.1, f32[128,2048]{1,0:T(8,128)S(1)} %copy-done.3, f32[16,2048]{1,0:T(8,128)S(1)} %copy-done.5, f32[1,2048]{1,0:T(1,128)S(1)} %bitcast.2, ...), custom_call_target="tpu_custom_call" | custom-call | tf_op jit(solution)/shard_map/forward_a/pallas_call | solution.py:359
  56.4 0.0 copy-start.4
  56.4 12.4 %all_to_all.42.got_ref = f32[32,16,128]{2,1,0:T(8,128)S(1)} all-to-all(f32[32,16,128]{2,1,0:T(8,128)S(1)} %get-tuple-element.35), channel_id=1, replica_groups=mesh['seq'=32] {'seq'}, dimensions={0} | all-to-all | bytes 524288 | tf_op jit(solution)/shard_map/all_to_all | solution.py:382
  68.8 0.1 link_b.1
  68.9 10.3 %all_to_all.43.arrive_ref = f32[32,8,128]{2,1,0:T(8,128)S(1)} all-to-all(f32[32,8,128]{2,1,0:T(8,128)S(1)} %get-tuple-element.36), channel_id=1, replica_groups=mesh['seq'=32] {'seq'}, dimensions={0} | all-to-all | bytes 262144 | tf_op jit(solution)/shard_map/all_to_all | solution.py:382
  79.2 0.0 copy-done.9
  79.2 0.0 copy-done.2
  79.2 7.3 %backward_a.1 = (f32[16,16,8,128]{3,2,1,0:T(8,128)S(1)}, f32[32,16,128]{2,1,0:T(8,128)S(1)}, f32[16,16,8,128]{3,2,1,0:T(8,128)S(1)}) custom-call(f32[16,16,8,128]{3,2,1,0:T(8,128)S(1)} %get-tuple-element.33.w_ref, f32[128,2048]{1,0:T(8,128)S(1)} %copy-done.2, f32[16,2048]{1,0:T(8,128)S(1)} %copy-done.5, f32[1,2048]{1,0:T(1,128)S(1)} %bitcast.3, ...), custom_call_target="tpu_custom_call" | custom-call | tf_op jit(solution)/shard_map/backward_a/pallas_call | solution.py:359
  86.5 12.3 %all_to_all.44.got_ref = f32[32,16,128]{2,1,0:T(8,128)S(1)} all-to-all(f32[32,16,128]{2,1,0:T(8,128)S(1)} %get-tuple-element.40), channel_id=1, replica_groups=mesh['seq'=32] {'seq'}, dimensions={0} | all-to-all | bytes 524288 | tf_op jit(solution)/shard_map/all_to_all | solution.py:382
  98.8 0.1 link_c.1
  99.0 10.4 %all_to_all.45.refs_10_ = f32[32,8,128]{2,1,0:T(8,128)S(1)} all-to-all(f32[32,8,128]{2,1,0:T(8,128)S(1)} %get-tuple-element.41), channel_id=1, replica_groups=mesh['seq'=32] {'seq'}, dimensions={0} | all-to-all | bytes 262144 | tf_op jit(solution)/shard_map/all_to_all | solution.py:382
  109.4 0.0 copy-done.4
  109.4 7.5 %forward_b.1 = (f32[16,16,8,128]{3,2,1,0:T(8,128)S(1)}, f32[32,16,128]{2,1,0:T(8,128)S(1)}, f32[16,16,8,128]{3,2,1,0:T(8,128)S(1)}, f32[16,16,8,128]{3,2,1,0:T(8,128)S(1)}) custom-call(f32[16,16,8,128]{3,2,1,0:T(8,128)S(1)} %get-tuple-element.38.refs_0_.r_ref, f32[128,2048]{1,0:T(8,128)S(1)} %copy-done.4, f32[16,2048]{1,0:T(8,128)S(1)} %copy-done.5, ...), custom_call_target="tpu_custom_call" | custom-call | tf_op jit(solution)/shard_map/forward_b/pallas_call | solution.py:359
  116.9 12.3 %all_to_all.46.got_ref = f32[32,16,128]{2,1,0:T(8,128)S(1)} all-to-all(f32[32,16,128]{2,1,0:T(8,128)S(1)} %get-tuple-element.47), channel_id=1, replica_groups=mesh['seq'=32] {'seq'}, dimensions={0} | all-to-all | bytes 524288 | tf_op jit(solution)/shard_map/all_to_all | solution.py:382
  129.3 0.1 link_d.1
  129.4 10.4 %all_to_all.47.arrive_ref = f32[32,8,128]{2,1,0:T(8,128)S(1)} all-to-all(f32[32,8,128]{2,1,0:T(8,128)S(1)} %get-tuple-element.48), channel_id=1, replica_groups=mesh['seq'=32] {'seq'}, dimensions={0} | all-to-all | bytes 262144 | tf_op jit(solution)/shard_map/all_to_all | solution.py:382
  139.8 5.9 %backward_b.1 = (f32[128,2048]{1,0:T(8,128)}, f32[128,2048]{1,0:T(8,128)}) custom-call(f32[16,16,8,128]{3,2,1,0:T(8,128)S(1)} %get-tuple-element.44.w_ref, f32[128,2048]{1,0:T(8,128)S(1)} %copy-done.2, f32[16,16,8,128]{3,2,1,0:T(8,128)S(1)} %get-tuple-element.38.refs_0_.r_ref, f32[16,16,8,128]{3,2,1,0:T(8,128)S(1)} %get-tuple-element.45.d_ref, ...), custom_call_target="tpu_custom_call" | custom-call | tf_op jit(solution)/shard_map/backward_b/pallas_call | solution.py:359
Async XLA Ops:
  0.6 78.6 %copy-start.9 = (f32[2048]{0:T(1024)S(1)}, f32[2048]{0:T(1024)}, u32[]{:S(2)}) copy-start(f32[2048]{0:T(1024)} %param.15) | copy-start | bytes 24580
  2.2 1.2 copy-start
  3.5 0.9 copy-start.5
  4.4 1.2 copy-start.6
  5.6 73.6 %copy-start.2 = (f32[128,2048]{1,0:T(8,128)S(1)}, f32[128,2048]{1,0:T(8,128)}, u32[]{:S(2)}) copy-start(f32[128,2048]{1,0:T(8,128)} %rhs_ref.5) | copy-start | bytes 3145732
  45.0 1.2 copy-start.1
  46.2 1.2 copy-start.3
  47.5 0.7 copy-start.7
  48.2 0.7 copy-start.8
  56.4 53.0 %copy-start.4 = (f32[128,2048]{1,0:T(8,128)S(1)}, f32[128,2048]{1,0:T(8,128)}, u32[]{:S(2)}) copy-start(f32[128,2048]{1,0:T(8,128)} %refs_1_.3) | copy-start | bytes 3145732

commit v2 on v1

v2 whole, which is shorter than its diff:
```python
import functools

import jax
import jax.numpy as jnp
from jax import lax
from jax.experimental import pallas as pl
from jax.experimental.pallas import tpu as pltpu
from jax.sharding import PartitionSpec as P

STREAMS = 1
SUB, LANE = 8, 128
LOG2E = 1.4426950408889634
LN2 = 0.6931471805599453
SMALL = 0.03
G1, G2, G3 = -LN2, -LN2 * LN2 / 2.0, -LN2 * LN2 * LN2 / 6.0
F32 = jnp.float32


def sub_index():
    return lax.broadcasted_iota(jnp.int32, (SUB, LANE), 0)


def spread(row):
    return jnp.broadcast_to(row, (SUB, LANE))


def rolled(x, shift):
    return pltpu.roll(x, shift % SUB, 0)


def scan_chunks(value, decay, backward):
    at = sub_index()
    edge = at == (SUB - 1 if backward else 0)
    keep = jnp.where(edge, 0.0, decay)
    for step in (1, 2, 4):
        shift = -step if backward else step
        value = value + keep * rolled(value, shift)
        if step < 4:
            keep = keep * rolled(keep, shift)
    entering = jnp.where(edge, 0.0, rolled(value, -1 if backward else 1))
    last = value[0:1] if backward else value[SUB - 1 : SUB]
    return entering, last


def total_around(total, backward):
    at = sub_index()
    edge = at == (SUB - 1 if backward else 0)
    side = -1 if backward else 1
    value = jnp.where(edge, 0.0, rolled(total, side))
    for step in (1, 2, 4):
        inside = at < SUB - step if backward else at >= step
        value = value + jnp.where(inside, rolled(value, side * step), 0.0)
    return value


def summed(parts):
    while len(parts) > 1:
        parts = [sum(parts[i : i + 2]) for i in range(0, len(parts), 2)]
    return parts[0]


class Sizes:
    def __init__(self, tokens, columns, entries, devices, streams):
        self.tokens, self.entries, self.devices = tokens, entries, devices
        self.steps = tokens // SUB
        self.blocks = columns // LANE // streams
        self.rows = entries * self.blocks // devices
        self.per = entries // self.rows


def cols(block):
    return pl.ds(pl.multiple_of(block * LANE, LANE), LANE)


def lane_row(row):
    return pl.ds(row * LANE, LANE)


def write_state(s, ref, block, rows_of):
    for n, value in enumerate(rows_of):
        ref[block * s.per + n // s.rows, 0:1, lane_row(n % s.rows)] = value


def read_state(s, ref, block):
    return [
        spread(ref[block * s.per + n // s.rows, 0:1, lane_row(n % s.rows)])
        for n in range(s.entries)
    ]


def load_rates(s, rate_ref, block):
    return [spread(rate_ref[n : n + 1, cols(block)]) for n in range(s.entries)]


def finish_summary(s, block, state, rates, total, e_ref, put, backward):
    lasts = []
    for n in range(s.entries):
        entering, last = scan_chunks(state[n], jnp.exp2(total * rates[n]), backward)
        e_ref[block, n] = entering
        lasts.append(last)
    write_state(s, put, block, lasts)


def zeros(count):
    return [jnp.zeros((SUB, LANE), F32)] * count


def first_kernel(s, offset, *refs):
    rhs_hbm, delta_hbm, curv_hbm, rate_hbm, skip_hbm, damp_hbm, bt_hbm, ct_hbm = refs[:8]
    (
        decay_ref, drive_ref, cx_ref, total_ref, e_ref, out_ref,
        rhs_ref, curv_ref, rate_ref, skip_ref, damp_ref, link_rate_ref,
    ) = refs[8:20]
    delta_ref, bx_ref, wide_ref, turn_ref, sem_d, sem_v, sem_c, sem_s = refs[20:]

    small = [
        pltpu.make_async_copy(src, dst, sem_s.at[i])
        for i, (src, dst) in enumerate(
            [
                (bt_hbm, wide_ref.at[0]), (ct_hbm, wide_ref.at[1]), (rate_hbm, rate_ref),
                (skip_hbm, skip_ref), (damp_hbm, damp_ref),
            ]
        )
    ]

    def block_copy(src, dst, sem, block):
        return pltpu.make_async_copy(
            src.at[:, cols(block + offset)], dst.at[block], sem.at[block]
        )

    for copy in small[:3]:
        copy.start()
    for block in range(s.blocks):
        block_copy(delta_hbm, delta_ref, sem_d, block).start()
        block_copy(rhs_hbm, rhs_ref, sem_v, block).start()
    for copy in small[3:]:
        copy.start()
    for block in range(s.blocks):
        block_copy(curv_hbm, curv_ref, sem_c, block).start()

    for index, dst in enumerate([bx_ref, cx_ref]):
        small[index].wait()
        turn_ref[index] = jnp.transpose(wide_ref[index])
        for j in range(s.steps):
            turned = turn_ref[index, pl.ds(j, SUB, stride=s.steps), :]
            for n in range(s.entries):
                dst[j, n] = jnp.broadcast_to(turned[:, n : n + 1], (SUB, LANE))
    small[2].wait()
    rate_ref[...] = rate_ref[...] * (-LOG2E)

    def body(block, carry):
        block_copy(delta_hbm, delta_ref, sem_d, block).wait()
        block_copy(rhs_hbm, rhs_ref, sem_v, block).wait()
        own = [rate_ref[n : n + 1, cols(block + offset)] for n in range(s.entries)]
        write_state(s, link_rate_ref, block, own)
        rates = [spread(row) for row in own]

        def advance(j, state):
            total, state = state[0], list(state[1:])
            rows = pl.ds(j, SUB, stride=s.steps)
            d = delta_ref[block, rows, :]
            v = rhs_ref[block, rows, :]
            total = total + d
            for n in range(s.entries):
                z = d * rates[n]
                decay = jnp.exp2(z)
                near = z * (G1 + z * (G2 + z * G3))
                drive = jnp.where(z > -SMALL, near, 1.0 - decay) * bx_ref[j, n]
                decay_ref[block, j, n] = decay
                drive_ref[block, j, n] = drive
                state[n] = decay * state[n] + drive * v
            return (total, *state)

        result = lax.fori_loop(0, s.steps, advance, tuple(zeros(s.entries + 1)), unroll=8)
        total, state = result[0], result[1:]
        total_ref[block] = total
        finish_summary(s, block, state, rates, total, e_ref, out_ref, False)
        whole = jnp.sum(total, axis=0, keepdims=True)
        for piece in range(s.per):
            out_ref[block * s.per + piece, 0:1, lane_row(s.rows)] = whole
        return carry

    lax.fori_loop(0, s.blocks, body, 0)
    small[3].wait()
    small[4].wait()

    def finish(block, carry):
        block_copy(curv_hbm, curv_ref, sem_c, block).wait()
        return carry

    lax.fori_loop(0, s.blocks, finish, 0)


def put_sums(s, out_ref, first, second):
    first = jnp.sum(first, axis=0, keepdims=True)
    second = jnp.sum(second, axis=0, keepdims=True)
    half = LANE // 2
    first = first + pltpu.roll(first, half, 1)
    second = second + pltpu.roll(second, half, 1)
    lane = lax.broadcasted_iota(jnp.int32, (1, LANE), 1)
    both = jnp.where(lane < half, first, second)

    def body(device, carry):
        out_ref[device, 0:1, lane_row(s.rows)] = both
        return carry

    lax.fori_loop(0, s.devices, body, 0, unroll=8)


def link_kernel(s, backward, first, *refs):
    if first:
        got_ref, link_rate_ref, arrive_ref, decay_ref = refs
        rates = link_rate_ref[lax.axis_index("seq")]
    else:
        got_ref, decay_ref, arrive_ref, sums_ref = refs
    wide = s.rows * LANE
    carried = jnp.zeros((1, wide), F32)
    tail = jnp.zeros((1, LANE), F32)
    order = range(s.devices)
    for device in reversed(order) if backward else order:
        extra = got_ref[device, :, lane_row(s.rows)]
        if first:
            decay = jnp.exp2(jnp.concatenate([extra] * s.rows, axis=1) * rates)
            decay_ref[device] = decay
        else:
            decay = decay_ref[device]
            tail = tail + extra
        arrive_ref[device] = carried
        carried = decay * carried + got_ref[device, :, 0:wide]
    if not first:
        lane = lax.broadcasted_iota(jnp.int32, (1, LANE), 1)
        low = jnp.where(lane < LANE // 2, tail, 0.0)
        high = jnp.where(lane < LANE // 2, 0.0, tail)
        sums_ref[0] = spread(jnp.sum(low, axis=1, keepdims=True))
        sums_ref[1] = spread(jnp.sum(high, axis=1, keepdims=True))


def total_sum(sums, index):
    return sum(ref[index] for ref in sums)


def enter(s, arrive_ref, e_ref, block, rates, around):
    arrive = read_state(s, arrive_ref, block)
    return [
        e_ref[block, n] + jnp.exp2(around * rates[n]) * arrive[n]
        for n in range(s.entries)
    ]


def forward_kernel(s, offset, first, *refs):
    refs = list(refs)
    rhs_ref, curv_ref, rate_ref, skip_ref, damp_ref = refs[:5]
    decay_ref, drive_ref, cx_ref, total_ref, e_in, arrive_ref = refs[5:11]
    refs = refs[11:]
    if not first:
        r_ref, y0_ref = refs[:2]
        sums_b, sums_c = refs[2 : 2 + STREAMS], refs[2 + STREAMS : 2 + 2 * STREAMS]
        refs = refs[2 + 2 * STREAMS :]
        ratio = total_sum(sums_c, 0) / total_sum(sums_b, 0)
    e_out, out_ref, w_ref, y_ref = refs

    def body(block, carry):
        squares, inner = carry
        rates = load_rates(s, rate_ref, block + offset)
        total = total_ref[block]
        skip = spread(skip_ref[0:1, cols(block + offset)])
        damp = spread(damp_ref[0:1, cols(block + offset)])
        before = total_around(total, False)
        state = enter(s, arrive_ref, e_in, block, rates, before)
        for j in range(s.steps):
            rows = pl.ds(j, SUB, stride=s.steps)
            rhs = rhs_ref[block, rows, :]
            v = rhs if first else r_ref[block, j]
            parts = [skip * v]
            for n in range(s.entries):
                state[n] = (
                    decay_ref[block, j, n] * state[n] + drive_ref[block, j, n] * v
                )
                parts.append(cx_ref[j, n] * state[n])
            y = summed(parts)
            if first:
                y_ref[block, j] = y
                squares = squares + v * v
                along = v
            else:
                y = y + ratio * y0_ref[block, j]
                along = v + ratio * rhs
                y_ref[block, j] = along
            w = curv_ref[block, rows, :] * y
            w_ref[block, j] = w
            inner = inner + (w * y + damp * (along * along))

        passed = zeros(s.entries)
        for j in reversed(range(s.steps)):
            w = w_ref[block, j]
            for n in range(s.entries):
                passed[n] = decay_ref[block, j, n] * (cx_ref[j, n] * w + passed[n])
        finish_summary(s, block, passed, rates, total, e_out, out_ref, True)
        return squares, inner

    squares, inner = lax.fori_loop(0, s.blocks, body, tuple(zeros(2)))
    put_sums(s, out_ref, squares, inner)


def backward_block(s, block, w_ref, skip, decay_ref, drive_ref, cx_ref, passed, use):
    for j in reversed(range(s.steps)):
        w = w_ref[block, j]
        parts = [skip * w]
        for n in range(s.entries):
            costate = cx_ref[j, n] * w + passed[n]
            passed[n] = decay_ref[block, j, n] * costate
            parts.append(drive_ref[block, j, n] * costate)
        use(j, summed(parts))


def backward_kernel(s, offset, *refs):
    rhs_ref, rate_ref, skip_ref, damp_ref = refs[:4]
    decay_ref, drive_ref, cx_ref, total_ref, e_in, arrive_ref, w_ref = refs[4:11]
    sums_b = refs[11 : 11 + STREAMS]
    e_out, out_ref, r_ref = refs[11 + STREAMS :]
    step = total_sum(sums_b, 0) / total_sum(sums_b, 1)

    def body(block, squares):
        rates = load_rates(s, rate_ref, block + offset)
        total = total_ref[block]
        skip = spread(skip_ref[0:1, cols(block + offset)])
        damp = spread(damp_ref[0:1, cols(block + offset)])
        after = total_around(total, True)
        passed = enter(s, arrive_ref, e_in, block, rates, after)
        acc = [squares]

        def use(j, product):
            v = rhs_ref[block, pl.ds(j, SUB, stride=s.steps), :]
            r = v - step * (product + damp * v)
            r_ref[block, j] = r
            acc[0] = acc[0] + r * r

        backward_block(
            s, block, w_ref, skip, decay_ref, drive_ref, cx_ref, passed, use
        )
        state = zeros(s.entries)
        for j in range(s.steps):
            v = r_ref[block, j]
            for n in range(s.entries):
                state[n] = (
                    decay_ref[block, j, n] * state[n] + drive_ref[block, j, n] * v
                )
        finish_summary(s, block, state, rates, total, e_out, out_ref, False)
        return acc[0]

    squares = lax.fori_loop(0, s.blocks, body, zeros(1)[0])
    put_sums(s, out_ref, squares, zeros(1)[0])


def last_kernel(s, offset, *refs):
    rhs_ref, rate_ref, skip_ref, damp_ref = refs[:4]
    decay_ref, drive_ref, cx_ref, total_ref, e_in, arrive_ref, w_ref = refs[4:11]
    r_ref, d_ref = refs[11:13]
    refs = refs[13:]
    sums_b, sums_c = refs[:STREAMS], refs[STREAMS : 2 * STREAMS]
    sums_d = refs[2 * STREAMS : 3 * STREAMS]
    refs = refs[3 * STREAMS :]
    if offset:
        refs = refs[2:]
    solution_ref, residual_ref, tile_s, tile_r, sem_s, sem_r = refs
    before_step = total_sum(sums_b, 0) / total_sum(sums_b, 1)
    step = total_sum(sums_c, 0) / total_sum(sums_d, 1)

    def copies(block):
        where = cols(block + offset)
        return (
            pltpu.make_async_copy(
                tile_s.at[block], solution_ref.at[:, where], sem_s.at[block]
            ),
            pltpu.make_async_copy(
                tile_r.at[block], residual_ref.at[:, where], sem_r.at[block]
            ),
        )

    def body(block, carry):
        rates = load_rates(s, rate_ref, block + offset)
        skip = spread(skip_ref[0:1, cols(block + offset)])
        damp = spread(damp_ref[0:1, cols(block + offset)])
        after = total_around(total_ref[block], True)
        passed = enter(s, arrive_ref, e_in, block, rates, after)

        def use(j, product):
            rows = pl.ds(j, SUB, stride=s.steps)
            along = d_ref[block, j]
            tile_s[block, rows, :] = (
                before_step * rhs_ref[block, rows, :] + step * along
            )
            tile_r[block, rows, :] = r_ref[block, j] - step * (product + damp * along)

        backward_block(
            s, block, w_ref, skip, decay_ref, drive_ref, cx_ref, passed, use
        )
        for copy in copies(block):
            copy.start()
        return carry

    lax.fori_loop(0, s.blocks, body, 0)

    def finish(block, carry):
        for copy in copies(block):
            copy.wait()
        return carry

    lax.fori_loop(0, s.blocks, finish, 0)


VM = pl.BlockSpec(memory_space=pltpu.VMEM)
HBM = pl.BlockSpec(memory_space=pltpu.HBM)
LIMIT = 4 * 1024 * 1024


def in_hbm(x):
    return pltpu.with_memory_space_constraint(x, pltpu.HBM)


def call(body, name, outs, scratch, args, passes, n_hbm=0, out_specs=None, aliases=()):
    work = passes * 16 * 128 * 2048 // STREAMS
    return pl.pallas_call(
        body,
        name=name,
        out_shape=outs,
        in_specs=[HBM] * n_hbm + [VM] * (len(args) - n_hbm),
        out_specs=out_specs or [VM] * len(outs),
        scratch_shapes=scratch,
        input_output_aliases=dict(aliases),
        cost_estimate=pl.CostEstimate(
            flops=work, bytes_accessed=work, transcendentals=0
        ),
        compiler_params=pltpu.CompilerParams(vmem_limit_bytes=LIMIT),
    )(*args)


def per_device(devices, rhs, rate, delta, b_proj, c_proj, skip, curvature, damping):
    tokens, columns = rhs.shape
    entries = rate.shape[0]
    s = Sizes(tokens, columns, entries, devices, STREAMS)
    held = pltpu.VMEM
    dma = pltpu.SemaphoreType.DMA
    every = range(STREAMS)
    per_token = held((s.blocks, s.steps, SUB, LANE), F32)
    expanded = (s.steps, entries, SUB, LANE)
    edge = held((s.blocks, entries, SUB, LANE), F32)
    whole_state = held((s.blocks, s.steps, entries, SUB, LANE), F32)
    tile = (s.blocks, tokens, LANE)
    packet = held((devices, 1, (s.rows + 1) * LANE), F32)
    linked = held((devices, 1, s.rows * LANE), F32)
    sums = held((2, SUB, LANE), F32)

    def exchange(send):
        return lax.all_to_all(send, "seq", 0, 0)

    def kernel(body, *more):
        return functools.partial(body, s, *more)

    offsets = [s.blocks * g for g in every]
    firsts = [
        call(
            kernel(first_kernel, offsets[g]),
            f"first_{g}",
            [
                whole_state, whole_state, held(expanded, F32),
                held((s.blocks, SUB, LANE), F32), edge, packet,
                held(tile, F32), held(tile, F32), held((entries, columns), F32),
                held((1, columns), F32), held((1, columns), F32), linked,
            ],
            [
                pltpu.VMEM(tile, F32), pltpu.VMEM(expanded, F32),
                pltpu.VMEM((2, entries, tokens), F32),
                pltpu.VMEM((2, tokens, entries), F32),
                dma((s.blocks,)), dma((s.blocks,)), dma((s.blocks,)), dma((5,)),
            ],
            [
                in_hbm(x)
                for x in (
                    rhs, delta, curvature, rate, skip[None], damping[None],
                    b_proj.T, c_proj.T,
                )
            ],
            2,
            n_hbm=8,
        )
        for g in every
    ]
    decay, drive, cx, total, e, send, rhs_v, curv, rates, skips, damps, link_rate = zip(
        *firsts
    )

    def link(g, got, backward, letter, decays=None):
        first = decays is None
        return call(
            kernel(link_kernel, backward, first),
            f"link_{letter}_{g}",
            [linked, linked if first else sums],
            [],
            (got, link_rate[g] if first else decays),
            1,
        )

    def around(send, backward, letter, decays):
        got = [exchange(send[g]) for g in every]
        pairs = [link(g, got[g], backward, letter, decays and decays[g]) for g in every]
        return [exchange(pairs[g][0]) for g in every], [pairs[g][1] for g in every]

    def common(g, e, arrive):
        return (decay[g], drive[g], cx[g], total[g], e[g], arrive[g])

    def consts(g):
        return (rates[g], skips[g], damps[g])

    arrive, decays = around(send, False, "a", None)
    e, send, w, y0 = zip(
        *[
            call(
                kernel(forward_kernel, offsets[g], True),
                f"forward_a_{g}",
                [edge, packet, per_token, per_token],
                [],
                (rhs_v[g], curv[g], *consts(g), *common(g, e, arrive)),
                2,
            )
            for g in every
        ]
    )
    arrive, sums_b = around(send, True, "b", decays)
    e, send, r = zip(
        *[
            call(
                kernel(backward_kernel, offsets[g]),
                f"backward_a_{g}",
                [edge, packet, per_token],
                [],
                (rhs_v[g], *consts(g), *common(g, e, arrive), w[g], *sums_b),
                2,
            )
            for g in every
        ]
    )
    arrive, sums_c = around(send, False, "c", decays)
    e, send, w, d = zip(
        *[
            call(
                kernel(forward_kernel, offsets[g], False),
                f"forward_b_{g}",
                [edge, packet, per_token, per_token],
                [],
                (
                    rhs_v[g], curv[g], *consts(g), *common(g, e, arrive),
                    r[g], y0[g], *sums_b, *sums_c,
                ),
                2,
            )
            for g in every
        ]
    )
    arrive, sums_d = around(send, True, "d", decays)
    outs = ()
    for g in every:
        args = (
            rhs_v[g], *consts(g), *common(g, e, arrive), w[g], r[g], d[g],
            *sums_b, *sums_c, *sums_d,
        )
        outs = pl.pallas_call(
            kernel(last_kernel, offsets[g]),
            name=f"backward_b_{g}",
            out_shape=[jax.ShapeDtypeStruct((tokens, columns), F32)] * 2,
            in_specs=[VM] * len(args) + [HBM] * len(outs),
            out_specs=[HBM] * 2,
            scratch_shapes=[
                pltpu.VMEM(tile, F32), pltpu.VMEM(tile, F32),
                dma((s.blocks,)), dma((s.blocks,)),
            ],
            input_output_aliases={len(args): 0, len(args) + 1: 1} if outs else {},
            compiler_params=pltpu.CompilerParams(vmem_limit_bytes=LIMIT),
        )(*args, *outs)
    return tuple(outs)


def solution(mesh):
    placed = (
        P("seq", None),
        P(),
        P("seq", None),
        P("seq", None),
        P("seq", None),
        P(),
        P("seq", None),
        P(),
    )
    return jax.shard_map(
        functools.partial(per_device, mesh.shape["seq"]),
        mesh=mesh,
        in_specs=placed,
        out_specs=(P("seq", None), P("seq", None)),
        check_vma=False,
    )
```

time: 146 us -> 123 us (0.84)
  blocking collectives: 96.3 us -> 86.5 us
  local copies, waits for them, and re-layouts: 8.8 us -> 0 us
  Pallas kernels: 39.9 us -> 35.9 us
    all_to_all x8, blocking collectives: 96.3 us -> 86.5 us  [exchange(): return lax.all_to_all(send, 'seq', 0, 0)]
    unnamed x22 -> x0, local copies, waits for them, and re-layouts: 8.8 us -> none
    pallas_call x9, Pallas kernels: 39.9 us -> 35.9 us  [the longest x8 31.3 us: call(): pl.pallas_call(body, name=name, out_shape=outs, in_specs=[HBM] * n_hbm +...]
where the time goes in v2:
time: 123 us
  blocking collectives  86.5 us (70%)
  Pallas kernels  35.9 us (29%)
    all_to_all x8, blocking collectives, exchange(): return lax.all_to_all(send, 'seq', 0, 0)  86.5 us
    pallas_call x8, Pallas kernels, call(): pl.pallas_call(body, name=name, out_shape=outs, in_specs=[HBM] * n_hbm +...  31.3 us
    pallas_call x1, Pallas kernels, per_device(): pl.pallas_call(kernel(last_kernel, offsets[g]), name=f'backward_b_{g}', o...  4.66 us

profile of v2, /device:TPU:0, one launch (start us, length us, event | category | flops | bytes accessed | tf_op | source)
XLA Modules:
  0.0 123.1 jit_solution(4288881217306474592)
XLA Ops:
  0.6 12.6 %first_0.1 = (f32[16,16,16,8,128]{4,3,2,1,0:T(8,128)S(1)}, f32[16,16,16,8,128]{4,3,2,1,0:T(8,128)S(1)}, f32[16,16,8,128]{3,2,1,0:T(8,128)S(1)}, f32[16,8,128]{2,...) custom-call(f32[128,2048]{1,0:T(8,128)} %refs_0_.1, ...), custom_call_target="tpu_custom_call" | custom-call | flops 8388608 | bytes 8388608 | tf_op jit(solution)/shard_map/first_0/pallas_call | solution.py:423
  13.3 15.5 %all_to_all.40.refs_0_ = f32[32,1,1152]{2,1,0:T(1,128)S(1)} all-to-all(f32[32,1,1152]{2,1,0:T(1,128)S(1)} %get-tuple-element.43), channel_id=1, replica_groups=mesh['seq'=32] {'seq'}, dimensions={0} | all-to-all | bytes 294912 | tf_op jit(solution)/shard_map/all_to_all | solution.py:455
  28.8 0.3 link_a_0.1
  29.1 10.1 %all_to_all.41.refs_10_ = f32[32,1,1024]{2,1,0:T(1,128)S(1)} all-to-all(f32[32,1,1024]{2,1,0:T(1,128)S(1)} %get-tuple-element.45), channel_id=1, replica_groups=mesh['seq'=32] {'seq'}, dimensions={0} | all-to-all | bytes 262144 | tf_op jit(solution)/shard_map/all_to_all | solution.py:455
  39.2 6.0 %forward_a_0.1 = (f32[16,16,8,128]{3,2,1,0:T(8,128)S(1)}, f32[32,1,1152]{2,1,0:T(1,128)S(1)}, f32[16,16,8,128]{3,2,1,0:T(8,128)S(1)}, f32[16,16,8,128]{3,2,1,0:T(8,128)S(1)}) custom-call(f32[16,128,128]{2,1,0:T(8,128)S(1)} %get-tuple-element.33.refs_0_, f32[16,128,128]{2,1,0:T(8,128)S(1)} %get-tuple-element.41.refs_1_, ...), custom_call_target="tpu_custom_call" | custom-call | flops 8388608 | bytes 8388608 | tf_op jit(solution)/shard_map/forward_a_0/pallas_call | solution.py:423
  45.2 10.2 %all_to_all.42.refs_0_ = f32[32,1,1152]{2,1,0:T(1,128)S(1)} all-to-all(f32[32,1,1152]{2,1,0:T(1,128)S(1)} %get-tuple-element.47), channel_id=1, replica_groups=mesh['seq'=32] {'seq'}, dimensions={0} | all-to-all | bytes 294912 | tf_op jit(solution)/shard_map/all_to_all | solution.py:455
  55.4 0.1 link_b_0.1
  55.5 10.1 %all_to_all.43.refs_9_ = f32[32,1,1024]{2,1,0:T(1,128)S(1)} all-to-all(f32[32,1,1024]{2,1,0:T(1,128)S(1)} %get-tuple-element.49), channel_id=1, replica_groups=mesh['seq'=32] {'seq'}, dimensions={0} | all-to-all | bytes 262144 | tf_op jit(solution)/shard_map/all_to_all | solution.py:455
  65.6 6.0 %backward_a_0.1 = (f32[16,16,8,128]{3,2,1,0:T(8,128)S(1)}, f32[32,1,1152]{2,1,0:T(1,128)S(1)}, f32[16,16,8,128]{3,2,1,0:T(8,128)S(1)}) custom-call(f32[16,128,128]{2,1,0:T(8,128)S(1)} %get-tuple-element.33.refs_0_, f32[16,2048]{1,0:T(8,128)S(1)} %get-tuple-element.34.refs_2_.refs_1_, f32[1,2048]{1,0:T(1,128)S(1)} %get-tuple-element.35.refs_3_.refs_2_, ...), custom_call_target="tpu_custom_call" | custom-call | flops 8388608 | bytes 8388608 | tf_op jit(solution)/shard_map/backward_a_0/pallas_call | solution.py:423
  71.6 10.2 %all_to_all.44.refs_0_ = f32[32,1,1152]{2,1,0:T(1,128)S(1)} all-to-all(f32[32,1,1152]{2,1,0:T(1,128)S(1)} %get-tuple-element.53), channel_id=1, replica_groups=mesh['seq'=32] {'seq'}, dimensions={0} | all-to-all | bytes 294912 | tf_op jit(solution)/shard_map/all_to_all | solution.py:455
  81.7 0.1 link_c_0.1
  81.9 10.1 %all_to_all.45.refs_10_ = f32[32,1,1024]{2,1,0:T(1,128)S(1)} all-to-all(f32[32,1,1024]{2,1,0:T(1,128)S(1)} %get-tuple-element.54), channel_id=1, replica_groups=mesh['seq'=32] {'seq'}, dimensions={0} | all-to-all | bytes 262144 | tf_op jit(solution)/shard_map/all_to_all | solution.py:455
  92.0 6.1 %forward_b_0.1 = (f32[16,16,8,128]{3,2,1,0:T(8,128)S(1)}, f32[32,1,1152]{2,1,0:T(1,128)S(1)}, f32[16,16,8,128]{3,2,1,0:T(8,128)S(1)}, f32[16,16,8,128]{3,2,1,0:T(8,128)S(1)}) custom-call(f32[16,128,128]{2,1,0:T(8,128)S(1)} %get-tuple-element.33.refs_0_, f32[16,128,128]{2,1,0:T(8,128)S(1)} %get-tuple-element.41.refs_1_, ...), custom_call_target="tpu_custom_call" | custom-call | flops 8388608 | bytes 8388608 | tf_op jit(solution)/shard_map/forward_b_0/pallas_call | solution.py:423
  98.1 10.2 %all_to_all.46.refs_0_ = f32[32,1,1152]{2,1,0:T(1,128)S(1)} all-to-all(f32[32,1,1152]{2,1,0:T(1,128)S(1)} %get-tuple-element.59), channel_id=1, replica_groups=mesh['seq'=32] {'seq'}, dimensions={0} | all-to-all | bytes 294912 | tf_op jit(solution)/shard_map/all_to_all | solution.py:455
  108.2 0.1 link_d_0.1
  108.3 10.1 %all_to_all.47.refs_9_ = f32[32,1,1024]{2,1,0:T(1,128)S(1)} all-to-all(f32[32,1,1024]{2,1,0:T(1,128)S(1)} %get-tuple-element.60), channel_id=1, replica_groups=mesh['seq'=32] {'seq'}, dimensions={0} | all-to-all | bytes 262144 | tf_op jit(solution)/shard_map/all_to_all | solution.py:455
  118.5 4.7 %backward_b_0.1 = (f32[128,2048]{1,0:T(8,128)}, f32[128,2048]{1,0:T(8,128)}) custom-call(f32[16,128,128]{2,1,0:T(8,128)S(1)} %get-tuple-element.33.refs_0_, f32[16,2048]{1,0:T(8,128)S(1)} %get-tuple-element.34.refs_2_.refs_1_, f32[1,2048]{1,0:T(1,128)S(1)} %get-tuple-element.35.refs_3_.refs_2_, f32[1,2048]{1,0:T(1,128)S(1)} %get-tuple-element.36.refs_4_.refs_3_, ...), custom_call_target="tpu_custom_call" | custom-call | tf_op jit(solution)/shard_map/backward_b_0/pallas_call | solution.py:567

commit v3 on v2

--- a/solution.py
+++ b/solution.py
@@ -10,9 +10,7 @@
 STREAMS = 1
 SUB, LANE = 8, 128
 LOG2E = 1.4426950408889634
-LN2 = 0.6931471805599453
-SMALL = 0.03
-G1, G2, G3 = -LN2, -LN2 * LN2 / 2.0, -LN2 * LN2 * LN2 / 6.0
+HALF = -0.5 * 0.6931471805599453
 F32 = jnp.float32
 
 
@@ -164,14 +162,13 @@
             for n in range(s.entries):
                 z = d * rates[n]
                 decay = jnp.exp2(z)
-                near = z * (G1 + z * (G2 + z * G3))
-                drive = jnp.where(z > -SMALL, near, 1.0 - decay) * bx_ref[j, n]
+                drive = jnp.tanh(z * HALF) * (bx_ref[j, n] * (1.0 + decay))
                 decay_ref[block, j, n] = decay
                 drive_ref[block, j, n] = drive
                 state[n] = decay * state[n] + drive * v
             return (total, *state)
 
-        result = lax.fori_loop(0, s.steps, advance, tuple(zeros(s.entries + 1)), unroll=8)
+        result = lax.fori_loop(0, s.steps, advance, tuple(zeros(s.entries + 1)), unroll=16)
         total, state = result[0], result[1:]
         total_ref[block] = total
         finish_summary(s, block, state, rates, total, e_ref, out_ref, False)

time: 123 us -> 121 us (0.984)
  Pallas kernels: 35.9 us -> 33.6 us
    pallas_call x8, Pallas kernels: 31.3 us -> 29 us  [call(): pl.pallas_call(body, name=name, out_shape=outs, in_specs=[HBM] * n_hbm +...]
where the time goes in v3:
time: 121 us
  blocking collectives  86.5 us (71%)
  Pallas kernels  33.6 us (28%)
    all_to_all x8, blocking collectives, exchange(): return lax.all_to_all(send, 'seq', 0, 0)  86.5 us
    pallas_call x8, Pallas kernels, call(): pl.pallas_call(body, name=name, out_shape=outs, in_specs=[HBM] * n_hbm +...  29 us
    pallas_call x1, Pallas kernels, per_device(): pl.pallas_call(kernel(last_kernel, offsets[g]), name=f'backward_b_{g}', o...  4.66 us

profile of v3, /device:TPU:0, one launch (start us, length us, event | category | flops | bytes accessed | tf_op | source)
XLA Modules:
  0.0 120.8 jit_solution(781658380153195988)
XLA Ops:
  0.6 10.3 %first_0.1 = (f32[16,16,16,8,128]{4,3,2,1,0:T(8,128)S(1)}, f32[16,16,16,8,128]{4,3,2,1,0:T(8,128)S(1)}, f32[16,16,8,128]{3,2,1,0:T(8,128)S(1)}, f32[16,8,128]{2,...) custom-call(f32[128,2048]{1,0:T(8,128)} %refs_0_.1, ...), custom_call_target="tpu_custom_call" | custom-call | flops 8388608 | bytes 8388608 | tf_op jit(solution)/shard_map/first_0/pallas_call | solution.py:420
  10.9 15.5 %all_to_all.40.refs_0_ = f32[32,1,1152]{2,1,0:T(1,128)S(1)} all-to-all(f32[32,1,1152]{2,1,0:T(1,128)S(1)} %get-tuple-element.43), channel_id=1, replica_groups=mesh['seq'=32] {'seq'}, dimensions={0} | all-to-all | bytes 294912 | tf_op jit(solution)/shard_map/all_to_all | solution.py:452
  26.5 0.3 link_a_0.1
  26.7 10.1 %all_to_all.41.refs_10_ = f32[32,1,1024]{2,1,0:T(1,128)S(1)} all-to-all(f32[32,1,1024]{2,1,0:T(1,128)S(1)} %get-tuple-element.45), channel_id=1, replica_groups=mesh['seq'=32] {'seq'}, dimensions={0} | all-to-all | bytes 262144 | tf_op jit(solution)/shard_map/all_to_all | solution.py:452
  36.9 6.0 %forward_a_0.1 = (f32[16,16,8,128]{3,2,1,0:T(8,128)S(1)}, f32[32,1,1152]{2,1,0:T(1,128)S(1)}, f32[16,16,8,128]{3,2,1,0:T(8,128)S(1)}, f32[16,16,8,128]{3,2,1,0:T(8,128)S(1)}) custom-call(f32[16,128,128]{2,1,0:T(8,128)S(1)} %get-tuple-element.33.refs_0_, f32[16,128,128]{2,1,0:T(8,128)S(1)} %get-tuple-element.41.refs_1_, ...), custom_call_target="tpu_custom_call" | custom-call | flops 8388608 | bytes 8388608 | tf_op jit(solution)/shard_map/forward_a_0/pallas_call | solution.py:420
  42.9 10.2 %all_to_all.42.refs_0_ = f32[32,1,1152]{2,1,0:T(1,128)S(1)} all-to-all(f32[32,1,1152]{2,1,0:T(1,128)S(1)} %get-tuple-element.47), channel_id=1, replica_groups=mesh['seq'=32] {'seq'}, dimensions={0} | all-to-all | bytes 294912 | tf_op jit(solution)/shard_map/all_to_all | solution.py:452
  53.1 0.1 link_b_0.1
  53.2 10.1 %all_to_all.43.refs_9_ = f32[32,1,1024]{2,1,0:T(1,128)S(1)} all-to-all(f32[32,1,1024]{2,1,0:T(1,128)S(1)} %get-tuple-element.49), channel_id=1, replica_groups=mesh['seq'=32] {'seq'}, dimensions={0} | all-to-all | bytes 262144 | tf_op jit(solution)/shard_map/all_to_all | solution.py:452
  63.3 6.0 %backward_a_0.1 = (f32[16,16,8,128]{3,2,1,0:T(8,128)S(1)}, f32[32,1,1152]{2,1,0:T(1,128)S(1)}, f32[16,16,8,128]{3,2,1,0:T(8,128)S(1)}) custom-call(f32[16,128,128]{2,1,0:T(8,128)S(1)} %get-tuple-element.33.refs_0_, f32[16,2048]{1,0:T(8,128)S(1)} %get-tuple-element.34.refs_2_.refs_1_, f32[1,2048]{1,0:T(1,128)S(1)} %get-tuple-element.35.refs_3_.refs_2_, ...), custom_call_target="tpu_custom_call" | custom-call | flops 8388608 | bytes 8388608 | tf_op jit(solution)/shard_map/backward_a_0/pallas_call | solution.py:420
  69.3 10.2 %all_to_all.44.refs_0_ = f32[32,1,1152]{2,1,0:T(1,128)S(1)} all-to-all(f32[32,1,1152]{2,1,0:T(1,128)S(1)} %get-tuple-element.53), channel_id=1, replica_groups=mesh['seq'=32] {'seq'}, dimensions={0} | all-to-all | bytes 294912 | tf_op jit(solution)/shard_map/all_to_all | solution.py:452
  79.4 0.1 link_c_0.1
  79.5 10.1 %all_to_all.45.refs_10_ = f32[32,1,1024]{2,1,0:T(1,128)S(1)} all-to-all(f32[32,1,1024]{2,1,0:T(1,128)S(1)} %get-tuple-element.54), channel_id=1, replica_groups=mesh['seq'=32] {'seq'}, dimensions={0} | all-to-all | bytes 262144 | tf_op jit(solution)/shard_map/all_to_all | solution.py:452
  89.6 6.1 %forward_b_0.1 = (f32[16,16,8,128]{3,2,1,0:T(8,128)S(1)}, f32[32,1,1152]{2,1,0:T(1,128)S(1)}, f32[16,16,8,128]{3,2,1,0:T(8,128)S(1)}, f32[16,16,8,128]{3,2,1,0:T(8,128)S(1)}) custom-call(f32[16,128,128]{2,1,0:T(8,128)S(1)} %get-tuple-element.33.refs_0_, f32[16,128,128]{2,1,0:T(8,128)S(1)} %get-tuple-element.41.refs_1_, ...), custom_call_target="tpu_custom_call" | custom-call | flops 8388608 | bytes 8388608 | tf_op jit(solution)/shard_map/forward_b_0/pallas_call | solution.py:420
  95.7 10.2 %all_to_all.46.refs_0_ = f32[32,1,1152]{2,1,0:T(1,128)S(1)} all-to-all(f32[32,1,1152]{2,1,0:T(1,128)S(1)} %get-tuple-element.59), channel_id=1, replica_groups=mesh['seq'=32] {'seq'}, dimensions={0} | all-to-all | bytes 294912 | tf_op jit(solution)/shard_map/all_to_all | solution.py:452
  105.9 0.1 link_d_0.1
  106.0 10.1 %all_to_all.47.refs_9_ = f32[32,1,1024]{2,1,0:T(1,128)S(1)} all-to-all(f32[32,1,1024]{2,1,0:T(1,128)S(1)} %get-tuple-element.60), channel_id=1, replica_groups=mesh['seq'=32] {'seq'}, dimensions={0} | all-to-all | bytes 262144 | tf_op jit(solution)/shard_map/all_to_all | solution.py:452
  116.1 4.7 %backward_b_0.1 = (f32[128,2048]{1,0:T(8,128)}, f32[128,2048]{1,0:T(8,128)}) custom-call(f32[16,128,128]{2,1,0:T(8,128)S(1)} %get-tuple-element.33.refs_0_, f32[16,2048]{1,0:T(8,128)S(1)} %get-tuple-element.34.refs_2_.refs_1_, f32[1,2048]{1,0:T(1,128)S(1)} %get-tuple-element.35.refs_3_.refs_2_, f32[1,2048]{1,0:T(1,128)S(1)} %get-tuple-element.36.refs_4_.refs_3_, ...), custom_call_target="tpu_custom_call" | custom-call | tf_op jit(solution)/shard_map/backward_b_0/pallas_call | solution.py:564

commit v4 on v3

--- a/solution.py
+++ b/solution.py
@@ -62,28 +62,57 @@
         self.tokens, self.entries, self.devices = tokens, entries, devices
         self.steps = tokens // SUB
         self.blocks = columns // LANE // streams
-        self.rows = entries * self.blocks // devices
-        self.per = entries // self.rows
+        self.half = self.blocks // 2
+        self.levels = []
+        stride = 2
+        while stride < devices:
+            radix = 4 if devices // stride % 4 == 0 else 2
+            self.levels.append((stride, radix))
+            stride *= radix
 
 
 def cols(block):
     return pl.ds(pl.multiple_of(block * LANE, LANE), LANE)
 
 
-def lane_row(row):
-    return pl.ds(row * LANE, LANE)
-
-
-def write_state(s, ref, block, rows_of):
+def my_core():
+    return lax.axis_index("seq") & 1
+
+
+def place_of(s, block):
+    upper = (block >= s.half).astype(jnp.int32)
+    return upper ^ my_core(), block - upper * s.half
+
+
+def write_state(s, both_ref, block, rows_of):
+    slot, place = place_of(s, block)
     for n, value in enumerate(rows_of):
-        ref[block * s.per + n // s.rows, 0:1, lane_row(n % s.rows)] = value
-
-
-def read_state(s, ref, block):
-    return [
-        spread(ref[block * s.per + n // s.rows, 0:1, lane_row(n % s.rows)])
-        for n in range(s.entries)
-    ]
+        both_ref[slot, place, n : n + 1, :] = value
+
+
+def over_blocks(s, scans, body, carry):
+    for upper, scan in enumerate(scans):
+
+        def one(place, carry, upper=upper, scan=scan):
+            return body(upper * s.half + place, scan, place, carry)
+
+        carry = lax.fori_loop(0, s.half, one, carry)
+    return carry
+
+
+def part_packets(both_ref, keep_ref, give_ref):
+    keep_ref[...] = both_ref[0]
+    give_ref[...] = both_ref[1]
+
+
+def gather_state(s, arrive, arrive_ref):
+    own_ref, got_ref = arrive
+    for slot, ref in ((my_core(), own_ref), (1 - my_core(), got_ref)):
+        arrive_ref[pl.ds(slot * s.half, s.half)] = ref[...]
+
+
+def read_state(s, arrive_ref, block):
+    return [spread(arrive_ref[block, n : n + 1, :]) for n in range(s.entries)]
 
 
 def load_rates(s, rate_ref, block):
@@ -106,10 +135,12 @@
 def first_kernel(s, offset, *refs):
     rhs_hbm, delta_hbm, curv_hbm, rate_hbm, skip_hbm, damp_hbm, bt_hbm, ct_hbm = refs[:8]
     (
-        decay_ref, drive_ref, cx_ref, total_ref, e_ref, out_ref,
-        rhs_ref, curv_ref, rate_ref, skip_ref, damp_ref, link_rate_ref,
+        low_scan, high_scan, cx_ref, total_ref, e_ref, keep_ref, give_ref,
+        rhs_ref, curv_ref, rate_ref, skip_ref, damp_ref,
     ) = refs[8:20]
-    delta_ref, bx_ref, wide_ref, turn_ref, sem_d, sem_v, sem_c, sem_s = refs[20:]
+    delta_ref, bx_ref, wide_ref, turn_ref, sem_d, sem_v, sem_c, sem_s, put = refs[20:]
+    for slot in (0, 1):
+        put[slot, s.half] = jnp.zeros((s.entries, LANE), F32)
 
     small = [
         pltpu.make_async_copy(src, dst, sem_s.at[i])
@@ -146,11 +177,10 @@
     small[2].wait()
     rate_ref[...] = rate_ref[...] * (-LOG2E)
 
-    def body(block, carry):
+    def body(block, scan, place, carry):
         block_copy(delta_hbm, delta_ref, sem_d, block).wait()
         block_copy(rhs_hbm, rhs_ref, sem_v, block).wait()
         own = [rate_ref[n : n + 1, cols(block + offset)] for n in range(s.entries)]
-        write_state(s, link_rate_ref, block, own)
         rates = [spread(row) for row in own]
 
         def advance(j, state):
@@ -163,21 +193,22 @@
                 z = d * rates[n]
                 decay = jnp.exp2(z)
                 drive = jnp.tanh(z * HALF) * (bx_ref[j, n] * (1.0 + decay))
-                decay_ref[block, j, n] = decay
-                drive_ref[block, j, n] = drive
+                scan[place, j, n, 0] = decay
+                scan[place, j, n, 1] = drive
                 state[n] = decay * state[n] + drive * v
             return (total, *state)
 
         result = lax.fori_loop(0, s.steps, advance, tuple(zeros(s.entries + 1)), unroll=16)
         total, state = result[0], result[1:]
         total_ref[block] = total
-        finish_summary(s, block, state, rates, total, e_ref, out_ref, False)
+        finish_summary(s, block, state, rates, total, e_ref, put, False)
         whole = jnp.sum(total, axis=0, keepdims=True)
-        for piece in range(s.per):
-            out_ref[block * s.per + piece, 0:1, lane_row(s.rows)] = whole
+        slot, row = place_of(s, block)
+        put[slot, s.half, pl.ds(row, 1), :] = whole
         return carry
 
-    lax.fori_loop(0, s.blocks, body, 0)
+    over_blocks(s, (low_scan, high_scan), body, 0)
+    part_packets(put, keep_ref, give_ref)
     small[3].wait()
     small[4].wait()
 
@@ -188,48 +219,127 @@
     lax.fori_loop(0, s.blocks, finish, 0)
 
 
-def put_sums(s, out_ref, first, second):
+def put_sums(s, put, keep_ref, give_ref, first, second):
     first = jnp.sum(first, axis=0, keepdims=True)
     second = jnp.sum(second, axis=0, keepdims=True)
-    half = LANE // 2
-    first = first + pltpu.roll(first, half, 1)
-    second = second + pltpu.roll(second, half, 1)
-    lane = lax.broadcasted_iota(jnp.int32, (1, LANE), 1)
-    both = jnp.where(lane < half, first, second)
-
-    def body(device, carry):
-        out_ref[device, 0:1, lane_row(s.rows)] = both
-        return carry
-
-    lax.fori_loop(0, s.devices, body, 0, unroll=8)
-
-
-def link_kernel(s, backward, first, *refs):
+    for slot in (0, 1):
+        put[slot, s.half] = jnp.zeros((s.entries, LANE), F32)
+        put[slot, s.half, 0:1, :] = first
+        put[slot, s.half, 1:2, :] = second
+    part_packets(put, keep_ref, give_ref)
+
+
+def half_rates(s, rate_ref, block):
+    return rate_ref[:, cols(my_core() * s.half + block)]
+
+
+def join_kernel(s, backward, first, *refs):
     if first:
-        got_ref, link_rate_ref, arrive_ref, decay_ref = refs
-        rates = link_rate_ref[lax.axis_index("seq")]
+        keep_ref, got_ref, rate_ref, chip_ref, core_ref = refs
     else:
-        got_ref, decay_ref, arrive_ref, sums_ref = refs
-    wide = s.rows * LANE
-    carried = jnp.zeros((1, wide), F32)
-    tail = jnp.zeros((1, LANE), F32)
-    order = range(s.devices)
-    for device in reversed(order) if backward else order:
-        extra = got_ref[device, :, lane_row(s.rows)]
+        keep_ref, got_ref, core_ref, chip_ref = refs
+    low = my_core() == 0
+    for block in range(s.half):
+        keep, got = keep_ref[block], got_ref[block]
         if first:
-            decay = jnp.exp2(jnp.concatenate([extra] * s.rows, axis=1) * rates)
-            decay_ref[device] = decay
-        else:
-            decay = decay_ref[device]
-            tail = tail + extra
-        arrive_ref[device] = carried
-        carried = decay * carried + got_ref[device, :, 0:wide]
-    if not first:
-        lane = lax.broadcasted_iota(jnp.int32, (1, LANE), 1)
-        low = jnp.where(lane < LANE // 2, tail, 0.0)
-        high = jnp.where(lane < LANE // 2, 0.0, tail)
-        sums_ref[0] = spread(jnp.sum(low, axis=1, keepdims=True))
-        sums_ref[1] = spread(jnp.sum(high, axis=1, keepdims=True))
+            rates = half_rates(s, rate_ref, block)
+            mine = keep_ref[s.half, block : block + 1, :]
+            other = got_ref[s.half, block : block + 1, :]
+            core_ref[0, block] = jnp.exp2(rates * jnp.where(low, mine, other))
+            core_ref[1, block] = jnp.exp2(rates * jnp.where(low, other, mine))
+        near = jnp.where(low, got, keep) if backward else jnp.where(low, keep, got)
+        far = jnp.where(low, keep, got) if backward else jnp.where(low, got, keep)
+        chip_ref[block] = core_ref[0 if backward else 1, block] * near + far
+    chip_ref[s.half] = keep_ref[s.half] + got_ref[s.half]
+
+
+def level_weights(s, stride, radix, packets, rate_ref, around_in, weight_ref, around_ref):
+    digit = lax.rem(lax.axis_index("seq") // stride, radix)
+    digits = [digit ^ k for k in range(radix)]
+    times = [packet[s.half, 0 : s.half, :] for packet in packets]
+    none = jnp.zeros_like(times[0])
+
+    def gathered(test):
+        return sum(jnp.where(test(d), t, 0.0) for d, t in zip(digits, times))
+
+    rates = [half_rates(s, rate_ref, block) for block in range(s.half)]
+    for side in (0, 1):
+        def beyond(a, b):
+            return a < b if side else a > b
+
+        start = around_in[side] if around_in is not None else none
+        for k in range(radix):
+            span = gathered(lambda d: beyond(d, digits[k]))
+            for block in range(s.half):
+                weight_ref[side, radix - 1 + k, block] = jnp.exp2(
+                    rates[block] * span[block : block + 1]
+                )
+            if k:
+                on = beyond(digit, digits[k])
+                gap = start + gathered(
+                    lambda d: jnp.logical_and(beyond(d, digits[k]), beyond(digit, d))
+                )
+                for block in range(s.half):
+                    weight_ref[side, k - 1, block] = jnp.where(
+                        on, jnp.exp2(rates[block] * gap[block : block + 1]), 0.0
+                    )
+        around_ref[side] = start + gathered(lambda d: beyond(digit, d))
+
+
+def level_kernel(s, level, backward, first, *refs):
+    stride, radix = s.levels[level]
+    last = level == len(s.levels) - 1
+    refs = list(refs)
+    packets, refs = refs[:radix], refs[radix:]
+    arrive_in = around_in = None
+    if level:
+        arrive_in = refs.pop(0)
+    if first:
+        rate_ref = refs.pop(0)
+        if level:
+            around_in = refs.pop(0)
+    else:
+        weight_ref = refs.pop(0)
+    if last:
+        keep_ref, got_ref, core_ref = refs[:3]
+        own_ref, give_ref, sums_ref = refs[3:6]
+        refs = refs[6:]
+    else:
+        group_ref, arrive_ref = refs[:2]
+        refs = refs[2:]
+    if first:
+        weight_ref, around_ref = refs
+        level_weights(
+            s, stride, radix, packets, rate_ref, around_in, weight_ref, around_ref
+        )
+    side = 1 if backward else 0
+    low = my_core() == 0
+    for block in range(s.half):
+        values = [packet[block] for packet in packets]
+        arrive = summed(
+            [weight_ref[side, k - 1, block] * values[k] for k in range(1, radix)]
+        )
+        if level:
+            arrive = arrive_in[block] + arrive
+        if not last:
+            arrive_ref[block] = arrive
+            group_ref[block] = summed(
+                [weight_ref[side, radix - 1 + k, block] * values[k] for k in range(radix)]
+            )
+            continue
+        keep, got = keep_ref[block], got_ref[block]
+        near = jnp.where(low, got, keep) if backward else jnp.where(low, keep, got)
+        far = core_ref[side, block] * arrive + near
+        at_near = jnp.logical_not(low) if backward else low
+        own_ref[block] = jnp.where(at_near, arrive, far)
+        give_ref[block] = jnp.where(at_near, far, arrive)
+    spare = summed([packet[s.half] for packet in packets])
+    if last:
+        whole = jnp.sum(spare[0:SUB], axis=1, keepdims=True)
+        sums_ref[0] = jnp.broadcast_to(whole[0:1], (SUB, LANE))
+        sums_ref[1] = jnp.broadcast_to(whole[1:2], (SUB, LANE))
+    else:
+        group_ref[s.half] = spare
 
 
 def total_sum(sums, index):
@@ -247,16 +357,17 @@
 def forward_kernel(s, offset, first, *refs):
     refs = list(refs)
     rhs_ref, curv_ref, rate_ref, skip_ref, damp_ref = refs[:5]
-    decay_ref, drive_ref, cx_ref, total_ref, e_in, arrive_ref = refs[5:11]
-    refs = refs[11:]
+    low_scan, high_scan, cx_ref, total_ref, e_in = refs[5:10]
+    arrive, refs = refs[10:12], refs[12:]
     if not first:
         r_ref, y0_ref = refs[:2]
         sums_b, sums_c = refs[2 : 2 + STREAMS], refs[2 + STREAMS : 2 + 2 * STREAMS]
         refs = refs[2 + 2 * STREAMS :]
         ratio = total_sum(sums_c, 0) / total_sum(sums_b, 0)
-    e_out, out_ref, w_ref, y_ref = refs
-
-    def body(block, carry):
+    e_out, keep_ref, give_ref, w_ref, y_ref, put, arrive_ref = refs
+    gather_state(s, arrive, arrive_ref)
+
+    def body(block, scan, place, carry):
         squares, inner = carry
         rates = load_rates(s, rate_ref, block + offset)
         total = total_ref[block]
@@ -271,7 +382,7 @@
             parts = [skip * v]
             for n in range(s.entries):
                 state[n] = (
-                    decay_ref[block, j, n] * state[n] + drive_ref[block, j, n] * v
+                    scan[place, j, n, 0] * state[n] + scan[place, j, n, 1] * v
                 )
                 parts.append(cx_ref[j, n] * state[n])
             y = summed(parts)
@@ -291,33 +402,35 @@
         for j in reversed(range(s.steps)):
             w = w_ref[block, j]
             for n in range(s.entries):
-                passed[n] = decay_ref[block, j, n] * (cx_ref[j, n] * w + passed[n])
-        finish_summary(s, block, passed, rates, total, e_out, out_ref, True)
+                passed[n] = scan[place, j, n, 0] * (cx_ref[j, n] * w + passed[n])
+        finish_summary(s, block, passed, rates, total, e_out, put, True)
         return squares, inner
 
-    squares, inner = lax.fori_loop(0, s.blocks, body, tuple(zeros(2)))
-    put_sums(s, out_ref, squares, inner)
-
-
-def backward_block(s, block, w_ref, skip, decay_ref, drive_ref, cx_ref, passed, use):
+    squares, inner = over_blocks(s, (low_scan, high_scan), body, tuple(zeros(2)))
+    put_sums(s, put, keep_ref, give_ref, squares, inner)
+
+
+def backward_block(s, block, scan, place, w_ref, skip, cx_ref, passed, use):
     for j in reversed(range(s.steps)):
         w = w_ref[block, j]
         parts = [skip * w]
         for n in range(s.entries):
             costate = cx_ref[j, n] * w + passed[n]
-            passed[n] = decay_ref[block, j, n] * costate
-            parts.append(drive_ref[block, j, n] * costate)
+            passed[n] = scan[place, j, n, 0] * costate
+            parts.append(scan[place, j, n, 1] * costate)
         use(j, summed(parts))
 
 
 def backward_kernel(s, offset, *refs):
     rhs_ref, rate_ref, skip_ref, damp_ref = refs[:4]
-    decay_ref, drive_ref, cx_ref, total_ref, e_in, arrive_ref, w_ref = refs[4:11]
-    sums_b = refs[11 : 11 + STREAMS]
-    e_out, out_ref, r_ref = refs[11 + STREAMS :]
+    low_scan, high_scan, cx_ref, total_ref, e_in = refs[4:9]
+    arrive, w_ref = refs[9:11], refs[11]
+    sums_b = refs[12 : 12 + STREAMS]
+    e_out, keep_ref, give_ref, r_ref, put, arrive_ref = refs[12 + STREAMS :]
+    gather_state(s, arrive, arrive_ref)
     step = total_sum(sums_b, 0) / total_sum(sums_b, 1)
 
-    def body(block, squares):
+    def body(block, scan, place, squares):
         rates = load_rates(s, rate_ref, block + offset)
         total = total_ref[block]
         skip = spread(skip_ref[0:1, cols(block + offset)])
@@ -332,34 +445,34 @@
             r_ref[block, j] = r
             acc[0] = acc[0] + r * r
 
-        backward_block(
-            s, block, w_ref, skip, decay_ref, drive_ref, cx_ref, passed, use
-        )
+        backward_block(s, block, scan, place, w_ref, skip, cx_ref, passed, use)
         state = zeros(s.entries)
         for j in range(s.steps):
             v = r_ref[block, j]
             for n in range(s.entries):
                 state[n] = (
-                    decay_ref[block, j, n] * state[n] + drive_ref[block, j, n] * v
+                    scan[place, j, n, 0] * state[n] + scan[place, j, n, 1] * v
                 )
-        finish_summary(s, block, state, rates, total, e_out, out_ref, False)
+        finish_summary(s, block, state, rates, total, e_out, put, False)
         return acc[0]
 
-    squares = lax.fori_loop(0, s.blocks, body, zeros(1)[0])
-    put_sums(s, out_ref, squares, zeros(1)[0])
+    squares = over_blocks(s, (low_scan, high_scan), body, zeros(1)[0])
+    put_sums(s, put, keep_ref, give_ref, squares, zeros(1)[0])
 
 
 def last_kernel(s, offset, *refs):
     rhs_ref, rate_ref, skip_ref, damp_ref = refs[:4]
-    decay_ref, drive_ref, cx_ref, total_ref, e_in, arrive_ref, w_ref = refs[4:11]
-    r_ref, d_ref = refs[11:13]
-    refs = refs[13:]
+    low_scan, high_scan, cx_ref, total_ref, e_in = refs[4:9]
+    arrive, w_ref = refs[9:11], refs[11]
+    r_ref, d_ref = refs[12:14]
+    refs = refs[14:]
     sums_b, sums_c = refs[:STREAMS], refs[STREAMS : 2 * STREAMS]
     sums_d = refs[2 * STREAMS : 3 * STREAMS]
     refs = refs[3 * STREAMS :]
     if offset:
         refs = refs[2:]
-    solution_ref, residual_ref, tile_s, tile_r, sem_s, sem_r = refs
+    solution_ref, residual_ref, tile_s, tile_r, sem_s, sem_r, arrive_ref = refs
+    gather_state(s, arrive, arrive_ref)
     before_step = total_sum(sums_b, 0) / total_sum(sums_b, 1)
     step = total_sum(sums_c, 0) / total_sum(sums_d, 1)
 
@@ -374,7 +487,7 @@
             ),
         )
 
-    def body(block, carry):
+    def body(block, scan, place, carry):
         rates = load_rates(s, rate_ref, block + offset)
         skip = spread(skip_ref[0:1, cols(block + offset)])
         damp = spread(damp_ref[0:1, cols(block + offset)])
@@ -389,14 +502,12 @@
             )
             tile_r[block, rows, :] = r_ref[block, j] - step * (product + damp * along)
 
-        backward_block(
-            s, block, w_ref, skip, decay_ref, drive_ref, cx_ref, passed, use
-        )
+        backward_block(s, block, scan, place, w_ref, skip, cx_ref, passed, use)
         for copy in copies(block):
             copy.start()
         return carry
 
-    lax.fori_loop(0, s.blocks, body, 0)
+    over_blocks(s, (low_scan, high_scan), body, 0)
 
     def finish(block, carry):
         for copy in copies(block):
@@ -408,7 +519,7 @@
 
 VM = pl.BlockSpec(memory_space=pltpu.VMEM)
 HBM = pl.BlockSpec(memory_space=pltpu.HBM)
-LIMIT = 4 * 1024 * 1024
+LIMIT = 6 * 1024 * 1024
 
 
 def in_hbm(x):
@@ -416,7 +527,7 @@
 
 
 def call(body, name, outs, scratch, args, passes, n_hbm=0, out_specs=None, aliases=()):
-    work = passes * 16 * 128 * 2048 // STREAMS
+    work = int(passes * 16 * 128 * 2048)
     return pl.pallas_call(
         body,
         name=name,
@@ -442,14 +553,17 @@
     per_token = held((s.blocks, s.steps, SUB, LANE), F32)
     expanded = (s.steps, entries, SUB, LANE)
     edge = held((s.blocks, entries, SUB, LANE), F32)
-    whole_state = held((s.blocks, s.steps, entries, SUB, LANE), F32)
+    half_state = held((s.half, s.steps, entries, 2, SUB, LANE), F32)
     tile = (s.blocks, tokens, LANE)
-    packet = held((devices, 1, (s.rows + 1) * LANE), F32)
-    linked = held((devices, 1, s.rows * LANE), F32)
+    packet = held((s.half + 1, entries, LANE), F32)
+    linked = held((s.half, entries, LANE), F32)
     sums = held((2, SUB, LANE), F32)
-
-    def exchange(send):
-        return lax.all_to_all(send, "seq", 0, 0)
+    both = pltpu.VMEM((2, s.half + 1, entries, LANE), F32)
+    joined = pltpu.VMEM((s.blocks, entries, LANE), F32)
+
+    def swap(send, distance):
+        pairs = [(device, device ^ distance) for device in range(devices)]
+        return lax.ppermute(send, "seq", pairs)
 
     def kernel(body, *more):
         return functools.partial(body, s, *more)
@@ -460,16 +574,17 @@
             kernel(first_kernel, offsets[g]),
             f"first_{g}",
             [
-                whole_state, whole_state, held(expanded, F32),
-                held((s.blocks, SUB, LANE), F32), edge, packet,
+                half_state, half_state, held(expanded, F32),
+                held((s.blocks, SUB, LANE), F32), edge, packet, packet,
                 held(tile, F32), held(tile, F32), held((entries, columns), F32),
-                held((1, columns), F32), held((1, columns), F32), linked,
+                held((1, columns), F32), held((1, columns), F32),
             ],
             [
                 pltpu.VMEM(tile, F32), pltpu.VMEM(expanded, F32),
                 pltpu.VMEM((2, entries, tokens), F32),
                 pltpu.VMEM((2, tokens, entries), F32),
                 dma((s.blocks,)), dma((s.blocks,)), dma((s.blocks,)), dma((5,)),
+                both,
             ],
             [
                 in_hbm(x)
@@ -483,68 +598,97 @@
         )
         for g in every
     ]
-    decay, drive, cx, total, e, send, rhs_v, curv, rates, skips, damps, link_rate = zip(
-        *firsts
-    )
-
-    def link(g, got, backward, letter, decays=None):
-        first = decays is None
-        return call(
-            kernel(link_kernel, backward, first),
-            f"link_{letter}_{g}",
-            [linked, linked if first else sums],
+    (
+        low_scan, high_scan, cx, total, e, keep, give, rhs_v, curv, rates, skips, damps,
+    ) = zip(*firsts)
+
+    def around(keep, give, backward, letter, known):
+        (keep,), (give,) = keep, give
+        first = known is None
+        made = []
+        got = swap(give, 1)
+        outs = [packet] + [held((2, s.half, entries, LANE), F32)] * first
+        chip = call(
+            kernel(join_kernel, backward, first),
+            f"join_{letter}",
+            outs,
             [],
-            (got, link_rate[g] if first else decays),
-            1,
+            (keep, got, rates[0] if first else known[0]),
+            0.02,
         )
-
-    def around(send, backward, letter, decays):
-        got = [exchange(send[g]) for g in every]
-        pairs = [link(g, got[g], backward, letter, decays and decays[g]) for g in every]
-        return [exchange(pairs[g][0]) for g in every], [pairs[g][1] for g in every]
+        core = chip[1] if first else known[0]
+        group, arrive, passing = chip[0], None, None
+        for level, (stride, radix) in enumerate(s.levels):
+            last = level == len(s.levels) - 1
+            packets = [group] + [swap(group, stride * k) for k in range(1, radix)]
+            args = packets + [arrive] * (level > 0)
+            args += [rates[0] if first else known[1 + level]]
+            args += [passing] * (first and level > 0)
+            outs = [linked, linked, sums] if last else [packet, linked]
+            if last:
+                args += [keep, got, core]
+            if first:
+                outs = outs + [
+                    held((2, 2 * radix - 1, s.half, entries, LANE), F32),
+                    held((2, s.half, LANE), F32),
+                ]
+            results = call(
+                kernel(level_kernel, level, backward, first),
+                f"level_{level}_{letter}",
+                outs,
+                [],
+                args,
+                0.02,
+            )
+            if first:
+                *results, weights, passing = results
+                made.append(weights)
+            group, arrive = results[:2]
+        own, give_back, total = results
+        return (own, swap(give_back, 1)), [total], known or [core, *made]
 
     def common(g, e, arrive):
-        return (decay[g], drive[g], cx[g], total[g], e[g], arrive[g])
+        return (low_scan[g], high_scan[g], cx[g], total[g], e[g], *arrive)
 
     def consts(g):
         return (rates[g], skips[g], damps[g])
 
-    arrive, decays = around(send, False, "a", None)
-    e, send, w, y0 = zip(
+    arrive, _, known = around(keep, give, False, "a", None)
+    e, keep, give, w, y0 = zip(
         *[
             call(
                 kernel(forward_kernel, offsets[g], True),
                 f"forward_a_{g}",
-                [edge, packet, per_token, per_token],
-                [],
+                [edge, packet, packet, per_token, per_token],
+                [both, joined],
                 (rhs_v[g], curv[g], *consts(g), *common(g, e, arrive)),
                 2,
             )
             for g in every
         ]
     )
-    arrive, sums_b = around(send, True, "b", decays)
-    e, send, r = zip(
+    arrive, sums_b, _ = around(keep, give, True, "b", known)
+    e, keep, give, r = zip(
         *[
             call(
                 kernel(backward_kernel, offsets[g]),
                 f"backward_a_{g}",
-                [edge, packet, per_token],
-                [],
+                [edge, packet, packet, per_token],
+                [both, joined],
                 (rhs_v[g], *consts(g), *common(g, e, arrive), w[g], *sums_b),
                 2,
             )
             for g in every
         ]
     )
-    arrive, sums_c = around(send, False, "c", decays)
-    e, send, w, d = zip(
+    arrive, sums_c, _ = around(keep, give, False, "c", known)
+    e, keep, give, w, d = zip(
         *[
             call(
                 kernel(forward_kernel, offsets[g], False),
                 f"forward_b_{g}",
-                [edge, packet, per_token, per_token],
-                [],
+                [edge, packet, packet, per_token, per_token],
+                [both, joined],
                 (
                     rhs_v[g], curv[g], *consts(g), *common(g, e, arrive),
                     r[g], y0[g], *sums_b, *sums_c,
@@ -554,7 +698,7 @@
             for g in every
         ]
     )
-    arrive, sums_d = around(send, True, "d", decays)
+    arrive, sums_d, _ = around(keep, give, True, "d", known)
     outs = ()
     for g in every:
         args = (
@@ -569,7 +713,7 @@
             out_specs=[HBM] * 2,
             scratch_shapes=[
                 pltpu.VMEM(tile, F32), pltpu.VMEM(tile, F32),
-                dma((s.blocks,)), dma((s.blocks,)),
+                dma((s.blocks,)), dma((s.blocks,)), joined,
             ],
             input_output_aliases={len(args): 0, len(args) + 1: 1} if outs else {},
             compiler_params=pltpu.CompilerParams(vmem_limit_bytes=LIMIT),

time: 121 us -> 117 us (0.967)
  blocking collectives: 86.5 us -> 0 us
  waiting for transfers between devices: 0 us -> 43.6 us
  starting transfers between devices: 0 us -> 34.2 us
  Pallas kernels: 33.6 us -> 38.1 us
    all_to_all x8 -> x0, blocking collectives: 86.5 us -> none  [exchange(): return lax.all_to_all(send, 'seq', 0, 0)]
    ppermute x0 -> x32, waiting for transfers between devices: none -> 43.6 us  [swap(): return lax.ppermute(send, 'seq', pairs)]
    ppermute x0 -> x32, starting transfers between devices: none -> 34.2 us  [swap(): return lax.ppermute(send, 'seq', pairs)]
    pallas_call x8 -> x16, Pallas kernels: 29 us -> 33.2 us  [call(): pl.pallas_call(body, name=name, out_shape=outs, in_specs=[HBM] * n_hbm +...]
  transfers between devices with their start and end apart: 0 -> 32, of which waited for: 0 -> 28; matrix products, arithmetic and copies ran while one was open for 0% -> 0% of each run, Pallas kernels for 0% -> 0%
where the time goes in v4:
time: 117 us
  waiting for transfers between devices  43.6 us (37%)
  Pallas kernels  38.1 us (33%)
  starting transfers between devices  34.2 us (29%)
    ppermute x32, waiting for transfers between devices, swap(): return lax.ppermute(send, 'seq', pairs)  43.6 us
    ppermute x32, starting transfers between devices, swap(): return lax.ppermute(send, 'seq', pairs)  34.2 us
    pallas_call x16, Pallas kernels, call(): pl.pallas_call(body, name=name, out_shape=outs, in_specs=[HBM] * n_hbm +...  33.2 us
    pallas_call x1, Pallas kernels, per_device(): pl.pallas_call(kernel(last_kernel, offsets[g]), name=f'backward_b_{g}', o...  4.84 us
  transfers between devices with their start and end apart: 32, of which 28 were waited for; matrix products, arithmetic and copies ran while one was open for 0% of the time, Pallas kernels for 0%

profile of v4, /device:TPU:0, one launch (start us, length us, event | category | flops | bytes accessed | tf_op | source)
XLA Modules:
  0.0 116.5 jit_solution(14709113419162568419)
XLA Ops:
  0.6 12.0 %first_0.1 = (f32[8,16,16,2,8,128]{5,4,3,2,1,0:T(8,128)S(1)}, f32[8,16,16,2,8,128]{5,4,3,2,1,0:T(8,128)S(1)}, f32[16,16,8,128]{3,2,1,0:T(8,128)S(1)}, f32[16,8,1...) custom-call(f32[128,2048]{1,0:T(8,128)} %refs_0_.1, ...), custom_call_target="tpu_custom_call" | custom-call | flops 8388608 | bytes 8388608 | tf_op jit(solution)/shard_map/first_0/pallas_call | solution.py:531
  13.2 0.9 collective-permute-done.refs_1_.refs_8_
  14.2 3.8 %collective-permute-start.3 = (f32[9,16,128]{2,1,0:T(8,128)S(1)}, f32[9,16,128]{2,1,0:T(8,128)S(1)}, u32[]{:S(2)}, u32[]{:S(2)}) collective-permute-start(f32[9,16,128]{2,1,0:T(8,128)S(1)} %get-tuple-element.64.refs_0_), channel_id=1, source_target_pairs={{0,6},{1,7},{2,4},{3,5},{4,2},{5,3},{6,0},{7,1},{8,14},{9,15},{10,... | collective-permute-start | bytes 221192 | tf_op jit(solution)/shard_map/ppermute | solution.py:566
  18.7 2.0 %collective-permute-done.3.refs_3_ = f32[9,16,128]{2,1,0:T(8,128)S(1)} collective-permute-done((f32[9,16,128]{2,1,0:T(8,128)S(1)}, f32[9,16,128]{2,1,0:T(8,128)S(1)}, u32[]{:S(2)}, u32[]{:S(2)}) %collective-permute-start.3) | collective-permute-done | bytes 73760 | tf_op jit(solution)/shard_map/ppermute | solution.py:566
  20.7 1.7 %collective-permute-done.2.refs_2_ = f32[9,16,128]{2,1,0:T(8,128)S(1)} collective-permute-done((f32[9,16,128]{2,1,0:T(8,128)S(1)}, f32[9,16,128]{2,1,0:T(8,128)S(1)}, u32[]{:S(2)}, u32[]{:S(2)}) %collective-permute-start.2) | collective-permute-done | bytes 73760 | tf_op jit(solution)/shard_map/ppermute | solution.py:566
  23.0 3.7 %collective-permute-start.6 = (f32[9,16,128]{2,1,0:T(8,128)S(1)}, f32[9,16,128]{2,1,0:T(8,128)S(1)}, u32[]{:S(2)}, u32[]{:S(2)}) collective-permute-start(f32[9,16,128]{2,1,0:T(8,128)S(1)} %get-tuple-element.65.refs_0_), channel_id=1, source_target_pairs={{0,24},{1,25},{2,26},{3,27},{4,28},{5,29},{6,30},{7,31},{8,16},{9,... | collective-permute-start | bytes 221192 | tf_op jit(solution)/shard_map/ppermute | solution.py:566
  26.7 0.8 collective-permute-start.4
  27.5 2.0 %collective-permute-done.6.refs_3_ = f32[9,16,128]{2,1,0:T(8,128)S(1)} collective-permute-done((f32[9,16,128]{2,1,0:T(8,128)S(1)}, f32[9,16,128]{2,1,0:T(8,128)S(1)}, u32[]{:S(2)}, u32[]{:S(2)}) %collective-permute-start.6) | collective-permute-done | bytes 73760 | tf_op jit(solution)/shard_map/ppermute | solution.py:566
  29.5 2.9 %collective-permute-done.5.refs_2_ = f32[9,16,128]{2,1,0:T(8,128)S(1)} collective-permute-done((f32[9,16,128]{2,1,0:T(8,128)S(1)}, f32[9,16,128]{2,1,0:T(8,128)S(1)}, u32[]{:S(2)}, u32[]{:S(2)}) %collective-permute-start.5) | collective-permute-done | bytes 73760 | tf_op jit(solution)/shard_map/ppermute | solution.py:566
  32.4 0.8 level_1_a.1
  33.2 1.3 %collective-permute-done.7.refs_11_ = f32[8,16,128]{2,1,0:T(8,128)S(1)} collective-permute-done((f32[8,16,128]{2,1,0:T(8,128)S(1)}, f32[8,16,128]{2,1,0:T(8,128)S(1)}, u32[]{:S(2)}, u32[]{:S(2)}) %collective-permute-start.7) | collective-permute-done | bytes 65568 | tf_op jit(solution)/shard_map/ppermute | solution.py:566
  34.5 6.6 %forward_a_0.1 = (f32[16,16,8,128]{3,2,1,0:T(8,128)S(1)}, f32[9,16,128]{2,1,0:T(8,128)S(1)}, f32[9,16,128]{2,1,0:T(8,128)S(1)}, f32[16,16,8,128]{3,2,1,0:T(8,128)S(1)}, f32[16,16,8,128]{3,2,1,0:T(8,128)S(1)}) custom-call(f32[16,128,128]{2,1,0:T(8,128)S(1)} %get-tuple-element.52.refs_0_, f32[16,128,128]{2,1,0:T(8,128)S(1)} %get-tuple-element.60.refs_1_, ...), custom_call_target="tpu_custom_call" | custom-call | flops 8388608 | bytes 8388608 | tf_op jit(solution)/shard_map/forward_a_0/pallas_call | solution.py:531
  41.2 1.1 collective-permute-done.8.refs_1_.refs_7_
  42.4 1.6 %collective-permute-start.11 = (f32[9,16,128]{2,1,0:T(8,128)S(1)}, f32[9,16,128]{2,1,0:T(8,128)S(1)}, u32[]{:S(2)}, u32[]{:S(2)}) collective-permute-start(f32[9,16,128]{2,1,0:T(8,128)S(1)} %join_b.1.refs_0_), channel_id=1, source_target_pairs={{0,6},{1,7},{2,4},{3,5},{4,2},{5,3},{6,0},{7,1},{8,14},{9,15},{10,... | collective-permute-start | bytes 221192 | tf_op jit(solution)/shard_map/ppermute | solution.py:566
  43.9 1.7 %collective-permute-start.10 = (f32[9,16,128]{2,1,0:T(8,128)S(1)}, f32[9,16,128]{2,1,0:T(8,128)S(1)}, u32[]{:S(2)}, u32[]{:S(2)}) collective-permute-start(f32[9,16,128]{2,1,0:T(8,128)S(1)} %join_b.1.refs_0_), channel_id=1, source_target_pairs={{0,4},{1,5},{2,6},{3,7},{4,0},{5,1},{6,2},{7,3},{8,12},{9,13},{10,... | collective-permute-start | bytes 221192 | tf_op jit(solution)/shard_map/ppermute | solution.py:566
  45.9 1.9 %collective-permute-done.11.refs_3_ = f32[9,16,128]{2,1,0:T(8,128)S(1)} collective-permute-done((f32[9,16,128]{2,1,0:T(8,128)S(1)}, f32[9,16,128]{2,1,0:T(8,128)S(1)}, u32[]{:S(2)}, u32[]{:S(2)}) %collective-permute-start.11) | collective-permute-done | bytes 73760 | tf_op jit(solution)/shard_map/ppermute | solution.py:566
  47.8 1.4 %collective-permute-done.10.refs_2_ = f32[9,16,128]{2,1,0:T(8,128)S(1)} collective-permute-done((f32[9,16,128]{2,1,0:T(8,128)S(1)}, f32[9,16,128]{2,1,0:T(8,128)S(1)}, u32[]{:S(2)}, u32[]{:S(2)}) %collective-permute-start.10) | collective-permute-done | bytes 73760 | tf_op jit(solution)/shard_map/ppermute | solution.py:566
  49.2 0.7 collective-permute-done.9.refs_1_
  50.0 2.7 %collective-permute-start.14 = (f32[9,16,128]{2,1,0:T(8,128)S(1)}, f32[9,16,128]{2,1,0:T(8,128)S(1)}, u32[]{:S(2)}, u32[]{:S(2)}) collective-permute-start(f32[9,16,128]{2,1,0:T(8,128)S(1)} %get-tuple-element.75.refs_0_), channel_id=1, source_target_pairs={{0,24},{1,25},{2,26},{3,27},{4,28},{5,29},{6,30},{7,31},{8,16},{9,... | collective-permute-start | bytes 221192 | tf_op jit(solution)/shard_map/ppermute | solution.py:566
  52.7 1.8 %collective-permute-start.12 = (f32[9,16,128]{2,1,0:T(8,128)S(1)}, f32[9,16,128]{2,1,0:T(8,128)S(1)}, u32[]{:S(2)}, u32[]{:S(2)}) collective-permute-start(f32[9,16,128]{2,1,0:T(8,128)S(1)} %get-tuple-element.75.refs_0_), channel_id=1, source_target_pairs={{0,8},{1,9},{2,10},{3,11},{4,12},{5,13},{6,14},{7,15},{8,0},{9,1},... | collective-permute-start | bytes 221192 | tf_op jit(solution)/shard_map/ppermute | solution.py:566
  54.4 1.9 %collective-permute-done.14.refs_3_ = f32[9,16,128]{2,1,0:T(8,128)S(1)} collective-permute-done((f32[9,16,128]{2,1,0:T(8,128)S(1)}, f32[9,16,128]{2,1,0:T(8,128)S(1)}, u32[]{:S(2)}, u32[]{:S(2)}) %collective-permute-start.14) | collective-permute-done | bytes 73760 | tf_op jit(solution)/shard_map/ppermute | solution.py:566
  56.4 2.9 %collective-permute-done.13.refs_2_ = f32[9,16,128]{2,1,0:T(8,128)S(1)} collective-permute-done((f32[9,16,128]{2,1,0:T(8,128)S(1)}, f32[9,16,128]{2,1,0:T(8,128)S(1)}, u32[]{:S(2)}, u32[]{:S(2)}) %collective-permute-start.13) | collective-permute-done | bytes 73760 | tf_op jit(solution)/shard_map/ppermute | solution.py:566
  59.4 1.2 %collective-permute-done.15.refs_10_ = f32[8,16,128]{2,1,0:T(8,128)S(1)} collective-permute-done((f32[8,16,128]{2,1,0:T(8,128)S(1)}, f32[8,16,128]{2,1,0:T(8,128)S(1)}, u32[]{:S(2)}, u32[]{:S(2)}) %collective-permute-start.15) | collective-permute-done | bytes 65568 | tf_op jit(solution)/shard_map/ppermute | solution.py:566
  60.7 6.3 %backward_a_0.1 = (f32[16,16,8,128]{3,2,1,0:T(8,128)S(1)}, f32[9,16,128]{2,1,0:T(8,128)S(1)}, f32[9,16,128]{2,1,0:T(8,128)S(1)}, f32[16,16,8,128]{3,2,1,0:T(8,128)S(1)}) custom-call(f32[16,128,128]{2,1,0:T(8,128)S(1)} %get-tuple-element.52.refs_0_, f32[16,2048]{1,0:T(8,128)S(1)} %get-tuple-element.53.refs_2_.refs_4_.refs_5_.refs_1_, ...), custom_call_target="tpu_custom_call" | custom-call | flops 8388608 | bytes 8388608 | tf_op jit(solution)/shard_map/backward_a_0/pallas_call | solution.py:531
  67.2 1.1 collective-permute-done.16.refs_1_.refs_7_
  68.3 1.6 %collective-permute-start.19 = (f32[9,16,128]{2,1,0:T(8,128)S(1)}, f32[9,16,128]{2,1,0:T(8,128)S(1)}, u32[]{:S(2)}, u32[]{:S(2)}) collective-permute-start(f32[9,16,128]{2,1,0:T(8,128)S(1)} %join_c.1.refs_0_), channel_id=1, source_target_pairs={{0,6},{1,7},{2,4},{3,5},{4,2},{5,3},{6,0},{7,1},{8,14},{9,15},{10,... | collective-permute-start | bytes 221192 | tf_op jit(solution)/shard_map/ppermute | solution.py:566
  69.9 1.2 %collective-permute-start.18 = (f32[9,16,128]{2,1,0:T(8,128)S(1)}, f32[9,16,128]{2,1,0:T(8,128)S(1)}, u32[]{:S(2)}, u32[]{:S(2)}) collective-permute-start(f32[9,16,128]{2,1,0:T(8,128)S(1)} %join_c.1.refs_0_), channel_id=1, source_target_pairs={{0,4},{1,5},{2,6},{3,7},{4,0},{5,1},{6,2},{7,3},{8,12},{9,13},{10,... | collective-permute-start | bytes 221192 | tf_op jit(solution)/shard_map/ppermute | solution.py:566
  71.1 0.8 collective-permute-start.17
  71.9 1.9 %collective-permute-done.19.refs_3_ = f32[9,16,128]{2,1,0:T(8,128)S(1)} collective-permute-done((f32[9,16,128]{2,1,0:T(8,128)S(1)}, f32[9,16,128]{2,1,0:T(8,128)S(1)}, u32[]{:S(2)}, u32[]{:S(2)}) %collective-permute-start.19) | collective-permute-done | bytes 73760 | tf_op jit(solution)/shard_map/ppermute | solution.py:566
  73.7 1.4 %collective-permute-done.18.refs_2_ = f32[9,16,128]{2,1,0:T(8,128)S(1)} collective-permute-done((f32[9,16,128]{2,1,0:T(8,128)S(1)}, f32[9,16,128]{2,1,0:T(8,128)S(1)}, u32[]{:S(2)}, u32[]{:S(2)}) %collective-permute-start.18) | collective-permute-done | bytes 73760 | tf_op jit(solution)/shard_map/ppermute | solution.py:566
  75.5 2.3 %collective-permute-start.22 = (f32[9,16,128]{2,1,0:T(8,128)S(1)}, f32[9,16,128]{2,1,0:T(8,128)S(1)}, u32[]{:S(2)}, u32[]{:S(2)}) collective-permute-start(f32[9,16,128]{2,1,0:T(8,128)S(1)} %get-tuple-element.85.refs_0_), channel_id=1, source_target_pairs={{0,24},{1,25},{2,26},{3,27},{4,28},{5,29},{6,30},{7,31},{8,16},{9,... | collective-permute-start | bytes 221192 | tf_op jit(solution)/shard_map/ppermute | solution.py:566
  77.8 2.1 %collective-permute-start.20 = (f32[9,16,128]{2,1,0:T(8,128)S(1)}, f32[9,16,128]{2,1,0:T(8,128)S(1)}, u32[]{:S(2)}, u32[]{:S(2)}) collective-permute-start(f32[9,16,128]{2,1,0:T(8,128)S(1)} %get-tuple-element.85.refs_0_), channel_id=1, source_target_pairs={{0,8},{1,9},{2,10},{3,11},{4,12},{5,13},{6,14},{7,15},{8,0},{9,1},... | collective-permute-start | bytes 221192 | tf_op jit(solution)/shard_map/ppermute | solution.py:566
  80.0 2.6 %collective-permute-done.22.refs_3_ = f32[9,16,128]{2,1,0:T(8,128)S(1)} collective-permute-done((f32[9,16,128]{2,1,0:T(8,128)S(1)}, f32[9,16,128]{2,1,0:T(8,128)S(1)}, u32[]{:S(2)}, u32[]{:S(2)}) %collective-permute-start.22) | collective-permute-done | bytes 73760 | tf_op jit(solution)/shard_map/ppermute | solution.py:566
  82.5 2.1 %collective-permute-done.21.refs_2_ = f32[9,16,128]{2,1,0:T(8,128)S(1)} collective-permute-done((f32[9,16,128]{2,1,0:T(8,128)S(1)}, f32[9,16,128]{2,1,0:T(8,128)S(1)}, u32[]{:S(2)}, u32[]{:S(2)}) %collective-permute-start.21) | collective-permute-done | bytes 73760 | tf_op jit(solution)/shard_map/ppermute | solution.py:566
  84.7 1.2 %collective-permute-done.23.refs_11_ = f32[8,16,128]{2,1,0:T(8,128)S(1)} collective-permute-done((f32[8,16,128]{2,1,0:T(8,128)S(1)}, f32[8,16,128]{2,1,0:T(8,128)S(1)}, u32[]{:S(2)}, u32[]{:S(2)}) %collective-permute-start.23) | collective-permute-done | bytes 65568 | tf_op jit(solution)/shard_map/ppermute | solution.py:566
  86.0 6.8 %forward_b_0.1 = (f32[16,16,8,128]{3,2,1,0:T(8,128)S(1)}, f32[9,16,128]{2,1,0:T(8,128)S(1)}, f32[9,16,128]{2,1,0:T(8,128)S(1)}, f32[16,16,8,128]{3,2,1,0:T(8,128)S(1)}, f32[16,16,8,128]{3,2,1,0:T(8,128)S(1)}) custom-call(f32[16,128,128]{2,1,0:T(8,128)S(1)} %get-tuple-element.52.refs_0_, f32[16,128,128]{2,1,0:T(8,128)S(1)} %get-tuple-element.60.refs_1_, ...), custom_call_target="tpu_custom_call" | custom-call | flops 8388608 | bytes 8388608 | tf_op jit(solution)/shard_map/forward_b_0/pallas_call | solution.py:531
  93.0 1.1 collective-permute-done.24.refs_1_.refs_7_
  94.2 1.6 %collective-permute-start.27 = (f32[9,16,128]{2,1,0:T(8,128)S(1)}, f32[9,16,128]{2,1,0:T(8,128)S(1)}, u32[]{:S(2)}, u32[]{:S(2)}) collective-permute-start(f32[9,16,128]{2,1,0:T(8,128)S(1)} %join_d.1.refs_0_), channel_id=1, source_target_pairs={{0,6},{1,7},{2,4},{3,5},{4,2},{5,3},{6,0},{7,1},{8,14},{9,15},{10,... | collective-permute-start | bytes 221192 | tf_op jit(solution)/shard_map/ppermute | solution.py:566
  95.8 1.0 collective-permute-start.26
  96.8 0.9 collective-permute-start.25
  97.7 1.8 %collective-permute-done.27.refs_3_ = f32[9,16,128]{2,1,0:T(8,128)S(1)} collective-permute-done((f32[9,16,128]{2,1,0:T(8,128)S(1)}, f32[9,16,128]{2,1,0:T(8,128)S(1)}, u32[]{:S(2)}, u32[]{:S(2)}) %collective-permute-start.27) | collective-permute-done | bytes 73760 | tf_op jit(solution)/shard_map/ppermute | solution.py:566
  99.6 1.5 %collective-permute-done.26.refs_2_ = f32[9,16,128]{2,1,0:T(8,128)S(1)} collective-permute-done((f32[9,16,128]{2,1,0:T(8,128)S(1)}, f32[9,16,128]{2,1,0:T(8,128)S(1)}, u32[]{:S(2)}, u32[]{:S(2)}) %collective-permute-start.26) | collective-permute-done | bytes 73760 | tf_op jit(solution)/shard_map/ppermute | solution.py:566
  101.2 2.3 %collective-permute-start.30 = (f32[9,16,128]{2,1,0:T(8,128)S(1)}, f32[9,16,128]{2,1,0:T(8,128)S(1)}, u32[]{:S(2)}, u32[]{:S(2)}) collective-permute-start(f32[9,16,128]{2,1,0:T(8,128)S(1)} %get-tuple-element.95.refs_0_), channel_id=1, source_target_pairs={{0,24},{1,25},{2,26},{3,27},{4,28},{5,29},{6,30},{7,31},{8,16},{9,... | collective-permute-start | bytes 221192 | tf_op jit(solution)/shard_map/ppermute | solution.py:566
  103.6 2.1 %collective-permute-start.28 = (f32[9,16,128]{2,1,0:T(8,128)S(1)}, f32[9,16,128]{2,1,0:T(8,128)S(1)}, u32[]{:S(2)}, u32[]{:S(2)}) collective-permute-start(f32[9,16,128]{2,1,0:T(8,128)S(1)} %get-tuple-element.95.refs_0_), channel_id=1, source_target_pairs={{0,8},{1,9},{2,10},{3,11},{4,12},{5,13},{6,14},{7,15},{8,0},{9,1},... | collective-permute-start | bytes 221192 | tf_op jit(solution)/shard_map/ppermute | solution.py:566
  105.7 2.6 %collective-permute-done.30.refs_3_ = f32[9,16,128]{2,1,0:T(8,128)S(1)} collective-permute-done((f32[9,16,128]{2,1,0:T(8,128)S(1)}, f32[9,16,128]{2,1,0:T(8,128)S(1)}, u32[]{:S(2)}, u32[]{:S(2)}) %collective-permute-start.30) | collective-permute-done | bytes 73760 | tf_op jit(solution)/shard_map/ppermute | solution.py:566
  108.2 2.1 %collective-permute-done.29.refs_2_ = f32[9,16,128]{2,1,0:T(8,128)S(1)} collective-permute-done((f32[9,16,128]{2,1,0:T(8,128)S(1)}, f32[9,16,128]{2,1,0:T(8,128)S(1)}, u32[]{:S(2)}, u32[]{:S(2)}) %collective-permute-start.29) | collective-permute-done | bytes 73760 | tf_op jit(solution)/shard_map/ppermute | solution.py:566
  110.5 1.2 %collective-permute-done.31.refs_10_ = f32[8,16,128]{2,1,0:T(8,128)S(1)} collective-permute-done((f32[8,16,128]{2,1,0:T(8,128)S(1)}, f32[8,16,128]{2,1,0:T(8,128)S(1)}, u32[]{:S(2)}, u32[]{:S(2)}) %collective-permute-start.31) | collective-permute-done | bytes 65568 | tf_op jit(solution)/shard_map/ppermute | solution.py:566
  111.7 4.8 %backward_b_0.1 = (f32[128,2048]{1,0:T(8,128)}, f32[128,2048]{1,0:T(8,128)}) custom-call(f32[16,128,128]{2,1,0:T(8,128)S(1)} %get-tuple-element.52.refs_0_, f32[16,2048]{1,0:T(8,128)S(1)} %get-tuple-element.53.refs_2_.refs_4_.refs_5_.refs_1_, f32[1,2048]{1,0:T(1,128)S(1)} %get-tuple-element.54.refs_3_.refs_2_, ...), custom_call_target="tpu_custom_call" | custom-call | tf_op jit(solution)/shard_map/backward_b_0/pallas_call | solution.py:708
  (33 shorter events, 3.9 us)
Async XLA Ops:
  12.7 1.5 %collective-permute-start = (f32[9,16,128]{2,1,0:T(8,128)S(1)}, f32[9,16,128]{2,1,0:T(8,128)S(1)}, u32[]{:S(2)}, u32[]{:S(2)}) collective-permute-start(f32[9,16,128]{2,1,0:T(8,128)S(1)} %get-tuple-element.63), channel_id=1, source_target_pairs={{0,1},{1,0},{2,3},{3,2},{4,5},{5,4},{6,7},{7,6},{8,9},{9,8},{10,11... | collective-permute-start | bytes 221192 | tf_op jit(solution)/shard_map/ppermute | solution.py:566
  14.2 6.5 %collective-permute-start.3 = (f32[9,16,128]{2,1,0:T(8,128)S(1)}, f32[9,16,128]{2,1,0:T(8,128)S(1)}, u32[]{:S(2)}, u32[]{:S(2)}) collective-permute-start(f32[9,16,128]{2,1,0:T(8,128)S(1)} %get-tuple-element.64.refs_0_), channel_id=1, source_target_pairs={{0,6},{1,7},{2,4},{3,5},{4,2},{5,3},{6,0},{7,1},{8,14},{9,15},{10,... | collective-permute-start | bytes 221192 | tf_op jit(solution)/shard_map/ppermute | solution.py:566
  18.0 4.4 %collective-permute-start.2 = (f32[9,16,128]{2,1,0:T(8,128)S(1)}, f32[9,16,128]{2,1,0:T(8,128)S(1)}, u32[]{:S(2)}, u32[]{:S(2)}) collective-permute-start(f32[9,16,128]{2,1,0:T(8,128)S(1)} %get-tuple-element.64.refs_0_), channel_id=1, source_target_pairs={{0,4},{1,5},{2,6},{3,7},{4,0},{5,1},{6,2},{7,3},{8,12},{9,13},{10,... | collective-permute-start | bytes 221192 | tf_op jit(solution)/shard_map/ppermute | solution.py:566
  18.5 4.4 %collective-permute-start.1 = (f32[9,16,128]{2,1,0:T(8,128)S(1)}, f32[9,16,128]{2,1,0:T(8,128)S(1)}, u32[]{:S(2)}, u32[]{:S(2)}) collective-permute-start(f32[9,16,128]{2,1,0:T(8,128)S(1)} %get-tuple-element.64.refs_0_), channel_id=1, source_target_pairs={{0,2},{1,3},{2,0},{3,1},{4,6},{5,7},{6,4},{7,5},{8,10},{9,11},{10,... | collective-permute-start | bytes 221192 | tf_op jit(solution)/shard_map/ppermute | solution.py:566
  23.0 6.5 %collective-permute-start.6 = (f32[9,16,128]{2,1,0:T(8,128)S(1)}, f32[9,16,128]{2,1,0:T(8,128)S(1)}, u32[]{:S(2)}, u32[]{:S(2)}) collective-permute-start(f32[9,16,128]{2,1,0:T(8,128)S(1)} %get-tuple-element.65.refs_0_), channel_id=1, source_target_pairs={{0,24},{1,25},{2,26},{3,27},{4,28},{5,29},{6,30},{7,31},{8,16},{9,... | collective-permute-start | bytes 221192 | tf_op jit(solution)/shard_map/ppermute | solution.py:566
  26.7 5.7 %collective-permute-start.5 = (f32[9,16,128]{2,1,0:T(8,128)S(1)}, f32[9,16,128]{2,1,0:T(8,128)S(1)}, u32[]{:S(2)}, u32[]{:S(2)}) collective-permute-start(f32[9,16,128]{2,1,0:T(8,128)S(1)} %get-tuple-element.65.refs_0_), channel_id=1, source_target_pairs={{0,16},{1,17},{2,18},{3,19},{4,20},{5,21},{6,22},{7,23},{8,24},{9,... | collective-permute-start | bytes 221192 | tf_op jit(solution)/shard_map/ppermute | solution.py:566
  26.7 5.7 %collective-permute-start.4 = (f32[9,16,128]{2,1,0:T(8,128)S(1)}, f32[9,16,128]{2,1,0:T(8,128)S(1)}, u32[]{:S(2)}, u32[]{:S(2)}) collective-permute-start(f32[9,16,128]{2,1,0:T(8,128)S(1)} %get-tuple-element.65.refs_0_), channel_id=1, source_target_pairs={{0,8},{1,9},{2,10},{3,11},{4,12},{5,13},{6,14},{7,15},{8,0},{9,1},... | collective-permute-start | bytes 221192 | tf_op jit(solution)/shard_map/ppermute | solution.py:566
  33.2 1.3 %collective-permute-start.7 = (f32[8,16,128]{2,1,0:T(8,128)S(1)}, f32[8,16,128]{2,1,0:T(8,128)S(1)}, u32[]{:S(2)}, u32[]{:S(2)}) collective-permute-start(f32[8,16,128]{2,1,0:T(8,128)S(1)} %get-tuple-element.70), channel_id=1, source_target_pairs={{0,1},{1,0},{2,3},{3,2},{4,5},{5,4},{6,7},{7,6},{8,9},{9,8},{10,11... | collective-permute-start | bytes 196616 | tf_op jit(solution)/shard_map/ppermute | solution.py:566
  41.0 1.3 %collective-permute-start.8 = (f32[9,16,128]{2,1,0:T(8,128)S(1)}, f32[9,16,128]{2,1,0:T(8,128)S(1)}, u32[]{:S(2)}, u32[]{:S(2)}) collective-permute-start(f32[9,16,128]{2,1,0:T(8,128)S(1)} %get-tuple-element.73), channel_id=1, source_target_pairs={{0,1},{1,0},{2,3},{3,2},{4,5},{5,4},{6,7},{7,6},{8,9},{9,8},{10,11... | collective-permute-start | bytes 221192 | tf_op jit(solution)/shard_map/ppermute | solution.py:566
  42.4 5.4 %collective-permute-start.11 = (f32[9,16,128]{2,1,0:T(8,128)S(1)}, f32[9,16,128]{2,1,0:T(8,128)S(1)}, u32[]{:S(2)}, u32[]{:S(2)}) collective-permute-start(f32[9,16,128]{2,1,0:T(8,128)S(1)} %join_b.1.refs_0_), channel_id=1, source_target_pairs={{0,6},{1,7},{2,4},{3,5},{4,2},{5,3},{6,0},{7,1},{8,14},{9,15},{10,... | collective-permute-start | bytes 221192 | tf_op jit(solution)/shard_map/ppermute | solution.py:566
  43.9 5.3 %collective-permute-start.10 = (f32[9,16,128]{2,1,0:T(8,128)S(1)}, f32[9,16,128]{2,1,0:T(8,128)S(1)}, u32[]{:S(2)}, u32[]{:S(2)}) collective-permute-start(f32[9,16,128]{2,1,0:T(8,128)S(1)} %join_b.1.refs_0_), channel_id=1, source_target_pairs={{0,4},{1,5},{2,6},{3,7},{4,0},{5,1},{6,2},{7,3},{8,12},{9,13},{10,... | collective-permute-start | bytes 221192 | tf_op jit(solution)/shard_map/ppermute | solution.py:566
  45.6 4.4 %collective-permute-start.9 = (f32[9,16,128]{2,1,0:T(8,128)S(1)}, f32[9,16,128]{2,1,0:T(8,128)S(1)}, u32[]{:S(2)}, u32[]{:S(2)}) collective-permute-start(f32[9,16,128]{2,1,0:T(8,128)S(1)} %join_b.1.refs_0_), channel_id=1, source_target_pairs={{0,2},{1,3},{2,0},{3,1},{4,6},{5,7},{6,4},{7,5},{8,10},{9,11},{10,... | collective-permute-start | bytes 221192 | tf_op jit(solution)/shard_map/ppermute | solution.py:566
  50.0 6.4 %collective-permute-start.14 = (f32[9,16,128]{2,1,0:T(8,128)S(1)}, f32[9,16,128]{2,1,0:T(8,128)S(1)}, u32[]{:S(2)}, u32[]{:S(2)}) collective-permute-start(f32[9,16,128]{2,1,0:T(8,128)S(1)} %get-tuple-element.75.refs_0_), channel_id=1, source_target_pairs={{0,24},{1,25},{2,26},{3,27},{4,28},{5,29},{6,30},{7,31},{8,16},{9,... | collective-permute-start | bytes 221192 | tf_op jit(solution)/shard_map/ppermute | solution.py:566
  52.7 6.6 %collective-permute-start.13 = (f32[9,16,128]{2,1,0:T(8,128)S(1)}, f32[9,16,128]{2,1,0:T(8,128)S(1)}, u32[]{:S(2)}, u32[]{:S(2)}) collective-permute-start(f32[9,16,128]{2,1,0:T(8,128)S(1)} %get-tuple-element.75.refs_0_), channel_id=1, source_target_pairs={{0,16},{1,17},{2,18},{3,19},{4,20},{5,21},{6,22},{7,23},{8,24},{9,... | collective-permute-start | bytes 221192 | tf_op jit(solution)/shard_map/ppermute | solution.py:566
  52.7 6.6 %collective-permute-start.12 = (f32[9,16,128]{2,1,0:T(8,128)S(1)}, f32[9,16,128]{2,1,0:T(8,128)S(1)}, u32[]{:S(2)}, u32[]{:S(2)}) collective-permute-start(f32[9,16,128]{2,1,0:T(8,128)S(1)} %get-tuple-element.75.refs_0_), channel_id=1, source_target_pairs={{0,8},{1,9},{2,10},{3,11},{4,12},{5,13},{6,14},{7,15},{8,0},{9,1},... | collective-permute-start | bytes 221192 | tf_op jit(solution)/shard_map/ppermute | solution.py:566
  59.4 1.3 %collective-permute-start.15 = (f32[8,16,128]{2,1,0:T(8,128)S(1)}, f32[8,16,128]{2,1,0:T(8,128)S(1)}, u32[]{:S(2)}, u32[]{:S(2)}) collective-permute-start(f32[8,16,128]{2,1,0:T(8,128)S(1)} %get-tuple-element.79), channel_id=1, source_target_pairs={{0,1},{1,0},{2,3},{3,2},{4,5},{5,4},{6,7},{7,6},{8,9},{9,8},{10,11... | collective-permute-start | bytes 196616 | tf_op jit(solution)/shard_map/ppermute | solution.py:566
  66.9 1.3 %collective-permute-start.16 = (f32[9,16,128]{2,1,0:T(8,128)S(1)}, f32[9,16,128]{2,1,0:T(8,128)S(1)}, u32[]{:S(2)}, u32[]{:S(2)}) collective-permute-start(f32[9,16,128]{2,1,0:T(8,128)S(1)} %get-tuple-element.84), channel_id=1, source_target_pairs={{0,1},{1,0},{2,3},{3,2},{4,5},{5,4},{6,7},{7,6},{8,9},{9,8},{10,11... | collective-permute-start | bytes 221192 | tf_op jit(solution)/shard_map/ppermute | solution.py:566
  68.3 5.4 %collective-permute-start.19 = (f32[9,16,128]{2,1,0:T(8,128)S(1)}, f32[9,16,128]{2,1,0:T(8,128)S(1)}, u32[]{:S(2)}, u32[]{:S(2)}) collective-permute-start(f32[9,16,128]{2,1,0:T(8,128)S(1)} %join_c.1.refs_0_), channel_id=1, source_target_pairs={{0,6},{1,7},{2,4},{3,5},{4,2},{5,3},{6,0},{7,1},{8,14},{9,15},{10,... | collective-permute-start | bytes 221192 | tf_op jit(solution)/shard_map/ppermute | solution.py:566
  69.9 5.3 %collective-permute-start.18 = (f32[9,16,128]{2,1,0:T(8,128)S(1)}, f32[9,16,128]{2,1,0:T(8,128)S(1)}, u32[]{:S(2)}, u32[]{:S(2)}) collective-permute-start(f32[9,16,128]{2,1,0:T(8,128)S(1)} %join_c.1.refs_0_), channel_id=1, source_target_pairs={{0,4},{1,5},{2,6},{3,7},{4,0},{5,1},{6,2},{7,3},{8,12},{9,13},{10,... | collective-permute-start | bytes 221192 | tf_op jit(solution)/shard_map/ppermute | solution.py:566
  71.1 4.4 %collective-permute-start.17 = (f32[9,16,128]{2,1,0:T(8,128)S(1)}, f32[9,16,128]{2,1,0:T(8,128)S(1)}, u32[]{:S(2)}, u32[]{:S(2)}) collective-permute-start(f32[9,16,128]{2,1,0:T(8,128)S(1)} %join_c.1.refs_0_), channel_id=1, source_target_pairs={{0,2},{1,3},{2,0},{3,1},{4,6},{5,7},{6,4},{7,5},{8,10},{9,11},{10,... | collective-permute-start | bytes 221192 | tf_op jit(solution)/shard_map/ppermute | solution.py:566
  75.5 7.0 %collective-permute-start.22 = (f32[9,16,128]{2,1,0:T(8,128)S(1)}, f32[9,16,128]{2,1,0:T(8,128)S(1)}, u32[]{:S(2)}, u32[]{:S(2)}) collective-permute-start(f32[9,16,128]{2,1,0:T(8,128)S(1)} %get-tuple-element.85.refs_0_), channel_id=1, source_target_pairs={{0,24},{1,25},{2,26},{3,27},{4,28},{5,29},{6,30},{7,31},{8,16},{9,... | collective-permute-start | bytes 221192 | tf_op jit(solution)/shard_map/ppermute | solution.py:566
  77.8 6.8 %collective-permute-start.21 = (f32[9,16,128]{2,1,0:T(8,128)S(1)}, f32[9,16,128]{2,1,0:T(8,128)S(1)}, u32[]{:S(2)}, u32[]{:S(2)}) collective-permute-start(f32[9,16,128]{2,1,0:T(8,128)S(1)} %get-tuple-element.85.refs_0_), channel_id=1, source_target_pairs={{0,16},{1,17},{2,18},{3,19},{4,20},{5,21},{6,22},{7,23},{8,24},{9,... | collective-permute-start | bytes 221192 | tf_op jit(solution)/shard_map/ppermute | solution.py:566
  77.8 6.8 %collective-permute-start.20 = (f32[9,16,128]{2,1,0:T(8,128)S(1)}, f32[9,16,128]{2,1,0:T(8,128)S(1)}, u32[]{:S(2)}, u32[]{:S(2)}) collective-permute-start(f32[9,16,128]{2,1,0:T(8,128)S(1)} %get-tuple-element.85.refs_0_), channel_id=1, source_target_pairs={{0,8},{1,9},{2,10},{3,11},{4,12},{5,13},{6,14},{7,15},{8,0},{9,1},... | collective-permute-start | bytes 221192 | tf_op jit(solution)/shard_map/ppermute | solution.py:566
  84.7 1.3 %collective-permute-start.23 = (f32[8,16,128]{2,1,0:T(8,128)S(1)}, f32[8,16,128]{2,1,0:T(8,128)S(1)}, u32[]{:S(2)}, u32[]{:S(2)}) collective-permute-start(f32[8,16,128]{2,1,0:T(8,128)S(1)} %get-tuple-element.88), channel_id=1, source_target_pairs={{0,1},{1,0},{2,3},{3,2},{4,5},{5,4},{6,7},{7,6},{8,9},{9,8},{10,11... | collective-permute-start | bytes 196616 | tf_op jit(solution)/shard_map/ppermute | solution.py:566
  92.8 1.3 %collective-permute-start.24 = (f32[9,16,128]{2,1,0:T(8,128)S(1)}, f32[9,16,128]{2,1,0:T(8,128)S(1)}, u32[]{:S(2)}, u32[]{:S(2)}) collective-permute-start(f32[9,16,128]{2,1,0:T(8,128)S(1)} %get-tuple-element.94), channel_id=1, source_target_pairs={{0,1},{1,0},{2,3},{3,2},{4,5},{5,4},{6,7},{7,6},{8,9},{9,8},{10,11... | collective-permute-start | bytes 221192 | tf_op jit(solution)/shard_map/ppermute | solution.py:566
  94.2 5.4 %collective-permute-start.27 = (f32[9,16,128]{2,1,0:T(8,128)S(1)}, f32[9,16,128]{2,1,0:T(8,128)S(1)}, u32[]{:S(2)}, u32[]{:S(2)}) collective-permute-start(f32[9,16,128]{2,1,0:T(8,128)S(1)} %join_d.1.refs_0_), channel_id=1, source_target_pairs={{0,6},{1,7},{2,4},{3,5},{4,2},{5,3},{6,0},{7,1},{8,14},{9,15},{10,... | collective-permute-start | bytes 221192 | tf_op jit(solution)/shard_map/ppermute | solution.py:566
  95.8 5.2 %collective-permute-start.26 = (f32[9,16,128]{2,1,0:T(8,128)S(1)}, f32[9,16,128]{2,1,0:T(8,128)S(1)}, u32[]{:S(2)}, u32[]{:S(2)}) collective-permute-start(f32[9,16,128]{2,1,0:T(8,128)S(1)} %join_d.1.refs_0_), channel_id=1, source_target_pairs={{0,4},{1,5},{2,6},{3,7},{4,0},{5,1},{6,2},{7,3},{8,12},{9,13},{10,... | collective-permute-start | bytes 221192 | tf_op jit(solution)/shard_map/ppermute | solution.py:566
  96.8 4.4 %collective-permute-start.25 = (f32[9,16,128]{2,1,0:T(8,128)S(1)}, f32[9,16,128]{2,1,0:T(8,128)S(1)}, u32[]{:S(2)}, u32[]{:S(2)}) collective-permute-start(f32[9,16,128]{2,1,0:T(8,128)S(1)} %join_d.1.refs_0_), channel_id=1, source_target_pairs={{0,2},{1,3},{2,0},{3,1},{4,6},{5,7},{6,4},{7,5},{8,10},{9,11},{10,... | collective-permute-start | bytes 221192 | tf_op jit(solution)/shard_map/ppermute | solution.py:566
  101.2 7.0 %collective-permute-start.30 = (f32[9,16,128]{2,1,0:T(8,128)S(1)}, f32[9,16,128]{2,1,0:T(8,128)S(1)}, u32[]{:S(2)}, u32[]{:S(2)}) collective-permute-start(f32[9,16,128]{2,1,0:T(8,128)S(1)} %get-tuple-element.95.refs_0_), channel_id=1, source_target_pairs={{0,24},{1,25},{2,26},{3,27},{4,28},{5,29},{6,30},{7,31},{8,16},{9,... | collective-permute-start | bytes 221192 | tf_op jit(solution)/shard_map/ppermute | solution.py:566
  103.6 6.8 %collective-permute-start.29 = (f32[9,16,128]{2,1,0:T(8,128)S(1)}, f32[9,16,128]{2,1,0:T(8,128)S(1)}, u32[]{:S(2)}, u32[]{:S(2)}) collective-permute-start(f32[9,16,128]{2,1,0:T(8,128)S(1)} %get-tuple-element.95.refs_0_), channel_id=1, source_target_pairs={{0,16},{1,17},{2,18},{3,19},{4,20},{5,21},{6,22},{7,23},{8,24},{9,... | collective-permute-start | bytes 221192 | tf_op jit(solution)/shard_map/ppermute | solution.py:566
  103.6 6.8 %collective-permute-start.28 = (f32[9,16,128]{2,1,0:T(8,128)S(1)}, f32[9,16,128]{2,1,0:T(8,128)S(1)}, u32[]{:S(2)}, u32[]{:S(2)}) collective-permute-start(f32[9,16,128]{2,1,0:T(8,128)S(1)} %get-tuple-element.95.refs_0_), channel_id=1, source_target_pairs={{0,8},{1,9},{2,10},{3,11},{4,12},{5,13},{6,14},{7,15},{8,0},{9,1},... | collective-permute-start | bytes 221192 | tf_op jit(solution)/shard_map/ppermute | solution.py:566
  110.4 1.3 %collective-permute-start.31 = (f32[8,16,128]{2,1,0:T(8,128)S(1)}, f32[8,16,128]{2,1,0:T(8,128)S(1)}, u32[]{:S(2)}, u32[]{:S(2)}) collective-permute-start(f32[8,16,128]{2,1,0:T(8,128)S(1)} %get-tuple-element.98), channel_id=1, source_target_pairs={{0,1},{1,0},{2,3},{3,2},{4,5},{5,4},{6,7},{7,6},{8,9},{9,8},{10,11... | collective-permute-start | bytes 196616 | tf_op jit(solution)/shard_map/ppermute | solution.py:566

commit v5 on v4

--- a/solution.py
+++ b/solution.py
@@ -86,8 +86,16 @@
 
 def write_state(s, both_ref, block, rows_of):
     slot, place = place_of(s, block)
-    for n, value in enumerate(rows_of):
-        both_ref[slot, place, n : n + 1, :] = value
+    if not isinstance(both_ref, tuple):
+        for n, value in enumerate(rows_of):
+            both_ref[slot, place, n : n + 1, :] = value
+        return
+    for index, ref in enumerate(both_ref):
+
+        @pl.when(slot == index)
+        def _(ref=ref):
+            for n, value in enumerate(rows_of):
+                ref[place, n : n + 1, :] = value
 
 
 def over_blocks(s, scans, body, carry):
@@ -138,9 +146,10 @@
         low_scan, high_scan, cx_ref, total_ref, e_ref, keep_ref, give_ref,
         rhs_ref, curv_ref, rate_ref, skip_ref, damp_ref,
     ) = refs[8:20]
-    delta_ref, bx_ref, wide_ref, turn_ref, sem_d, sem_v, sem_c, sem_s, put = refs[20:]
-    for slot in (0, 1):
-        put[slot, s.half] = jnp.zeros((s.entries, LANE), F32)
+    delta_ref, bx_ref, wide_ref, turn_ref, sem_d, sem_v, sem_c, sem_s = refs[20:]
+    put = keep_ref, give_ref
+    for ref in put:
+        ref[s.half] = jnp.zeros((s.entries, LANE), F32)
 
     small = [
         pltpu.make_async_copy(src, dst, sem_s.at[i])
@@ -204,11 +213,15 @@
         finish_summary(s, block, state, rates, total, e_ref, put, False)
         whole = jnp.sum(total, axis=0, keepdims=True)
         slot, row = place_of(s, block)
-        put[slot, s.half, pl.ds(row, 1), :] = whole
+        for index, ref in enumerate(put):
+
+            @pl.when(slot == index)
+            def _(ref=ref):
+                ref[s.half, pl.ds(row, 1), :] = whole
+
         return carry
 
     over_blocks(s, (low_scan, high_scan), body, 0)
-    part_packets(put, keep_ref, give_ref)
     small[3].wait()
     small[4].wait()
 
@@ -584,7 +597,6 @@
                 pltpu.VMEM((2, entries, tokens), F32),
                 pltpu.VMEM((2, tokens, entries), F32),
                 dma((s.blocks,)), dma((s.blocks,)), dma((s.blocks,)), dma((5,)),
-                both,
             ],
             [
                 in_hbm(x)

time: 117 us -> 115 us (0.983)
  Pallas kernels: 38.1 us -> 36.4 us
    pallas_call x16, Pallas kernels: 33.2 us -> 31.6 us  [call(): pl.pallas_call(body, name=name, out_shape=outs, in_specs=[HBM] * n_hbm +...]
where the time goes in v5:
time: 115 us
  waiting for transfers between devices  43.6 us (38%)
  Pallas kernels  36.4 us (32%)
  starting transfers between devices  34.2 us (30%)
    ppermute x32, waiting for transfers between devices, swap(): return lax.ppermute(send, 'seq', pairs)  43.6 us
    ppermute x32, starting transfers between devices, swap(): return lax.ppermute(send, 'seq', pairs)  34.2 us
    pallas_call x16, Pallas kernels, call(): pl.pallas_call(body, name=name, out_shape=outs, in_specs=[HBM] * n_hbm +...  31.6 us
    pallas_call x1, Pallas kernels, per_device(): pl.pallas_call(kernel(last_kernel, offsets[g]), name=f'backward_b_{g}', o...  4.84 us
  transfers between devices with their start and end apart: 32, of which 28 were waited for; matrix products, arithmetic and copies ran while one was open for 0% of the time, Pallas kernels for 0%

profile of v5, /device:TPU:0, one launch (start us, length us, event | category | flops | bytes accessed | tf_op | source)
XLA Modules:
  0.0 114.9 jit_solution(11644989482924681825)
XLA Ops:
  0.6 10.4 %first_0.1 = (f32[8,16,16,2,8,128]{5,4,3,2,1,0:T(8,128)S(1)}, f32[8,16,16,2,8,128]{5,4,3,2,1,0:T(8,128)S(1)}, f32[16,16,8,128]{3,2,1,0:T(8,128)S(1)}, f32[16,8,1...) custom-call(f32[128,2048]{1,0:T(8,128)} %refs_0_.1, ...), custom_call_target="tpu_custom_call" | custom-call | flops 8388608 | bytes 8388608 | tf_op jit(solution)/shard_map/first_0/pallas_call | solution.py:544
  11.6 0.9 collective-permute-done.refs_1_.refs_8_
  12.6 3.8 %collective-permute-start.3 = (f32[9,16,128]{2,1,0:T(8,128)S(1)}, f32[9,16,128]{2,1,0:T(8,128)S(1)}, u32[]{:S(2)}, u32[]{:S(2)}) collective-permute-start(f32[9,16,128]{2,1,0:T(8,128)S(1)} %get-tuple-element.64.refs_0_), channel_id=1, source_target_pairs={{0,6},{1,7},{2,4},{3,5},{4,2},{5,3},{6,0},{7,1},{8,14},{9,15},{10,... | collective-permute-start | bytes 221192 | tf_op jit(solution)/shard_map/ppermute | solution.py:579
  17.0 2.0 %collective-permute-done.3.refs_3_ = f32[9,16,128]{2,1,0:T(8,128)S(1)} collective-permute-done((f32[9,16,128]{2,1,0:T(8,128)S(1)}, f32[9,16,128]{2,1,0:T(8,128)S(1)}, u32[]{:S(2)}, u32[]{:S(2)}) %collective-permute-start.3) | collective-permute-done | bytes 73760 | tf_op jit(solution)/shard_map/ppermute | solution.py:579
  19.1 1.7 %collective-permute-done.2.refs_2_ = f32[9,16,128]{2,1,0:T(8,128)S(1)} collective-permute-done((f32[9,16,128]{2,1,0:T(8,128)S(1)}, f32[9,16,128]{2,1,0:T(8,128)S(1)}, u32[]{:S(2)}, u32[]{:S(2)}) %collective-permute-start.2) | collective-permute-done | bytes 73760 | tf_op jit(solution)/shard_map/ppermute | solution.py:579
  21.4 3.7 %collective-permute-start.6 = (f32[9,16,128]{2,1,0:T(8,128)S(1)}, f32[9,16,128]{2,1,0:T(8,128)S(1)}, u32[]{:S(2)}, u32[]{:S(2)}) collective-permute-start(f32[9,16,128]{2,1,0:T(8,128)S(1)} %get-tuple-element.65.refs_0_), channel_id=1, source_target_pairs={{0,24},{1,25},{2,26},{3,27},{4,28},{5,29},{6,30},{7,31},{8,16},{9,... | collective-permute-start | bytes 221192 | tf_op jit(solution)/shard_map/ppermute | solution.py:579
  25.1 0.8 collective-permute-start.4
  25.9 2.0 %collective-permute-done.6.refs_3_ = f32[9,16,128]{2,1,0:T(8,128)S(1)} collective-permute-done((f32[9,16,128]{2,1,0:T(8,128)S(1)}, f32[9,16,128]{2,1,0:T(8,128)S(1)}, u32[]{:S(2)}, u32[]{:S(2)}) %collective-permute-start.6) | collective-permute-done | bytes 73760 | tf_op jit(solution)/shard_map/ppermute | solution.py:579
  27.9 2.9 %collective-permute-done.5.refs_2_ = f32[9,16,128]{2,1,0:T(8,128)S(1)} collective-permute-done((f32[9,16,128]{2,1,0:T(8,128)S(1)}, f32[9,16,128]{2,1,0:T(8,128)S(1)}, u32[]{:S(2)}, u32[]{:S(2)}) %collective-permute-start.5) | collective-permute-done | bytes 73760 | tf_op jit(solution)/shard_map/ppermute | solution.py:579
  30.8 0.8 level_1_a.1
  31.6 1.3 %collective-permute-done.7.refs_11_ = f32[8,16,128]{2,1,0:T(8,128)S(1)} collective-permute-done((f32[8,16,128]{2,1,0:T(8,128)S(1)}, f32[8,16,128]{2,1,0:T(8,128)S(1)}, u32[]{:S(2)}, u32[]{:S(2)}) %collective-permute-start.7) | collective-permute-done | bytes 65568 | tf_op jit(solution)/shard_map/ppermute | solution.py:579
  32.8 6.6 %forward_a_0.1 = (f32[16,16,8,128]{3,2,1,0:T(8,128)S(1)}, f32[9,16,128]{2,1,0:T(8,128)S(1)}, f32[9,16,128]{2,1,0:T(8,128)S(1)}, f32[16,16,8,128]{3,2,1,0:T(8,128)S(1)}, f32[16,16,8,128]{3,2,1,0:T(8,128)S(1)}) custom-call(f32[16,128,128]{2,1,0:T(8,128)S(1)} %get-tuple-element.52.refs_0_, f32[16,128,128]{2,1,0:T(8,128)S(1)} %get-tuple-element.60.refs_1_, ...), custom_call_target="tpu_custom_call" | custom-call | flops 8388608 | bytes 8388608 | tf_op jit(solution)/shard_map/forward_a_0/pallas_call | solution.py:544
  39.6 1.1 collective-permute-done.8.refs_1_.refs_7_
  40.8 1.6 %collective-permute-start.11 = (f32[9,16,128]{2,1,0:T(8,128)S(1)}, f32[9,16,128]{2,1,0:T(8,128)S(1)}, u32[]{:S(2)}, u32[]{:S(2)}) collective-permute-start(f32[9,16,128]{2,1,0:T(8,128)S(1)} %join_b.1.refs_0_), channel_id=1, source_target_pairs={{0,6},{1,7},{2,4},{3,5},{4,2},{5,3},{6,0},{7,1},{8,14},{9,15},{10,... | collective-permute-start | bytes 221192 | tf_op jit(solution)/shard_map/ppermute | solution.py:579
  42.3 1.7 %collective-permute-start.10 = (f32[9,16,128]{2,1,0:T(8,128)S(1)}, f32[9,16,128]{2,1,0:T(8,128)S(1)}, u32[]{:S(2)}, u32[]{:S(2)}) collective-permute-start(f32[9,16,128]{2,1,0:T(8,128)S(1)} %join_b.1.refs_0_), channel_id=1, source_target_pairs={{0,4},{1,5},{2,6},{3,7},{4,0},{5,1},{6,2},{7,3},{8,12},{9,13},{10,... | collective-permute-start | bytes 221192 | tf_op jit(solution)/shard_map/ppermute | solution.py:579
  44.3 1.9 %collective-permute-done.11.refs_3_ = f32[9,16,128]{2,1,0:T(8,128)S(1)} collective-permute-done((f32[9,16,128]{2,1,0:T(8,128)S(1)}, f32[9,16,128]{2,1,0:T(8,128)S(1)}, u32[]{:S(2)}, u32[]{:S(2)}) %collective-permute-start.11) | collective-permute-done | bytes 73760 | tf_op jit(solution)/shard_map/ppermute | solution.py:579
  46.2 1.4 %collective-permute-done.10.refs_2_ = f32[9,16,128]{2,1,0:T(8,128)S(1)} collective-permute-done((f32[9,16,128]{2,1,0:T(8,128)S(1)}, f32[9,16,128]{2,1,0:T(8,128)S(1)}, u32[]{:S(2)}, u32[]{:S(2)}) %collective-permute-start.10) | collective-permute-done | bytes 73760 | tf_op jit(solution)/shard_map/ppermute | solution.py:579
  47.6 0.7 collective-permute-done.9.refs_1_
  48.4 2.7 %collective-permute-start.14 = (f32[9,16,128]{2,1,0:T(8,128)S(1)}, f32[9,16,128]{2,1,0:T(8,128)S(1)}, u32[]{:S(2)}, u32[]{:S(2)}) collective-permute-start(f32[9,16,128]{2,1,0:T(8,128)S(1)} %get-tuple-element.75.refs_0_), channel_id=1, source_target_pairs={{0,24},{1,25},{2,26},{3,27},{4,28},{5,29},{6,30},{7,31},{8,16},{9,... | collective-permute-start | bytes 221192 | tf_op jit(solution)/shard_map/ppermute | solution.py:579
  51.1 1.8 %collective-permute-start.12 = (f32[9,16,128]{2,1,0:T(8,128)S(1)}, f32[9,16,128]{2,1,0:T(8,128)S(1)}, u32[]{:S(2)}, u32[]{:S(2)}) collective-permute-start(f32[9,16,128]{2,1,0:T(8,128)S(1)} %get-tuple-element.75.refs_0_), channel_id=1, source_target_pairs={{0,8},{1,9},{2,10},{3,11},{4,12},{5,13},{6,14},{7,15},{8,0},{9,1},... | collective-permute-start | bytes 221192 | tf_op jit(solution)/shard_map/ppermute | solution.py:579
  52.8 1.9 %collective-permute-done.14.refs_3_ = f32[9,16,128]{2,1,0:T(8,128)S(1)} collective-permute-done((f32[9,16,128]{2,1,0:T(8,128)S(1)}, f32[9,16,128]{2,1,0:T(8,128)S(1)}, u32[]{:S(2)}, u32[]{:S(2)}) %collective-permute-start.14) | collective-permute-done | bytes 73760 | tf_op jit(solution)/shard_map/ppermute | solution.py:579
  54.8 2.9 %collective-permute-done.13.refs_2_ = f32[9,16,128]{2,1,0:T(8,128)S(1)} collective-permute-done((f32[9,16,128]{2,1,0:T(8,128)S(1)}, f32[9,16,128]{2,1,0:T(8,128)S(1)}, u32[]{:S(2)}, u32[]{:S(2)}) %collective-permute-start.13) | collective-permute-done | bytes 73760 | tf_op jit(solution)/shard_map/ppermute | solution.py:579
  57.8 1.2 %collective-permute-done.15.refs_10_ = f32[8,16,128]{2,1,0:T(8,128)S(1)} collective-permute-done((f32[8,16,128]{2,1,0:T(8,128)S(1)}, f32[8,16,128]{2,1,0:T(8,128)S(1)}, u32[]{:S(2)}, u32[]{:S(2)}) %collective-permute-start.15) | collective-permute-done | bytes 65568 | tf_op jit(solution)/shard_map/ppermute | solution.py:579
  59.1 6.3 %backward_a_0.1 = (f32[16,16,8,128]{3,2,1,0:T(8,128)S(1)}, f32[9,16,128]{2,1,0:T(8,128)S(1)}, f32[9,16,128]{2,1,0:T(8,128)S(1)}, f32[16,16,8,128]{3,2,1,0:T(8,128)S(1)}) custom-call(f32[16,128,128]{2,1,0:T(8,128)S(1)} %get-tuple-element.52.refs_0_, f32[16,2048]{1,0:T(8,128)S(1)} %get-tuple-element.53.refs_2_.refs_4_.refs_5_.refs_1_, ...), custom_call_target="tpu_custom_call" | custom-call | flops 8388608 | bytes 8388608 | tf_op jit(solution)/shard_map/backward_a_0/pallas_call | solution.py:544
  65.6 1.1 collective-permute-done.16.refs_1_.refs_7_
  66.7 1.6 %collective-permute-start.19 = (f32[9,16,128]{2,1,0:T(8,128)S(1)}, f32[9,16,128]{2,1,0:T(8,128)S(1)}, u32[]{:S(2)}, u32[]{:S(2)}) collective-permute-start(f32[9,16,128]{2,1,0:T(8,128)S(1)} %join_c.1.refs_0_), channel_id=1, source_target_pairs={{0,6},{1,7},{2,4},{3,5},{4,2},{5,3},{6,0},{7,1},{8,14},{9,15},{10,... | collective-permute-start | bytes 221192 | tf_op jit(solution)/shard_map/ppermute | solution.py:579
  68.3 1.2 %collective-permute-start.18 = (f32[9,16,128]{2,1,0:T(8,128)S(1)}, f32[9,16,128]{2,1,0:T(8,128)S(1)}, u32[]{:S(2)}, u32[]{:S(2)}) collective-permute-start(f32[9,16,128]{2,1,0:T(8,128)S(1)} %join_c.1.refs_0_), channel_id=1, source_target_pairs={{0,4},{1,5},{2,6},{3,7},{4,0},{5,1},{6,2},{7,3},{8,12},{9,13},{10,... | collective-permute-start | bytes 221192 | tf_op jit(solution)/shard_map/ppermute | solution.py:579
  69.5 0.8 collective-permute-start.17
  70.3 1.9 %collective-permute-done.19.refs_3_ = f32[9,16,128]{2,1,0:T(8,128)S(1)} collective-permute-done((f32[9,16,128]{2,1,0:T(8,128)S(1)}, f32[9,16,128]{2,1,0:T(8,128)S(1)}, u32[]{:S(2)}, u32[]{:S(2)}) %collective-permute-start.19) | collective-permute-done | bytes 73760 | tf_op jit(solution)/shard_map/ppermute | solution.py:579
  72.1 1.4 %collective-permute-done.18.refs_2_ = f32[9,16,128]{2,1,0:T(8,128)S(1)} collective-permute-done((f32[9,16,128]{2,1,0:T(8,128)S(1)}, f32[9,16,128]{2,1,0:T(8,128)S(1)}, u32[]{:S(2)}, u32[]{:S(2)}) %collective-permute-start.18) | collective-permute-done | bytes 73760 | tf_op jit(solution)/shard_map/ppermute | solution.py:579
  73.9 2.3 %collective-permute-start.22 = (f32[9,16,128]{2,1,0:T(8,128)S(1)}, f32[9,16,128]{2,1,0:T(8,128)S(1)}, u32[]{:S(2)}, u32[]{:S(2)}) collective-permute-start(f32[9,16,128]{2,1,0:T(8,128)S(1)} %get-tuple-element.85.refs_0_), channel_id=1, source_target_pairs={{0,24},{1,25},{2,26},{3,27},{4,28},{5,29},{6,30},{7,31},{8,16},{9,... | collective-permute-start | bytes 221192 | tf_op jit(solution)/shard_map/ppermute | solution.py:579
  76.2 2.1 %collective-permute-start.20 = (f32[9,16,128]{2,1,0:T(8,128)S(1)}, f32[9,16,128]{2,1,0:T(8,128)S(1)}, u32[]{:S(2)}, u32[]{:S(2)}) collective-permute-start(f32[9,16,128]{2,1,0:T(8,128)S(1)} %get-tuple-element.85.refs_0_), channel_id=1, source_target_pairs={{0,8},{1,9},{2,10},{3,11},{4,12},{5,13},{6,14},{7,15},{8,0},{9,1},... | collective-permute-start | bytes 221192 | tf_op jit(solution)/shard_map/ppermute | solution.py:579
  78.3 2.6 %collective-permute-done.22.refs_3_ = f32[9,16,128]{2,1,0:T(8,128)S(1)} collective-permute-done((f32[9,16,128]{2,1,0:T(8,128)S(1)}, f32[9,16,128]{2,1,0:T(8,128)S(1)}, u32[]{:S(2)}, u32[]{:S(2)}) %collective-permute-start.22) | collective-permute-done | bytes 73760 | tf_op jit(solution)/shard_map/ppermute | solution.py:579
  80.9 2.1 %collective-permute-done.21.refs_2_ = f32[9,16,128]{2,1,0:T(8,128)S(1)} collective-permute-done((f32[9,16,128]{2,1,0:T(8,128)S(1)}, f32[9,16,128]{2,1,0:T(8,128)S(1)}, u32[]{:S(2)}, u32[]{:S(2)}) %collective-permute-start.21) | collective-permute-done | bytes 73760 | tf_op jit(solution)/shard_map/ppermute | solution.py:579
  83.1 1.2 %collective-permute-done.23.refs_11_ = f32[8,16,128]{2,1,0:T(8,128)S(1)} collective-permute-done((f32[8,16,128]{2,1,0:T(8,128)S(1)}, f32[8,16,128]{2,1,0:T(8,128)S(1)}, u32[]{:S(2)}, u32[]{:S(2)}) %collective-permute-start.23) | collective-permute-done | bytes 65568 | tf_op jit(solution)/shard_map/ppermute | solution.py:579
  84.4 6.8 %forward_b_0.1 = (f32[16,16,8,128]{3,2,1,0:T(8,128)S(1)}, f32[9,16,128]{2,1,0:T(8,128)S(1)}, f32[9,16,128]{2,1,0:T(8,128)S(1)}, f32[16,16,8,128]{3,2,1,0:T(8,128)S(1)}, f32[16,16,8,128]{3,2,1,0:T(8,128)S(1)}) custom-call(f32[16,128,128]{2,1,0:T(8,128)S(1)} %get-tuple-element.52.refs_0_, f32[16,128,128]{2,1,0:T(8,128)S(1)} %get-tuple-element.60.refs_1_, ...), custom_call_target="tpu_custom_call" | custom-call | flops 8388608 | bytes 8388608 | tf_op jit(solution)/shard_map/forward_b_0/pallas_call | solution.py:544
  91.4 1.1 collective-permute-done.24.refs_1_.refs_7_
  92.6 1.6 %collective-permute-start.27 = (f32[9,16,128]{2,1,0:T(8,128)S(1)}, f32[9,16,128]{2,1,0:T(8,128)S(1)}, u32[]{:S(2)}, u32[]{:S(2)}) collective-permute-start(f32[9,16,128]{2,1,0:T(8,128)S(1)} %join_d.1.refs_0_), channel_id=1, source_target_pairs={{0,6},{1,7},{2,4},{3,5},{4,2},{5,3},{6,0},{7,1},{8,14},{9,15},{10,... | collective-permute-start | bytes 221192 | tf_op jit(solution)/shard_map/ppermute | solution.py:579
  94.2 1.0 collective-permute-start.26
  95.2 0.9 collective-permute-start.25
  96.1 1.8 %collective-permute-done.27.refs_3_ = f32[9,16,128]{2,1,0:T(8,128)S(1)} collective-permute-done((f32[9,16,128]{2,1,0:T(8,128)S(1)}, f32[9,16,128]{2,1,0:T(8,128)S(1)}, u32[]{:S(2)}, u32[]{:S(2)}) %collective-permute-start.27) | collective-permute-done | bytes 73760 | tf_op jit(solution)/shard_map/ppermute | solution.py:579
  98.0 1.5 %collective-permute-done.26.refs_2_ = f32[9,16,128]{2,1,0:T(8,128)S(1)} collective-permute-done((f32[9,16,128]{2,1,0:T(8,128)S(1)}, f32[9,16,128]{2,1,0:T(8,128)S(1)}, u32[]{:S(2)}, u32[]{:S(2)}) %collective-permute-start.26) | collective-permute-done | bytes 73760 | tf_op jit(solution)/shard_map/ppermute | solution.py:579
  99.6 2.3 %collective-permute-start.30 = (f32[9,16,128]{2,1,0:T(8,128)S(1)}, f32[9,16,128]{2,1,0:T(8,128)S(1)}, u32[]{:S(2)}, u32[]{:S(2)}) collective-permute-start(f32[9,16,128]{2,1,0:T(8,128)S(1)} %get-tuple-element.95.refs_0_), channel_id=1, source_target_pairs={{0,24},{1,25},{2,26},{3,27},{4,28},{5,29},{6,30},{7,31},{8,16},{9,... | collective-permute-start | bytes 221192 | tf_op jit(solution)/shard_map/ppermute | solution.py:579
  101.9 2.1 %collective-permute-start.28 = (f32[9,16,128]{2,1,0:T(8,128)S(1)}, f32[9,16,128]{2,1,0:T(8,128)S(1)}, u32[]{:S(2)}, u32[]{:S(2)}) collective-permute-start(f32[9,16,128]{2,1,0:T(8,128)S(1)} %get-tuple-element.95.refs_0_), channel_id=1, source_target_pairs={{0,8},{1,9},{2,10},{3,11},{4,12},{5,13},{6,14},{7,15},{8,0},{9,1},... | collective-permute-start | bytes 221192 | tf_op jit(solution)/shard_map/ppermute | solution.py:579
  104.1 2.6 %collective-permute-done.30.refs_3_ = f32[9,16,128]{2,1,0:T(8,128)S(1)} collective-permute-done((f32[9,16,128]{2,1,0:T(8,128)S(1)}, f32[9,16,128]{2,1,0:T(8,128)S(1)}, u32[]{:S(2)}, u32[]{:S(2)}) %collective-permute-start.30) | collective-permute-done | bytes 73760 | tf_op jit(solution)/shard_map/ppermute | solution.py:579
  106.6 2.1 %collective-permute-done.29.refs_2_ = f32[9,16,128]{2,1,0:T(8,128)S(1)} collective-permute-done((f32[9,16,128]{2,1,0:T(8,128)S(1)}, f32[9,16,128]{2,1,0:T(8,128)S(1)}, u32[]{:S(2)}, u32[]{:S(2)}) %collective-permute-start.29) | collective-permute-done | bytes 73760 | tf_op jit(solution)/shard_map/ppermute | solution.py:579
  108.8 1.2 %collective-permute-done.31.refs_10_ = f32[8,16,128]{2,1,0:T(8,128)S(1)} collective-permute-done((f32[8,16,128]{2,1,0:T(8,128)S(1)}, f32[8,16,128]{2,1,0:T(8,128)S(1)}, u32[]{:S(2)}, u32[]{:S(2)}) %collective-permute-start.31) | collective-permute-done | bytes 65568 | tf_op jit(solution)/shard_map/ppermute | solution.py:579
  110.1 4.8 %backward_b_0.1 = (f32[128,2048]{1,0:T(8,128)}, f32[128,2048]{1,0:T(8,128)}) custom-call(f32[16,128,128]{2,1,0:T(8,128)S(1)} %get-tuple-element.52.refs_0_, f32[16,2048]{1,0:T(8,128)S(1)} %get-tuple-element.53.refs_2_.refs_4_.refs_5_.refs_1_, f32[1,2048]{1,0:T(1,128)S(1)} %get-tuple-element.54.refs_3_.refs_2_, ...), custom_call_target="tpu_custom_call" | custom-call | tf_op jit(solution)/shard_map/backward_b_0/pallas_call | solution.py:720
  (33 shorter events, 3.9 us)
Async XLA Ops:
  11.0 1.5 %collective-permute-start = (f32[9,16,128]{2,1,0:T(8,128)S(1)}, f32[9,16,128]{2,1,0:T(8,128)S(1)}, u32[]{:S(2)}, u32[]{:S(2)}) collective-permute-start(f32[9,16,128]{2,1,0:T(8,128)S(1)} %get-tuple-element.63), channel_id=1, source_target_pairs={{0,1},{1,0},{2,3},{3,2},{4,5},{5,4},{6,7},{7,6},{8,9},{9,8},{10,11... | collective-permute-start | bytes 221192 | tf_op jit(solution)/shard_map/ppermute | solution.py:579
  12.6 6.5 %collective-permute-start.3 = (f32[9,16,128]{2,1,0:T(8,128)S(1)}, f32[9,16,128]{2,1,0:T(8,128)S(1)}, u32[]{:S(2)}, u32[]{:S(2)}) collective-permute-start(f32[9,16,128]{2,1,0:T(8,128)S(1)} %get-tuple-element.64.refs_0_), channel_id=1, source_target_pairs={{0,6},{1,7},{2,4},{3,5},{4,2},{5,3},{6,0},{7,1},{8,14},{9,15},{10,... | collective-permute-start | bytes 221192 | tf_op jit(solution)/shard_map/ppermute | solution.py:579
  16.4 4.4 %collective-permute-start.2 = (f32[9,16,128]{2,1,0:T(8,128)S(1)}, f32[9,16,128]{2,1,0:T(8,128)S(1)}, u32[]{:S(2)}, u32[]{:S(2)}) collective-permute-start(f32[9,16,128]{2,1,0:T(8,128)S(1)} %get-tuple-element.64.refs_0_), channel_id=1, source_target_pairs={{0,4},{1,5},{2,6},{3,7},{4,0},{5,1},{6,2},{7,3},{8,12},{9,13},{10,... | collective-permute-start | bytes 221192 | tf_op jit(solution)/shard_map/ppermute | solution.py:579
  16.9 4.4 %collective-permute-start.1 = (f32[9,16,128]{2,1,0:T(8,128)S(1)}, f32[9,16,128]{2,1,0:T(8,128)S(1)}, u32[]{:S(2)}, u32[]{:S(2)}) collective-permute-start(f32[9,16,128]{2,1,0:T(8,128)S(1)} %get-tuple-element.64.refs_0_), channel_id=1, source_target_pairs={{0,2},{1,3},{2,0},{3,1},{4,6},{5,7},{6,4},{7,5},{8,10},{9,11},{10,... | collective-permute-start | bytes 221192 | tf_op jit(solution)/shard_map/ppermute | solution.py:579
  21.4 6.5 %collective-permute-start.6 = (f32[9,16,128]{2,1,0:T(8,128)S(1)}, f32[9,16,128]{2,1,0:T(8,128)S(1)}, u32[]{:S(2)}, u32[]{:S(2)}) collective-permute-start(f32[9,16,128]{2,1,0:T(8,128)S(1)} %get-tuple-element.65.refs_0_), channel_id=1, source_target_pairs={{0,24},{1,25},{2,26},{3,27},{4,28},{5,29},{6,30},{7,31},{8,16},{9,... | collective-permute-start | bytes 221192 | tf_op jit(solution)/shard_map/ppermute | solution.py:579
  25.1 5.7 %collective-permute-start.5 = (f32[9,16,128]{2,1,0:T(8,128)S(1)}, f32[9,16,128]{2,1,0:T(8,128)S(1)}, u32[]{:S(2)}, u32[]{:S(2)}) collective-permute-start(f32[9,16,128]{2,1,0:T(8,128)S(1)} %get-tuple-element.65.refs_0_), channel_id=1, source_target_pairs={{0,16},{1,17},{2,18},{3,19},{4,20},{5,21},{6,22},{7,23},{8,24},{9,... | collective-permute-start | bytes 221192 | tf_op jit(solution)/shard_map/ppermute | solution.py:579
  25.1 5.7 %collective-permute-start.4 = (f32[9,16,128]{2,1,0:T(8,128)S(1)}, f32[9,16,128]{2,1,0:T(8,128)S(1)}, u32[]{:S(2)}, u32[]{:S(2)}) collective-permute-start(f32[9,16,128]{2,1,0:T(8,128)S(1)} %get-tuple-element.65.refs_0_), channel_id=1, source_target_pairs={{0,8},{1,9},{2,10},{3,11},{4,12},{5,13},{6,14},{7,15},{8,0},{9,1},... | collective-permute-start | bytes 221192 | tf_op jit(solution)/shard_map/ppermute | solution.py:579
  31.6 1.3 %collective-permute-start.7 = (f32[8,16,128]{2,1,0:T(8,128)S(1)}, f32[8,16,128]{2,1,0:T(8,128)S(1)}, u32[]{:S(2)}, u32[]{:S(2)}) collective-permute-start(f32[8,16,128]{2,1,0:T(8,128)S(1)} %get-tuple-element.70), channel_id=1, source_target_pairs={{0,1},{1,0},{2,3},{3,2},{4,5},{5,4},{6,7},{7,6},{8,9},{9,8},{10,11... | collective-permute-start | bytes 196616 | tf_op jit(solution)/shard_map/ppermute | solution.py:579
  39.4 1.3 %collective-permute-start.8 = (f32[9,16,128]{2,1,0:T(8,128)S(1)}, f32[9,16,128]{2,1,0:T(8,128)S(1)}, u32[]{:S(2)}, u32[]{:S(2)}) collective-permute-start(f32[9,16,128]{2,1,0:T(8,128)S(1)} %get-tuple-element.73), channel_id=1, source_target_pairs={{0,1},{1,0},{2,3},{3,2},{4,5},{5,4},{6,7},{7,6},{8,9},{9,8},{10,11... | collective-permute-start | bytes 221192 | tf_op jit(solution)/shard_map/ppermute | solution.py:579
  40.8 5.4 %collective-permute-start.11 = (f32[9,16,128]{2,1,0:T(8,128)S(1)}, f32[9,16,128]{2,1,0:T(8,128)S(1)}, u32[]{:S(2)}, u32[]{:S(2)}) collective-permute-start(f32[9,16,128]{2,1,0:T(8,128)S(1)} %join_b.1.refs_0_), channel_id=1, source_target_pairs={{0,6},{1,7},{2,4},{3,5},{4,2},{5,3},{6,0},{7,1},{8,14},{9,15},{10,... | collective-permute-start | bytes 221192 | tf_op jit(solution)/shard_map/ppermute | solution.py:579
  42.3 5.3 %collective-permute-start.10 = (f32[9,16,128]{2,1,0:T(8,128)S(1)}, f32[9,16,128]{2,1,0:T(8,128)S(1)}, u32[]{:S(2)}, u32[]{:S(2)}) collective-permute-start(f32[9,16,128]{2,1,0:T(8,128)S(1)} %join_b.1.refs_0_), channel_id=1, source_target_pairs={{0,4},{1,5},{2,6},{3,7},{4,0},{5,1},{6,2},{7,3},{8,12},{9,13},{10,... | collective-permute-start | bytes 221192 | tf_op jit(solution)/shard_map/ppermute | solution.py:579
  44.0 4.4 %collective-permute-start.9 = (f32[9,16,128]{2,1,0:T(8,128)S(1)}, f32[9,16,128]{2,1,0:T(8,128)S(1)}, u32[]{:S(2)}, u32[]{:S(2)}) collective-permute-start(f32[9,16,128]{2,1,0:T(8,128)S(1)} %join_b.1.refs_0_), channel_id=1, source_target_pairs={{0,2},{1,3},{2,0},{3,1},{4,6},{5,7},{6,4},{7,5},{8,10},{9,11},{10,... | collective-permute-start | bytes 221192 | tf_op jit(solution)/shard_map/ppermute | solution.py:579
  48.4 6.4 %collective-permute-start.14 = (f32[9,16,128]{2,1,0:T(8,128)S(1)}, f32[9,16,128]{2,1,0:T(8,128)S(1)}, u32[]{:S(2)}, u32[]{:S(2)}) collective-permute-start(f32[9,16,128]{2,1,0:T(8,128)S(1)} %get-tuple-element.75.refs_0_), channel_id=1, source_target_pairs={{0,24},{1,25},{2,26},{3,27},{4,28},{5,29},{6,30},{7,31},{8,16},{9,... | collective-permute-start | bytes 221192 | tf_op jit(solution)/shard_map/ppermute | solution.py:579
  51.1 6.6 %collective-permute-start.13 = (f32[9,16,128]{2,1,0:T(8,128)S(1)}, f32[9,16,128]{2,1,0:T(8,128)S(1)}, u32[]{:S(2)}, u32[]{:S(2)}) collective-permute-start(f32[9,16,128]{2,1,0:T(8,128)S(1)} %get-tuple-element.75.refs_0_), channel_id=1, source_target_pairs={{0,16},{1,17},{2,18},{3,19},{4,20},{5,21},{6,22},{7,23},{8,24},{9,... | collective-permute-start | bytes 221192 | tf_op jit(solution)/shard_map/ppermute | solution.py:579
  51.1 6.6 %collective-permute-start.12 = (f32[9,16,128]{2,1,0:T(8,128)S(1)}, f32[9,16,128]{2,1,0:T(8,128)S(1)}, u32[]{:S(2)}, u32[]{:S(2)}) collective-permute-start(f32[9,16,128]{2,1,0:T(8,128)S(1)} %get-tuple-element.75.refs_0_), channel_id=1, source_target_pairs={{0,8},{1,9},{2,10},{3,11},{4,12},{5,13},{6,14},{7,15},{8,0},{9,1},... | collective-permute-start | bytes 221192 | tf_op jit(solution)/shard_map/ppermute | solution.py:579
  57.8 1.3 %collective-permute-start.15 = (f32[8,16,128]{2,1,0:T(8,128)S(1)}, f32[8,16,128]{2,1,0:T(8,128)S(1)}, u32[]{:S(2)}, u32[]{:S(2)}) collective-permute-start(f32[8,16,128]{2,1,0:T(8,128)S(1)} %get-tuple-element.79), channel_id=1, source_target_pairs={{0,1},{1,0},{2,3},{3,2},{4,5},{5,4},{6,7},{7,6},{8,9},{9,8},{10,11... | collective-permute-start | bytes 196616 | tf_op jit(solution)/shard_map/ppermute | solution.py:579
  65.3 1.3 %collective-permute-start.16 = (f32[9,16,128]{2,1,0:T(8,128)S(1)}, f32[9,16,128]{2,1,0:T(8,128)S(1)}, u32[]{:S(2)}, u32[]{:S(2)}) collective-permute-start(f32[9,16,128]{2,1,0:T(8,128)S(1)} %get-tuple-element.84), channel_id=1, source_target_pairs={{0,1},{1,0},{2,3},{3,2},{4,5},{5,4},{6,7},{7,6},{8,9},{9,8},{10,11... | collective-permute-start | bytes 221192 | tf_op jit(solution)/shard_map/ppermute | solution.py:579
  66.7 5.4 %collective-permute-start.19 = (f32[9,16,128]{2,1,0:T(8,128)S(1)}, f32[9,16,128]{2,1,0:T(8,128)S(1)}, u32[]{:S(2)}, u32[]{:S(2)}) collective-permute-start(f32[9,16,128]{2,1,0:T(8,128)S(1)} %join_c.1.refs_0_), channel_id=1, source_target_pairs={{0,6},{1,7},{2,4},{3,5},{4,2},{5,3},{6,0},{7,1},{8,14},{9,15},{10,... | collective-permute-start | bytes 221192 | tf_op jit(solution)/shard_map/ppermute | solution.py:579
  68.3 5.3 %collective-permute-start.18 = (f32[9,16,128]{2,1,0:T(8,128)S(1)}, f32[9,16,128]{2,1,0:T(8,128)S(1)}, u32[]{:S(2)}, u32[]{:S(2)}) collective-permute-start(f32[9,16,128]{2,1,0:T(8,128)S(1)} %join_c.1.refs_0_), channel_id=1, source_target_pairs={{0,4},{1,5},{2,6},{3,7},{4,0},{5,1},{6,2},{7,3},{8,12},{9,13},{10,... | collective-permute-start | bytes 221192 | tf_op jit(solution)/shard_map/ppermute | solution.py:579
  69.5 4.4 %collective-permute-start.17 = (f32[9,16,128]{2,1,0:T(8,128)S(1)}, f32[9,16,128]{2,1,0:T(8,128)S(1)}, u32[]{:S(2)}, u32[]{:S(2)}) collective-permute-start(f32[9,16,128]{2,1,0:T(8,128)S(1)} %join_c.1.refs_0_), channel_id=1, source_target_pairs={{0,2},{1,3},{2,0},{3,1},{4,6},{5,7},{6,4},{7,5},{8,10},{9,11},{10,... | collective-permute-start | bytes 221192 | tf_op jit(solution)/shard_map/ppermute | solution.py:579
  73.9 7.0 %collective-permute-start.22 = (f32[9,16,128]{2,1,0:T(8,128)S(1)}, f32[9,16,128]{2,1,0:T(8,128)S(1)}, u32[]{:S(2)}, u32[]{:S(2)}) collective-permute-start(f32[9,16,128]{2,1,0:T(8,128)S(1)} %get-tuple-element.85.refs_0_), channel_id=1, source_target_pairs={{0,24},{1,25},{2,26},{3,27},{4,28},{5,29},{6,30},{7,31},{8,16},{9,... | collective-permute-start | bytes 221192 | tf_op jit(solution)/shard_map/ppermute | solution.py:579
  76.2 6.8 %collective-permute-start.21 = (f32[9,16,128]{2,1,0:T(8,128)S(1)}, f32[9,16,128]{2,1,0:T(8,128)S(1)}, u32[]{:S(2)}, u32[]{:S(2)}) collective-permute-start(f32[9,16,128]{2,1,0:T(8,128)S(1)} %get-tuple-element.85.refs_0_), channel_id=1, source_target_pairs={{0,16},{1,17},{2,18},{3,19},{4,20},{5,21},{6,22},{7,23},{8,24},{9,... | collective-permute-start | bytes 221192 | tf_op jit(solution)/shard_map/ppermute | solution.py:579
  76.2 6.8 %collective-permute-start.20 = (f32[9,16,128]{2,1,0:T(8,128)S(1)}, f32[9,16,128]{2,1,0:T(8,128)S(1)}, u32[]{:S(2)}, u32[]{:S(2)}) collective-permute-start(f32[9,16,128]{2,1,0:T(8,128)S(1)} %get-tuple-element.85.refs_0_), channel_id=1, source_target_pairs={{0,8},{1,9},{2,10},{3,11},{4,12},{5,13},{6,14},{7,15},{8,0},{9,1},... | collective-permute-start | bytes 221192 | tf_op jit(solution)/shard_map/ppermute | solution.py:579
  83.1 1.3 %collective-permute-start.23 = (f32[8,16,128]{2,1,0:T(8,128)S(1)}, f32[8,16,128]{2,1,0:T(8,128)S(1)}, u32[]{:S(2)}, u32[]{:S(2)}) collective-permute-start(f32[8,16,128]{2,1,0:T(8,128)S(1)} %get-tuple-element.88), channel_id=1, source_target_pairs={{0,1},{1,0},{2,3},{3,2},{4,5},{5,4},{6,7},{7,6},{8,9},{9,8},{10,11... | collective-permute-start | bytes 196616 | tf_op jit(solution)/shard_map/ppermute | solution.py:579
  91.2 1.3 %collective-permute-start.24 = (f32[9,16,128]{2,1,0:T(8,128)S(1)}, f32[9,16,128]{2,1,0:T(8,128)S(1)}, u32[]{:S(2)}, u32[]{:S(2)}) collective-permute-start(f32[9,16,128]{2,1,0:T(8,128)S(1)} %get-tuple-element.94), channel_id=1, source_target_pairs={{0,1},{1,0},{2,3},{3,2},{4,5},{5,4},{6,7},{7,6},{8,9},{9,8},{10,11... | collective-permute-start | bytes 221192 | tf_op jit(solution)/shard_map/ppermute | solution.py:579
  92.6 5.4 %collective-permute-start.27 = (f32[9,16,128]{2,1,0:T(8,128)S(1)}, f32[9,16,128]{2,1,0:T(8,128)S(1)}, u32[]{:S(2)}, u32[]{:S(2)}) collective-permute-start(f32[9,16,128]{2,1,0:T(8,128)S(1)} %join_d.1.refs_0_), channel_id=1, source_target_pairs={{0,6},{1,7},{2,4},{3,5},{4,2},{5,3},{6,0},{7,1},{8,14},{9,15},{10,... | collective-permute-start | bytes 221192 | tf_op jit(solution)/shard_map/ppermute | solution.py:579
  94.2 5.2 %collective-permute-start.26 = (f32[9,16,128]{2,1,0:T(8,128)S(1)}, f32[9,16,128]{2,1,0:T(8,128)S(1)}, u32[]{:S(2)}, u32[]{:S(2)}) collective-permute-start(f32[9,16,128]{2,1,0:T(8,128)S(1)} %join_d.1.refs_0_), channel_id=1, source_target_pairs={{0,4},{1,5},{2,6},{3,7},{4,0},{5,1},{6,2},{7,3},{8,12},{9,13},{10,... | collective-permute-start | bytes 221192 | tf_op jit(solution)/shard_map/ppermute | solution.py:579
  95.2 4.4 %collective-permute-start.25 = (f32[9,16,128]{2,1,0:T(8,128)S(1)}, f32[9,16,128]{2,1,0:T(8,128)S(1)}, u32[]{:S(2)}, u32[]{:S(2)}) collective-permute-start(f32[9,16,128]{2,1,0:T(8,128)S(1)} %join_d.1.refs_0_), channel_id=1, source_target_pairs={{0,2},{1,3},{2,0},{3,1},{4,6},{5,7},{6,4},{7,5},{8,10},{9,11},{10,... | collective-permute-start | bytes 221192 | tf_op jit(solution)/shard_map/ppermute | solution.py:579
  99.6 7.0 %collective-permute-start.30 = (f32[9,16,128]{2,1,0:T(8,128)S(1)}, f32[9,16,128]{2,1,0:T(8,128)S(1)}, u32[]{:S(2)}, u32[]{:S(2)}) collective-permute-start(f32[9,16,128]{2,1,0:T(8,128)S(1)} %get-tuple-element.95.refs_0_), channel_id=1, source_target_pairs={{0,24},{1,25},{2,26},{3,27},{4,28},{5,29},{6,30},{7,31},{8,16},{9,... | collective-permute-start | bytes 221192 | tf_op jit(solution)/shard_map/ppermute | solution.py:579
  101.9 6.8 %collective-permute-start.29 = (f32[9,16,128]{2,1,0:T(8,128)S(1)}, f32[9,16,128]{2,1,0:T(8,128)S(1)}, u32[]{:S(2)}, u32[]{:S(2)}) collective-permute-start(f32[9,16,128]{2,1,0:T(8,128)S(1)} %get-tuple-element.95.refs_0_), channel_id=1, source_target_pairs={{0,16},{1,17},{2,18},{3,19},{4,20},{5,21},{6,22},{7,23},{8,24},{9,... | collective-permute-start | bytes 221192 | tf_op jit(solution)/shard_map/ppermute | solution.py:579
  101.9 6.8 %collective-permute-start.28 = (f32[9,16,128]{2,1,0:T(8,128)S(1)}, f32[9,16,128]{2,1,0:T(8,128)S(1)}, u32[]{:S(2)}, u32[]{:S(2)}) collective-permute-start(f32[9,16,128]{2,1,0:T(8,128)S(1)} %get-tuple-element.95.refs_0_), channel_id=1, source_target_pairs={{0,8},{1,9},{2,10},{3,11},{4,12},{5,13},{6,14},{7,15},{8,0},{9,1},... | collective-permute-start | bytes 221192 | tf_op jit(solution)/shard_map/ppermute | solution.py:579
  108.8 1.3 %collective-permute-start.31 = (f32[8,16,128]{2,1,0:T(8,128)S(1)}, f32[8,16,128]{2,1,0:T(8,128)S(1)}, u32[]{:S(2)}, u32[]{:S(2)}) collective-permute-start(f32[8,16,128]{2,1,0:T(8,128)S(1)} %get-tuple-element.98), channel_id=1, source_target_pairs={{0,1},{1,0},{2,3},{3,2},{4,5},{5,4},{6,7},{7,6},{8,9},{9,8},{10,11... | collective-permute-start | bytes 196616 | tf_op jit(solution)/shard_map/ppermute | solution.py:579
